TPU v7x, 256 devices: a whole 4x4x8 slice. The times are simulated.
256 devices in a mesh: gx: 32 (over x, z_hi, core), sec: 8 (over z_lo, y).
Axes of the slice: x: 4, y: 4, z: 8 (z_hi: 4, z_lo: 2; z = z_hi * 2 + z_lo), core: 2. Of those that a mesh axis runs over, the one named last changes fastest.
Arguments:
- state_init: float32 [16, 256, 64, 128], P(None, 'gx', 'sec'), may hold values from -6 to 6
- rock_type: int32 [256, 4096], P('gx', 'sec'), may hold values from 0 to 15
- perm_table: float32 [3, 16], replicated, may hold values from 0.2 to 1
- well_cells: int32 [256], replicated, may hold values from 0 to 1048575
- well_rate: float32 [16, 256], replicated, may hold values from -12 to 12
- basis_in: bfloat16 [256, 64, 128, 256], P(('gx', 'sec')), may hold values from -4 to 4
- singular: float32 [256], replicated, may hold values from 0.5 to 2
Outputs:
- state_out: float32 [16, 256, 64, 128], P(None, 'gx', 'sec')
- basis_out: bfloat16 [256, 64, 128, 256], P(('gx', 'sec'))
- singular_out: float32 [256], replicated
All inputs are finite; a program needn't handle non-finite values.
Results may differ from a plain program's by a relative error of at most 0.0059.
Values may be sent and summed in bfloat16 or wider, within the bound.
A program may use at most 128 MiB of HBM per device.

v0:
```python
import jax
import jax.numpy as jnp
from jax import lax
from jax.sharding import PartitionSpec as P

MG = 8
STEPS = 4
GROUPS = 2


DT_PRESSURE = 0.12
DT_SATURATION = 0.06
DT_ADVECT = 0.15


def with_halo(block, sides, width):
    for axis, dim in sides:
        count = lax.axis_size(axis)
        forward = [(i, i + 1) for i in range(count - 1)]
        backward = [(target, source) for source, target in forward]
        low = lax.ppermute(
            lax.slice_in_dim(block, block.shape[dim] - width, None, axis=dim), axis, forward
        )
        high = lax.ppermute(lax.slice_in_dim(block, 0, width, axis=dim), axis, backward)
        block = jnp.concatenate([low, block, high], axis=dim)
    return block


def harmonic(left, right):
    return 2.0 * left * right / (left + right)


def shift_layers(fields):
    blank = jnp.zeros_like(fields[..., :1])
    return (
        jnp.concatenate([fields[..., 1:], blank], -1),
        jnp.concatenate([blank, fields[..., :-1]], -1),
    )


def advance(fields, besides, weights, inflow, layers):
    column = lax.broadcasted_iota(jnp.int32, (fields.shape[-1],), 0)
    step_sizes = jnp.where(column < layers, DT_PRESSURE, DT_SATURATION)
    is_sat = (column >= layers).astype(fields.dtype)
    press_both = jnp.concatenate([fields[..., :layers], fields[..., :layers]], -1)
    spread = jnp.zeros_like(fields)
    carried = jnp.zeros_like(fields)
    for beside, weight in zip(besides, weights):
        spread = spread + weight * (beside - fields)
        beside_press = jnp.concatenate([beside[..., :layers], beside[..., :layers]], -1)
        pushed = weight * (beside_press - press_both)
        carried = carried + jnp.maximum(pushed, 0.0) * beside + jnp.minimum(pushed, 0.0) * fields
    return fields + step_sizes * spread + DT_ADVECT * is_sat * carried + DT_PRESSURE * inflow


def small_rotation(coeffs, lower, sigma):
    count = sigma.shape[0]
    extra = lower.shape[0]
    top = jnp.concatenate([jnp.diag(sigma), coeffs.T], 1)
    bottom = jnp.concatenate([jnp.zeros((extra, count), sigma.dtype), lower.T], 1)
    core = jnp.concatenate([top, bottom], 0)
    leading = jnp.dot(core, top.T, precision=lax.Precision.HIGHEST)
    inner = jnp.dot(leading.T, leading, precision=lax.Precision.HIGHEST)
    factor = jnp.linalg.cholesky(inner)
    rotation = lax.linalg.triangular_solve(factor, leading.T, left_side=True, lower=True).T
    energy = jnp.dot(core.T, rotation, precision=lax.Precision.HIGHEST)
    return (rotation, jnp.sqrt(jnp.sum(energy * energy, axis=0)))


def compress(stacked, basis_now, sigma, rows_total):
    count = stacked.shape[0]
    snaps = stacked.reshape(count, -1)
    flat_basis = basis_now.reshape(snaps.shape[1], basis_now.shape[-1])
    basis_count = flat_basis.shape[1]
    local_proj = jnp.dot(snaps, flat_basis, preferred_element_type=jnp.float32)
    coeffs = lax.psum(local_proj, ("gx", "sec")) / rows_total
    rounded = coeffs.astype(jnp.bfloat16)
    resid = snaps.astype(jnp.float32) - lax.dot_general(
        rounded, flat_basis, (((1,), (1,)), ((), ())), preferred_element_type=jnp.float32
    )
    gram = (
        lax.psum(jnp.dot(resid, resid.T, precision=lax.Precision.HIGHEST), ("gx", "sec"))
        / rows_total
    )
    lower = jnp.linalg.cholesky(gram)
    ortho = lax.linalg.triangular_solve(lower, resid, left_side=True, lower=True).astype(
        jnp.bfloat16
    )
    rotation, sigma_next = small_rotation(coeffs, lower, sigma)
    mixing = rotation.astype(jnp.bfloat16)
    fresh = jnp.dot(flat_basis, mixing[:basis_count], preferred_element_type=jnp.float32)
    fresh = fresh + lax.dot_general(
        ortho, mixing[basis_count:], (((0,), (0,)), ((), ())), preferred_element_type=jnp.float32
    )
    return (fresh.astype(jnp.bfloat16).reshape(basis_now.shape), sigma_next)


def body(state_init, rock_type, perm_table, well_cells, well_rate, basis_in, singular):
    across = state_init.shape[1]
    along = state_init.shape[2]
    layers = state_init.shape[3] // 2
    sec_count = lax.axis_size("sec")
    rock_count = perm_table.shape[1]
    kinds = lax.broadcasted_iota(jnp.int32, (rock_count, 1, 1), 0)
    picks = (rock_type[None] == kinds).astype(jnp.float32)
    perm = jnp.einsum("dr,rxc->dxc", perm_table, picks, precision=lax.Precision.HIGHEST).reshape(
        3, across, along, layers
    )
    paired = jnp.concatenate([perm[0], perm[1]], -1)
    bordered_perm = with_halo(paired.astype(jnp.bfloat16), (("gx", 0), ("sec", 1)), 1).astype(
        paired.dtype
    )
    perm_xh = bordered_perm[..., :layers]
    perm_yh = bordered_perm[..., layers:]
    x_up = harmonic(perm[0], perm_xh[2:, 1:-1])
    x_down = harmonic(perm_xh[:-2, 1:-1], perm[0])
    y_up = harmonic(perm[1], perm_yh[1:-1, 2:])
    y_down = harmonic(perm_yh[1:-1, :-2], perm[1])
    z_padded = jnp.pad(perm[2], ((0, 0), (0, 0), (1, 1)))
    z_up = harmonic(perm[2], z_padded[..., 2:])
    z_down = harmonic(z_padded[..., :-2], perm[2])
    weights = [
        jnp.concatenate([face, face], -1) for face in (x_up, x_down, y_up, y_down, z_up, z_down)
    ]
    x_start = lax.axis_index("gx") * across
    y_start = lax.axis_index("sec") * along
    total_y = along * sec_count
    x_pos = lax.broadcasted_iota(jnp.int32, (across, along, layers), 0)
    y_pos = lax.broadcasted_iota(jnp.int32, (across, along, layers), 1)
    z_pos = lax.broadcasted_iota(jnp.int32, (across, along, layers), 2)
    cell_ids = ((x_start + x_pos) * total_y + y_start + y_pos) * layers + z_pos
    hits = (well_cells[:, None] == cell_ids.reshape(1, -1)).astype(jnp.float32)
    source = jnp.dot(well_rate, hits, precision=lax.Precision.HIGHEST).reshape(
        state_init.shape[0], across, along, layers
    )
    source_full = jnp.concatenate([source, jnp.zeros_like(source)], -1)
    local_rows = basis_in.shape[0] * basis_in.shape[1] * basis_in.shape[2]
    rows_total = local_rows * lax.axis_size("gx") * sec_count
    basis_now = basis_in
    sigma = singular
    finals = []
    for group in range(GROUPS):
        fields = state_init[group * MG : (group + 1) * MG]
        inflow = source_full[group * MG : (group + 1) * MG]
        saved = []
        for step_index in range(STEPS):
            bordered = with_halo(fields.astype(jnp.bfloat16), (("gx", 1), ("sec", 2)), 1).astype(
                fields.dtype
            )
            up_layer, down_layer = shift_layers(fields)
            besides = [
                bordered[:, 2:, 1:-1],
                bordered[:, :-2, 1:-1],
                bordered[:, 1:-1, 2:],
                bordered[:, 1:-1, :-2],
                up_layer,
                down_layer,
            ]
            fields = advance(fields, besides, weights, inflow, layers)
            snapshot = fields.astype(jnp.bfloat16)
            saved.append(snapshot)
        finals.append(fields)
        stacked = jnp.concatenate(saved, 0)
        stacked = lax.all_to_all(stacked, "sec", split_axis=1, concat_axis=2, tiled=True)
        basis_now, sigma = compress(stacked, basis_now, sigma, rows_total)
    return (jnp.concatenate(finals, 0), basis_now, sigma)


def solution(mesh):
    return jax.shard_map(
        body,
        mesh=mesh,
        in_specs=(
            P(None, "gx", "sec", None),
            P("gx", "sec"),
            P(),
            P(),
            P(),
            P(("gx", "sec"), None, None, None),
            P(),
        ),
        out_specs=(P(None, "gx", "sec", None), P(("gx", "sec"), None, None, None), P()),
        check_vma=False,
    )
```

profile of v0, /device:TPU:1, one launch (start us, length us, event | category | flops | bytes accessed | tf_op | source)
XLA Modules:
  0.0 677.7 jit_solution(60793899374076487)
XLA Ops:
  2.6 6.3 collective-permute-start
  8.9 1.9 collective-permute-start.1
  12.5 4.5 collective-permute-start.4
  17.0 1.9 collective-permute-start.5
  19.6 4.5 collective-permute-start.20
  24.1 2.2 fusion.148
  29.4 2.1 convolution_bitcast_fusion.1
  31.9 1.5 pad_maximum_fusion.50
  33.4 3.2 collective-permute-start.2
  39.3 1.9 collective-permute-start.21
  43.3 3.9 collective-permute-start.6
  49.4 4.0 collective-permute-start.22
  55.8 2.0 fusion.134
  61.2 7.0 %collective-permute-start.8 = (bf16[8,1,8,128]{3,2,0,1:T(8,128)(2,1)S(1)}, bf16[8,1,8,128]{3,2,0,1:T(8,128)(2,1)S(1)}, u32[]{:S(2)}, u32[]{:S(2)}) collective-permute-start(bf16[8,1,8,128]{3,2,0,1:T(8,128)(2,1)S(1)} %get-tuple-element.151), channel_id=1, source_target_pairs={{0,8},{8,16},{16,24},{24,32},{32,40},{40,48},{48,56},{56,64},{64,7... | collective-permute-start | bytes 49160 | tf_op jit(solution)/shard_map/ppermute | solution.py:21
  68.3 1.9 collective-permute-start.9
  70.3 4.5 collective-permute-start.24
  74.9 1.9 collective-permute-start.25
  77.0 3.6 collective-permute-start.10
  82.6 5.3 collective-permute-start.26
  90.8 4.2 collective-permute-done.27
  96.6 7.8 %collective-permute-start.12 = (bf16[8,1,8,128]{3,2,0,1:T(8,128)(2,1)S(1)}, bf16[8,1,8,128]{3,2,0,1:T(8,128)(2,1)S(1)}, u32[]{:S(2)}, u32[]{:S(2)}) collective-permute-start(bf16[8,1,8,128]{3,2,0,1:T(8,128)(2,1)S(1)} %get-tuple-element.149), channel_id=1, source_target_pairs={{0,8},{8,16},{16,24},{24,32},{32,40},{40,48},{48,56},{56,64},{64,7... | collective-permute-start | bytes 49160 | tf_op jit(solution)/shard_map/ppermute | solution.py:21
  104.5 1.9 collective-permute-start.13
  106.6 4.5 collective-permute-start.28
  111.1 1.9 collective-permute-start.29
  113.3 3.6 collective-permute-start.14
  119.5 4.5 collective-permute-start.30
  124.1 1.5 collective-permute-start.31
  127.2 4.0 collective-permute-done.31
  132.8 8.4 %collective-permute-start.16 = (bf16[8,1,8,128]{3,2,0,1:T(8,128)(2,1)S(1)}, bf16[8,1,8,128]{3,2,0,1:T(8,128)(2,1)S(1)}, u32[]{:S(2)}, u32[]{:S(2)}) collective-permute-start(bf16[8,1,8,128]{3,2,0,1:T(8,128)(2,1)S(1)} %get-tuple-element.147), channel_id=1, source_target_pairs={{0,8},{8,16},{16,24},{24,32},{32,40},{40,48},{48,56},{56,64},{64,7... | collective-permute-start | bytes 49160 | tf_op jit(solution)/shard_map/ppermute | solution.py:21
  141.2 1.9 collective-permute-start.17
  143.3 4.5 collective-permute-start.32
  147.9 1.9 collective-permute-start.33
  150.0 3.6 collective-permute-start.18
  156.3 3.6 collective-permute-start.34
  161.6 1.8 fusion.131
  164.2 9.1 %all-to-all-start = ((bf16[32,8,8,128]{3,2,0,1:T(8,128)(2,1)}), bf16[32,8,8,128]{3,2,0,1:T(8,128)(2,1)S(1)}, u32[]{:S(2)}, u32[]{:S(2)}) async-start(bf16[32,8,8,128]{3,2,0,1:T(8,128)(2,1)} %pad_maximum_fusion.1), calls=%async_computation | async-start | bytes 1048576 | tf_op jit(solution)/shard_map/all_to_all | solution.py:164
  176.5 5.4 all-to-all-done
  181.8 3.5 all-to-all-start.1
  185.5 3.0 fusion.9
  188.5 89.6 %psum.28 = f32[32,256]{1,0:T(8,128)S(1)} all-reduce(f32[32,256]{1,0:T(8,128)S(1)} %fusion.9), channel_id=1, replica_groups=mesh['gx'=32,'sec'=8] {'gx','sec'}, use_global_device_ids=true, to_apply=%region_0.1 | all-reduce | flops 8192 | bytes 65536 | tf_op jit(solution)/shard_map/psum | solution.py:76
  278.1 3.6 convolution_subtract_fusion.1
  282.7 74.5 %psum.29 = f32[32,32]{0,1:T(8,128)S(1)} all-reduce(f32[32,32]{0,1:T(8,128)S(1)} %fusion.171), channel_id=1, replica_groups=mesh['gx'=32,'sec'=8] {'gx','sec'}, use_global_device_ids=true, to_apply=%region_1.2 | all-reduce | flops 1024 | bytes 8192 | tf_op jit(solution)/shard_map/psum | solution.py:82
  357.2 2.9 cholesky.170
  363.2 11.7 %cholesky.183 = f32[128,128]{1,0:T(8,128)S(1)} custom-call(f32[128,128]{1,0:T(8,128)S(1)} %cholesky.258), custom_call_target="Cholesky" | custom-call | tf_op jit(solution)/shard_map/jit(cholesky)/cholesky | solution.py:64
  375.6 9.8 %custom-call.19 = f32[1,128,128]{1,2,0:T(8,128)S(1)} custom-call(f32[1,128,128]{2,1,0:T(8,128)S(1)} %get-tuple-element.176), custom_call_target="InvertDiagBlocksLowerTriangular" | custom-call | tf_op jit(solution)/shard_map/jit(cholesky)/cholesky | solution.py:64
  385.9 11.7 %cholesky.200 = f32[128,128]{1,0:T(8,128)S(1)} custom-call(f32[128,128]{1,0:T(8,128)S(1)} %convolution_subtract_fusion.5), custom_call_target="Cholesky" | custom-call | tf_op jit(solution)/shard_map/jit(cholesky)/cholesky | solution.py:64
  399.9 4.0 while.4
  403.9 19.7 %custom-call.20 = f32[2,128,128]{1,2,0:T(8,128)S(1)} custom-call(f32[2,128,128]{2,1,0:T(8,128)S(1)} %get-tuple-element.21), custom_call_target="InvertDiagBlocksLowerTriangular" | custom-call | tf_op jit(solution)/shard_map/triangular_solve/custom-call.4 | solution.py:65
  424.5 6.8 %convolution_bitcast_fusion = f32[8192,256]{0,1:T(8,128)} fusion(bf16[8192,256]{1,0:T(8,128)(2,1)} %bitcast.138, bf16[288,256]{1,0:T(8,128)(2,1)S(1)} %fusion.85), kind=kOutput, calls=%fused_computation.6 | convolution fusion | flops 1073741824 | bytes 12713984 | tf_op jit(solution)/shard_map/dot_general | solution.py:91
  431.3 2.4 custom-call.21
  435.7 6.7 fusion
  442.5 3.5 fusion.7
  446.1 73.6 %psum.30 = f32[32,256]{1,0:T(8,128)S(1)} all-reduce(f32[32,256]{1,0:T(8,128)S(1)} %fusion.7), channel_id=1, replica_groups=mesh['gx'=32,'sec'=8] {'gx','sec'}, use_global_device_ids=true, to_apply=%region_9.14 | all-reduce | flops 8192 | bytes 65536 | tf_op jit(solution)/shard_map/psum | solution.py:76
  519.7 3.1 convolution_subtract_fusion
  524.0 74.3 %psum.31 = f32[32,32]{0,1:T(8,128)S(1)} all-reduce(f32[32,32]{0,1:T(8,128)S(1)} %fusion.173), channel_id=1, replica_groups=mesh['gx'=32,'sec'=8] {'gx','sec'}, use_global_device_ids=true, to_apply=%region_10.15 | all-reduce | flops 1024 | bytes 8192 | tf_op jit(solution)/shard_map/psum | solution.py:82
  598.4 2.9 cholesky.215
  604.4 11.7 %cholesky.228 = f32[128,128]{1,0:T(8,128)S(1)} custom-call(f32[128,128]{1,0:T(8,128)S(1)} %cholesky.261), custom_call_target="Cholesky" | custom-call | tf_op jit(solution)/shard_map/jit(cholesky)/cholesky | solution.py:64
  616.8 9.8 %custom-call.22 = f32[1,128,128]{1,2,0:T(8,128)S(1)} custom-call(f32[1,128,128]{2,1,0:T(8,128)S(1)} %get-tuple-element.172), custom_call_target="InvertDiagBlocksLowerTriangular" | custom-call | tf_op jit(solution)/shard_map/jit(cholesky)/cholesky | solution.py:64
  627.1 11.7 %cholesky.245 = f32[128,128]{1,0:T(8,128)S(1)} custom-call(f32[128,128]{1,0:T(8,128)S(1)} %convolution_subtract_fusion.4), custom_call_target="Cholesky" | custom-call | tf_op jit(solution)/shard_map/jit(cholesky)/cholesky | solution.py:64
  641.0 3.8 while.5
  644.8 19.7 %custom-call.23 = f32[2,128,128]{1,2,0:T(8,128)S(1)} custom-call(f32[2,128,128]{2,1,0:T(8,128)S(1)} %get-tuple-element.22), custom_call_target="InvertDiagBlocksLowerTriangular" | custom-call | tf_op jit(solution)/shard_map/triangular_solve/custom-call.4 | solution.py:65
  666.3 2.4 custom-call.24
  670.4 3.5 fusion.91
  673.9 3.3 fusion.1
  (242 shorter events, 68.4 us)
Async XLA Ops:
  0.6 28.7 %copy-start = (f32[16,256]{1,0:T(8,128)S(1)}, f32[16,256]{1,0:T(8,128)}, u32[]{:S(2)}) copy-start(f32[16,256]{1,0:T(8,128)} %param.17) | copy-start | bytes 49156
  0.6 25.7 %copy-start.2 = (f32[16,8,8,128]{3,2,1,0:T(8,128)S(1)}, f32[16,8,8,128]{3,2,1,0:T(8,128)}, u32[]{:S(2)}) copy-start(f32[16,8,8,128]{3,2,1,0:T(8,128)} %param.13) | copy-start | bytes 1572868
  0.7 26.2 %copy-start.15 = (f32[256]{0:T(256)S(1)}, f32[256]{0:T(256)}, u32[]{:S(2)}) copy-start(f32[256]{0:T(256)} %param.19) | copy-start | bytes 3076
  1.9 26.1 %copy-start.8 = (bf16[8,8,64]{2,1,0:T(8,128)(2,1)}, bf16[8,8,64]{2,1,0:T(8,128)(2,1)S(1)}, u32[]{:S(2)}) copy-start(bf16[8,8,64]{2,1,0:T(8,128)(2,1)S(1)} %convert.6) | copy-start | bytes 24580
  2.0 26.0 %copy-start.9 = (bf16[8,8,64]{2,1,0:T(8,128)(2,1)}, bf16[8,8,64]{2,1,0:T(8,128)(2,1)S(1)}, u32[]{:S(2)}) copy-start(bf16[8,8,64]{2,1,0:T(8,128)(2,1)S(1)} %convert.7) | copy-start | bytes 24580
  2.6 29.3 %collective-permute-start = (bf16[1,8,128]{2,1,0:T(8,128)(2,1)}, bf16[1,8,128]{2,1,0:T(8,128)(2,1)}, u32[]{:S(2)}, u32[]{:S(2)}) collective-permute-start(bf16[1,8,128]{2,1,0:T(8,128)(2,1)} %get-tuple-element.179), channel_id=1, source_target_pairs={{0,8},{8,16},{16,24},{24,32},{32,40},{40,48},{48,56},{56,64},{64,7... | collective-permute-start | bytes 6152 | tf_op jit(solution)/shard_map/ppermute | solution.py:21
  8.9 23.1 %collective-permute-start.1 = (bf16[1,8,128]{2,1,0:T(8,128)(2,1)}, bf16[1,8,128]{2,1,0:T(8,128)(2,1)}, u32[]{:S(2)}, u32[]{:S(2)}) collective-permute-start(bf16[1,8,128]{2,1,0:T(8,128)(2,1)} %get-tuple-element.180), channel_id=1, source_target_pairs={{8,0},{16,8},{24,16},{32,24},{40,32},{48,40},{56,48},{64,56},{72,6... | collective-permute-start | bytes 6152 | tf_op jit(solution)/shard_map/ppermute | solution.py:24
  12.5 29.9 %collective-permute-start.4 = (bf16[8,1,8,128]{3,2,0,1:T(8,128)(2,1)}, bf16[8,1,8,128]{3,2,0,1:T(8,128)(2,1)}, u32[]{:S(2)}, u32[]{:S(2)}) collective-permute-start(bf16[8,1,8,128]{3,2,0,1:T(8,128)(2,1)} %get-tuple-element.153), channel_id=1, source_target_pairs={{0,8},{8,16},{16,24},{24,32},{32,40},{40,48},{48,56},{56,64},{64,7... | collective-permute-start | bytes 49160 | tf_op jit(solution)/shard_map/ppermute | solution.py:21
  17.0 25.4 %collective-permute-start.5 = (bf16[8,1,8,128]{3,2,0,1:T(8,128)(2,1)}, bf16[8,1,8,128]{3,2,0,1:T(8,128)(2,1)}, u32[]{:S(2)}, u32[]{:S(2)}) collective-permute-start(bf16[8,1,8,128]{3,2,0,1:T(8,128)(2,1)} %get-tuple-element.154), channel_id=1, source_target_pairs={{8,0},{16,8},{24,16},{32,24},{40,32},{48,40},{56,48},{64,56},{72,6... | collective-permute-start | bytes 49160 | tf_op jit(solution)/shard_map/ppermute | solution.py:24
  19.6 28.9 %collective-permute-start.20 = (bf16[8,1,8,128]{3,2,0,1:T(8,128)(2,1)}, bf16[8,1,8,128]{3,2,0,1:T(8,128)(2,1)}, u32[]{:S(2)}, u32[]{:S(2)}) collective-permute-start(bf16[8,1,8,128]{3,2,0,1:T(8,128)(2,1)} %get-tuple-element.161), channel_id=1, source_target_pairs={{0,8},{8,16},{16,24},{24,32},{32,40},{40,48},{48,56},{56,64},{64,7... | collective-permute-start | bytes 49160 | tf_op jit(solution)/shard_map/ppermute | solution.py:21
  29.3 26.4 %copy-start.3 = (f32[8,8,8,128]{3,2,1,0:T(8,128)S(1)}, f32[8,8,8,128]{3,2,1,0:T(8,128)}, u32[]{:S(2)}) copy-start(f32[8,8,8,128]{3,2,1,0:T(8,128)} %get-tuple-element.191) | copy-start | bytes 786436
  29.3 26.4 %copy-start.4 = (f32[8,8,8,128]{3,2,1,0:T(8,128)S(1)}, f32[8,8,8,128]{3,2,1,0:T(8,128)}, u32[]{:S(2)}) copy-start(f32[8,8,8,128]{3,2,1,0:T(8,128)} %get-tuple-element.192) | copy-start | bytes 786436
  33.4 5.3 collective-permute-start.2
  36.6 4.7 collective-permute-start.3
  38.7 17.1 %copy-start.10 = (f32[128]{0:T(128)S(1)}, f32[128]{0:T(128)}, u32[]{:S(2)}) copy-start(f32[128]{0:T(128)} %get-tuple-element.201) | copy-start | bytes 1540
  38.7 17.1 %copy-start.12 = (f32[128]{0:T(128)S(1)}, f32[128]{0:T(128)}, u32[]{:S(2)}) copy-start(f32[128]{0:T(128)} %get-tuple-element.202) | copy-start | bytes 1540
  38.7 0.6 copy-start.14
  39.3 9.2 %collective-permute-start.21 = (bf16[8,1,8,128]{3,2,0,1:T(8,128)(2,1)}, bf16[8,1,8,128]{3,2,0,1:T(8,128)(2,1)S(1)}, u32[]{:S(2)}, u32[]{:S(2)}) collective-permute-start(bf16[8,1,8,128]{3,2,0,1:T(8,128)(2,1)} %get-tuple-element.162), channel_id=1, source_target_pairs={{8,0},{16,8},{24,16},{32,24},{40,32},{48,40},{56,48},{64,56},{72,6... | collective-permute-start | bytes 49160 | tf_op jit(solution)/shard_map/ppermute | solution.py:24
  43.3 11.4 %collective-permute-start.6 = (bf16[8,10,1,128]{3,2,0,1:T(2,128)(2,1)S(1)}, bf16[8,10,1,128]{3,2,0,1:T(2,128)(2,1)S(1)}, u32[]{:S(2)}, u32[]{:S(2)}) collective-permute-start(bf16[8,10,1,128]{3,2,0,1:T(2,128)(2,1)S(1)} %get-tuple-element.137), channel_id=1, source_target_pairs={{0,1},{1,2},{2,3},{3,4},{4,5},{5,6},{6,7},{8,9},{9,10},{10,11},{11... | collective-permute-start | bytes 61448 | tf_op jit(solution)/shard_map/ppermute | solution.py:21
  47.2 7.5 %collective-permute-start.7 = (bf16[8,10,1,128]{3,2,0,1:T(2,128)(2,1)S(1)}, bf16[8,10,1,128]{3,2,0,1:T(2,128)(2,1)S(1)}, u32[]{:S(2)}, u32[]{:S(2)}) collective-permute-start(bf16[8,10,1,128]{3,2,0,1:T(2,128)(2,1)S(1)} %get-tuple-element.138), channel_id=1, source_target_pairs={{1,0},{2,1},{3,2},{4,3},{5,4},{6,5},{7,6},{9,8},{10,9},{11,10},{12... | collective-permute-start | bytes 61448 | tf_op jit(solution)/shard_map/ppermute | solution.py:24
  49.4 8.6 %collective-permute-start.22 = (bf16[8,10,1,128]{3,2,0,1:T(2,128)(2,1)S(1)}, bf16[8,10,1,128]{3,2,0,1:T(2,128)(2,1)S(1)}, u32[]{:S(2)}, u32[]{:S(2)}) collective-permute-start(bf16[8,10,1,128]{3,2,0,1:T(2,128)(2,1)S(1)} %get-tuple-element.145), channel_id=1, source_target_pairs={{0,1},{1,2},{2,3},{3,4},{4,5},{5,6},{6,7},{8,9},{9,10},{10,11},{11... | collective-permute-start | bytes 61448 | tf_op jit(solution)/shard_map/ppermute | solution.py:21
  53.4 5.5 collective-permute-start.23
  55.8 4.2 copy-start.6
  61.2 15.7 %collective-permute-start.8 = (bf16[8,1,8,128]{3,2,0,1:T(8,128)(2,1)S(1)}, bf16[8,1,8,128]{3,2,0,1:T(8,128)(2,1)S(1)}, u32[]{:S(2)}, u32[]{:S(2)}) collective-permute-start(bf16[8,1,8,128]{3,2,0,1:T(8,128)(2,1)S(1)} %get-tuple-element.151), channel_id=1, source_target_pairs={{0,8},{8,16},{16,24},{24,32},{32,40},{40,48},{48,56},{56,64},{64,7... | collective-permute-start | bytes 49160 | tf_op jit(solution)/shard_map/ppermute | solution.py:21
  68.3 8.7 %collective-permute-start.9 = (bf16[8,1,8,128]{3,2,0,1:T(8,128)(2,1)S(1)}, bf16[8,1,8,128]{3,2,0,1:T(8,128)(2,1)S(1)}, u32[]{:S(2)}, u32[]{:S(2)}) collective-permute-start(bf16[8,1,8,128]{3,2,0,1:T(8,128)(2,1)S(1)} %get-tuple-element.152), channel_id=1, source_target_pairs={{8,0},{16,8},{24,16},{32,24},{40,32},{48,40},{56,48},{64,56},{72,6... | collective-permute-start | bytes 49160 | tf_op jit(solution)/shard_map/ppermute | solution.py:24
  70.3 11.6 %collective-permute-start.24 = (bf16[8,1,8,128]{3,2,0,1:T(8,128)(2,1)S(1)}, bf16[8,1,8,128]{3,2,0,1:T(8,128)(2,1)S(1)}, u32[]{:S(2)}, u32[]{:S(2)}) collective-permute-start(bf16[8,1,8,128]{3,2,0,1:T(8,128)(2,1)S(1)} %get-tuple-element.159), channel_id=1, source_target_pairs={{0,8},{8,16},{16,24},{24,32},{32,40},{40,48},{48,56},{56,64},{64,7... | collective-permute-start | bytes 49160 | tf_op jit(solution)/shard_map/ppermute | solution.py:21
  74.9 7.6 %collective-permute-start.25 = (bf16[8,1,8,128]{3,2,0,1:T(8,128)(2,1)S(1)}, bf16[8,1,8,128]{3,2,0,1:T(8,128)(2,1)S(1)}, u32[]{:S(2)}, u32[]{:S(2)}) collective-permute-start(bf16[8,1,8,128]{3,2,0,1:T(8,128)(2,1)S(1)} %get-tuple-element.160), channel_id=1, source_target_pairs={{8,0},{16,8},{24,16},{32,24},{40,32},{48,40},{56,48},{64,56},{72,6... | collective-permute-start | bytes 49160 | tf_op jit(solution)/shard_map/ppermute | solution.py:24
  77.0 12.1 %collective-permute-start.10 = (bf16[8,10,1,128]{3,2,0,1:T(2,128)(2,1)S(1)}, bf16[8,10,1,128]{3,2,0,1:T(2,128)(2,1)S(1)}, u32[]{:S(2)}, u32[]{:S(2)}) collective-permute-start(bf16[8,10,1,128]{3,2,0,1:T(2,128)(2,1)S(1)} %get-tuple-element.135), channel_id=1, source_target_pairs={{0,1},{1,2},{2,3},{3,4},{4,5},{5,6},{6,7},{8,9},{9,10},{10,11},{11... | collective-permute-start | bytes 61448 | tf_op jit(solution)/shard_map/ppermute | solution.py:21
  80.7 8.5 %collective-permute-start.11 = (bf16[8,10,1,128]{3,2,0,1:T(2,128)(2,1)S(1)}, bf16[8,10,1,128]{3,2,0,1:T(2,128)(2,1)S(1)}, u32[]{:S(2)}, u32[]{:S(2)}) collective-permute-start(bf16[8,10,1,128]{3,2,0,1:T(2,128)(2,1)S(1)} %get-tuple-element.136), channel_id=1, source_target_pairs={{1,0},{2,1},{3,2},{4,3},{5,4},{6,5},{7,6},{9,8},{10,9},{11,10},{12... | collective-permute-start | bytes 61448 | tf_op jit(solution)/shard_map/ppermute | solution.py:24
  82.6 8.3 %collective-permute-start.26 = (bf16[8,10,1,128]{3,2,0,1:T(2,128)(2,1)S(1)}, bf16[8,10,1,128]{3,2,0,1:T(2,128)(2,1)S(1)}, u32[]{:S(2)}, u32[]{:S(2)}) collective-permute-start(bf16[8,10,1,128]{3,2,0,1:T(2,128)(2,1)S(1)} %get-tuple-element.143), channel_id=1, source_target_pairs={{0,1},{1,2},{2,3},{3,4},{4,5},{5,6},{6,7},{8,9},{9,10},{10,11},{11... | collective-permute-start | bytes 61448 | tf_op jit(solution)/shard_map/ppermute | solution.py:21
  87.9 7.1 %collective-permute-start.27 = (bf16[8,10,1,128]{3,2,0,1:T(2,128)(2,1)S(1)}, bf16[8,10,1,128]{3,2,0,1:T(2,128)(2,1)S(1)}, u32[]{:S(2)}, u32[]{:S(2)}) collective-permute-start(bf16[8,10,1,128]{3,2,0,1:T(2,128)(2,1)S(1)} %get-tuple-element.144), channel_id=1, source_target_pairs={{1,0},{2,1},{3,2},{4,3},{5,4},{6,5},{7,6},{9,8},{10,9},{11,10},{12... | collective-permute-start | bytes 61448 | tf_op jit(solution)/shard_map/ppermute | solution.py:24
  96.6 16.5 %collective-permute-start.12 = (bf16[8,1,8,128]{3,2,0,1:T(8,128)(2,1)S(1)}, bf16[8,1,8,128]{3,2,0,1:T(8,128)(2,1)S(1)}, u32[]{:S(2)}, u32[]{:S(2)}) collective-permute-start(bf16[8,1,8,128]{3,2,0,1:T(8,128)(2,1)S(1)} %get-tuple-element.149), channel_id=1, source_target_pairs={{0,8},{8,16},{16,24},{24,32},{32,40},{40,48},{48,56},{56,64},{64,7... | collective-permute-start | bytes 49160 | tf_op jit(solution)/shard_map/ppermute | solution.py:21
  104.5 8.7 %collective-permute-start.13 = (bf16[8,1,8,128]{3,2,0,1:T(8,128)(2,1)S(1)}, bf16[8,1,8,128]{3,2,0,1:T(8,128)(2,1)S(1)}, u32[]{:S(2)}, u32[]{:S(2)}) collective-permute-start(bf16[8,1,8,128]{3,2,0,1:T(8,128)(2,1)S(1)} %get-tuple-element.150), channel_id=1, source_target_pairs={{8,0},{16,8},{24,16},{32,24},{40,32},{48,40},{56,48},{64,56},{72,6... | collective-permute-start | bytes 49160 | tf_op jit(solution)/shard_map/ppermute | solution.py:24
  106.6 11.6 %collective-permute-start.28 = (bf16[8,1,8,128]{3,2,0,1:T(8,128)(2,1)S(1)}, bf16[8,1,8,128]{3,2,0,1:T(8,128)(2,1)S(1)}, u32[]{:S(2)}, u32[]{:S(2)}) collective-permute-start(bf16[8,1,8,128]{3,2,0,1:T(8,128)(2,1)S(1)} %get-tuple-element.157), channel_id=1, source_target_pairs={{0,8},{8,16},{16,24},{24,32},{32,40},{40,48},{48,56},{56,64},{64,7... | collective-permute-start | bytes 49160 | tf_op jit(solution)/shard_map/ppermute | solution.py:21
  111.1 8.4 %collective-permute-start.29 = (bf16[8,1,8,128]{3,2,0,1:T(8,128)(2,1)S(1)}, bf16[8,1,8,128]{3,2,0,1:T(8,128)(2,1)S(1)}, u32[]{:S(2)}, u32[]{:S(2)}) collective-permute-start(bf16[8,1,8,128]{3,2,0,1:T(8,128)(2,1)S(1)} %get-tuple-element.158), channel_id=1, source_target_pairs={{8,0},{16,8},{24,16},{32,24},{40,32},{48,40},{56,48},{64,56},{72,6... | collective-permute-start | bytes 49160 | tf_op jit(solution)/shard_map/ppermute | solution.py:24
  113.3 12.3 %collective-permute-start.14 = (bf16[8,10,1,128]{3,2,0,1:T(2,128)(2,1)S(1)}, bf16[8,10,1,128]{3,2,0,1:T(2,128)(2,1)S(1)}, u32[]{:S(2)}, u32[]{:S(2)}) collective-permute-start(bf16[8,10,1,128]{3,2,0,1:T(2,128)(2,1)S(1)} %get-tuple-element.133), channel_id=1, source_target_pairs={{0,1},{1,2},{2,3},{3,4},{4,5},{5,6},{6,7},{8,9},{9,10},{10,11},{11... | collective-permute-start | bytes 61448 | tf_op jit(solution)/shard_map/ppermute | solution.py:21
  116.9 8.7 %collective-permute-start.15 = (bf16[8,10,1,128]{3,2,0,1:T(2,128)(2,1)S(1)}, bf16[8,10,1,128]{3,2,0,1:T(2,128)(2,1)S(1)}, u32[]{:S(2)}, u32[]{:S(2)}) collective-permute-start(bf16[8,10,1,128]{3,2,0,1:T(2,128)(2,1)S(1)} %get-tuple-element.134), channel_id=1, source_target_pairs={{1,0},{2,1},{3,2},{4,3},{5,4},{6,5},{7,6},{9,8},{10,9},{11,10},{12... | collective-permute-start | bytes 61448 | tf_op jit(solution)/shard_map/ppermute | solution.py:24
  119.5 7.7 %collective-permute-start.30 = (bf16[8,10,1,128]{3,2,0,1:T(2,128)(2,1)S(1)}, bf16[8,10,1,128]{3,2,0,1:T(2,128)(2,1)S(1)}, u32[]{:S(2)}, u32[]{:S(2)}) collective-permute-start(bf16[8,10,1,128]{3,2,0,1:T(2,128)(2,1)S(1)} %get-tuple-element.141), channel_id=1, source_target_pairs={{0,1},{1,2},{2,3},{3,4},{4,5},{5,6},{6,7},{8,9},{9,10},{10,11},{11... | collective-permute-start | bytes 61448 | tf_op jit(solution)/shard_map/ppermute | solution.py:21
  124.1 7.1 %collective-permute-start.31 = (bf16[8,10,1,128]{3,2,0,1:T(2,128)(2,1)S(1)}, bf16[8,10,1,128]{3,2,0,1:T(2,128)(2,1)S(1)}, u32[]{:S(2)}, u32[]{:S(2)}) collective-permute-start(bf16[8,10,1,128]{3,2,0,1:T(2,128)(2,1)S(1)} %get-tuple-element.142), channel_id=1, source_target_pairs={{1,0},{2,1},{3,2},{4,3},{5,4},{6,5},{7,6},{9,8},{10,9},{11,10},{12... | collective-permute-start | bytes 61448 | tf_op jit(solution)/shard_map/ppermute | solution.py:24
  132.8 17.1 %collective-permute-start.16 = (bf16[8,1,8,128]{3,2,0,1:T(8,128)(2,1)S(1)}, bf16[8,1,8,128]{3,2,0,1:T(8,128)(2,1)S(1)}, u32[]{:S(2)}, u32[]{:S(2)}) collective-permute-start(bf16[8,1,8,128]{3,2,0,1:T(8,128)(2,1)S(1)} %get-tuple-element.147), channel_id=1, source_target_pairs={{0,8},{8,16},{16,24},{24,32},{32,40},{40,48},{48,56},{56,64},{64,7... | collective-permute-start | bytes 49160 | tf_op jit(solution)/shard_map/ppermute | solution.py:21
  141.2 8.7 %collective-permute-start.17 = (bf16[8,1,8,128]{3,2,0,1:T(8,128)(2,1)S(1)}, bf16[8,1,8,128]{3,2,0,1:T(8,128)(2,1)S(1)}, u32[]{:S(2)}, u32[]{:S(2)}) collective-permute-start(bf16[8,1,8,128]{3,2,0,1:T(8,128)(2,1)S(1)} %get-tuple-element.148), channel_id=1, source_target_pairs={{8,0},{16,8},{24,16},{32,24},{40,32},{48,40},{56,48},{64,56},{72,6... | collective-permute-start | bytes 49160 | tf_op jit(solution)/shard_map/ppermute | solution.py:24
  143.3 11.6 %collective-permute-start.32 = (bf16[8,1,8,128]{3,2,0,1:T(8,128)(2,1)S(1)}, bf16[8,1,8,128]{3,2,0,1:T(8,128)(2,1)S(1)}, u32[]{:S(2)}, u32[]{:S(2)}) collective-permute-start(bf16[8,1,8,128]{3,2,0,1:T(8,128)(2,1)S(1)} %get-tuple-element.155), channel_id=1, source_target_pairs={{0,8},{8,16},{16,24},{24,32},{32,40},{40,48},{48,56},{56,64},{64,7... | collective-permute-start | bytes 49160 | tf_op jit(solution)/shard_map/ppermute | solution.py:21
  147.9 8.4 %collective-permute-start.33 = (bf16[8,1,8,128]{3,2,0,1:T(8,128)(2,1)S(1)}, bf16[8,1,8,128]{3,2,0,1:T(8,128)(2,1)S(1)}, u32[]{:S(2)}, u32[]{:S(2)}) collective-permute-start(bf16[8,1,8,128]{3,2,0,1:T(8,128)(2,1)S(1)} %get-tuple-element.156), channel_id=1, source_target_pairs={{8,0},{16,8},{24,16},{32,24},{40,32},{48,40},{56,48},{64,56},{72,6... | collective-permute-start | bytes 49160 | tf_op jit(solution)/shard_map/ppermute | solution.py:24
  150.0 11.2 %collective-permute-start.18 = (bf16[8,10,1,128]{3,2,0,1:T(2,128)(2,1)S(1)}, bf16[8,10,1,128]{3,2,0,1:T(2,128)(2,1)S(1)}, u32[]{:S(2)}, u32[]{:S(2)}) collective-permute-start(bf16[8,10,1,128]{3,2,0,1:T(2,128)(2,1)S(1)} %get-tuple-element.131), channel_id=1, source_target_pairs={{0,1},{1,2},{2,3},{3,4},{4,5},{5,6},{6,7},{8,9},{9,10},{10,11},{11... | collective-permute-start | bytes 61448 | tf_op jit(solution)/shard_map/ppermute | solution.py:21
  153.7 7.6 %collective-permute-start.19 = (bf16[8,10,1,128]{3,2,0,1:T(2,128)(2,1)S(1)}, bf16[8,10,1,128]{3,2,0,1:T(2,128)(2,1)S(1)}, u32[]{:S(2)}, u32[]{:S(2)}) collective-permute-start(bf16[8,10,1,128]{3,2,0,1:T(2,128)(2,1)S(1)} %get-tuple-element.132), channel_id=1, source_target_pairs={{1,0},{2,1},{3,2},{4,3},{5,4},{6,5},{7,6},{9,8},{10,9},{11,10},{12... | collective-permute-start | bytes 61448 | tf_op jit(solution)/shard_map/ppermute | solution.py:24
  156.3 17.0 %collective-permute-start.34 = (bf16[8,10,1,128]{3,2,0,1:T(2,128)(2,1)S(1)}, bf16[8,10,1,128]{3,2,0,1:T(2,128)(2,1)S(1)}, u32[]{:S(2)}, u32[]{:S(2)}) collective-permute-start(bf16[8,10,1,128]{3,2,0,1:T(2,128)(2,1)S(1)} %get-tuple-element.139), channel_id=1, source_target_pairs={{0,1},{1,2},{2,3},{3,4},{4,5},{5,6},{6,7},{8,9},{9,10},{10,11},{11... | collective-permute-start | bytes 61448 | tf_op jit(solution)/shard_map/ppermute | solution.py:21
  159.9 13.4 %collective-permute-start.35 = (bf16[8,10,1,128]{3,2,0,1:T(2,128)(2,1)S(1)}, bf16[8,10,1,128]{3,2,0,1:T(2,128)(2,1)S(1)}, u32[]{:S(2)}, u32[]{:S(2)}) collective-permute-start(bf16[8,10,1,128]{3,2,0,1:T(2,128)(2,1)S(1)} %get-tuple-element.140), channel_id=1, source_target_pairs={{1,0},{2,1},{3,2},{4,3},{5,4},{6,5},{7,6},{9,8},{10,9},{11,10},{12... | collective-permute-start | bytes 61448 | tf_op jit(solution)/shard_map/ppermute | solution.py:24
  161.6 12.1 %copy-start.11 = (f32[128]{0:T(128)S(1)}, f32[128]{0:T(128)}, u32[]{:S(2)}) copy-start(f32[128]{0:T(128)} %get-tuple-element.201) | copy-start | bytes 1540
  161.6 12.1 %copy-start.13 = (f32[128]{0:T(128)S(1)}, f32[128]{0:T(128)}, u32[]{:S(2)}) copy-start(f32[128]{0:T(128)} %get-tuple-element.202) | copy-start | bytes 1540
  164.2 17.6 %all-to-all-start = ((bf16[32,8,8,128]{3,2,0,1:T(8,128)(2,1)}), bf16[32,8,8,128]{3,2,0,1:T(8,128)(2,1)S(1)}, u32[]{:S(2)}, u32[]{:S(2)}) async-start(bf16[32,8,8,128]{3,2,0,1:T(8,128)(2,1)} %pad_maximum_fusion.1), calls=%async_computation | async-start | bytes 1048576 | tf_op jit(solution)/shard_map/all_to_all | solution.py:164
  173.3 1.4 copy-start.5
  181.8 260.6 %all-to-all-start.1 = ((bf16[32,8,8,128]{3,2,0,1:T(8,128)(2,1)}), bf16[32,8,8,128]{3,2,0,1:T(8,128)(2,1)S(1)}, u32[]{:S(2)}, u32[]{:S(2)}) async-start(bf16[32,8,8,128]{3,2,0,1:T(8,128)(2,1)} %pad_maximum_fusion.2), calls=%async_computation.1 | async-start | bytes 1048576 | tf_op jit(solution)/shard_map/all_to_all | solution.py:164
  278.1 83.5 %copy-start.7 = (f32[256,256]{1,0:T(8,128)S(1)}, f32[256,256]{1,0:T(8,128)}, u32[]{:S(2)}) copy-start(f32[256,256]{1,0:T(8,128)} %fusion.74) | copy-start | bytes 786436
  281.6 118.2 %copy-start.16 = (s32[2]{0:T(128)S(1)}, s32[2]{0:T(128)}, u32[]{:S(2)}) copy-start(s32[2]{0:T(128)} %iota_multiply_fusion) | copy-start | bytes 28
  670.4 6.8 %copy-start.1 = (f32[16,256]{1,0:T(8,128)S(1)}, f32[16,256]{1,0:T(8,128)}, u32[]{:S(2)}) copy-start(f32[16,256]{1,0:T(8,128)} %param.17) | copy-start | bytes 49156
where the time goes:
time: 688 us; the launch traced here: 678 us
  blocking collectives  312 us (45%)
  other arithmetic  146 us (21%)
  starting transfers between devices  129 us (19%)
  matrix products  47.9 us (7%)
  local copies, waits for them, and re-layouts  19.7 us (3%)
  waiting for transfers between devices  17.6 us (3%)
    psum x2, blocking collectives, compress(): coeffs = lax.psum(local_proj, ('gx', 'sec')) / rows_total  163 us
    psum x2, blocking collectives, compress(): lax.psum(jnp.dot(resid, resid.T, precision=lax.Precision.HIGHEST), ('gx',...  149 us
    ppermute x18, starting transfers between devices, with_halo(): lax.ppermute(lax.slice_in_dim(block, block.shape[dim] - width, None, axis...  87.7 us
    another operation x14, other arithmetic, small_rotation(): factor = jnp.linalg.cholesky(inner)  69.6 us
    another operation x5, other arithmetic, small_rotation(): lax.linalg.triangular_solve(factor, leading.T, left_side=True, lower=True)  40 us
    ppermute x18, starting transfers between devices, with_halo(): lax.ppermute(lax.slice_in_dim(block, 0, width, axis=dim), axis, backward)  29.1 us
  transfers between devices with their start and end apart: 38, of which 8 were waited for; matrix products, arithmetic and copies ran while one was open for 18% of the time, Pallas kernels for 0%

commit v1 on v0

--- a/solution.py
+++ b/solution.py
@@ -53,46 +53,50 @@
     return fields + step_sizes * spread + DT_ADVECT * is_sat * carried + DT_PRESSURE * inflow
 
 
-def small_rotation(coeffs, lower, sigma):
-    count = sigma.shape[0]
-    extra = lower.shape[0]
-    top = jnp.concatenate([jnp.diag(sigma), coeffs.T], 1)
-    bottom = jnp.concatenate([jnp.zeros((extra, count), sigma.dtype), lower.T], 1)
-    core = jnp.concatenate([top, bottom], 0)
-    leading = jnp.dot(core, top.T, precision=lax.Precision.HIGHEST)
-    inner = jnp.dot(leading.T, leading, precision=lax.Precision.HIGHEST)
+HIGH = lax.Precision.HIGHEST
+
+
+def hdot(a, b):
+    return jnp.dot(a, b, precision=HIGH)
+
+
+def batch_update(coeffs, gram_of, sigma):
+    rounded = coeffs.astype(jnp.bfloat16).astype(jnp.float32)
+    gram = gram_of(coeffs, rounded)
+    square = jnp.diag(sigma * sigma)
+    total = square + hdot(coeffs.T, coeffs)
+    inner = hdot(total, total) + hdot(coeffs.T, hdot(gram, coeffs))
     factor = jnp.linalg.cholesky(inner)
-    rotation = lax.linalg.triangular_solve(factor, leading.T, left_side=True, lower=True).T
-    energy = jnp.dot(core.T, rotation, precision=lax.Precision.HIGHEST)
-    return (rotation, jnp.sqrt(jnp.sum(energy * energy, axis=0)))
-
-
-def compress(stacked, basis_now, sigma, rows_total):
-    count = stacked.shape[0]
-    snaps = stacked.reshape(count, -1)
-    flat_basis = basis_now.reshape(snaps.shape[1], basis_now.shape[-1])
-    basis_count = flat_basis.shape[1]
-    local_proj = jnp.dot(snaps, flat_basis, preferred_element_type=jnp.float32)
-    coeffs = lax.psum(local_proj, ("gx", "sec")) / rows_total
-    rounded = coeffs.astype(jnp.bfloat16)
-    resid = snaps.astype(jnp.float32) - lax.dot_general(
-        rounded, flat_basis, (((1,), (1,)), ((), ())), preferred_element_type=jnp.float32
-    )
-    gram = (
-        lax.psum(jnp.dot(resid, resid.T, precision=lax.Precision.HIGHEST), ("gx", "sec"))
-        / rows_total
-    )
-    lower = jnp.linalg.cholesky(gram)
-    ortho = lax.linalg.triangular_solve(lower, resid, left_side=True, lower=True).astype(
-        jnp.bfloat16
-    )
-    rotation, sigma_next = small_rotation(coeffs, lower, sigma)
-    mixing = rotation.astype(jnp.bfloat16)
-    fresh = jnp.dot(flat_basis, mixing[:basis_count], preferred_element_type=jnp.float32)
-    fresh = fresh + lax.dot_general(
-        ortho, mixing[basis_count:], (((0,), (0,)), ((), ())), preferred_element_type=jnp.float32
-    )
-    return (fresh.astype(jnp.bfloat16).reshape(basis_now.shape), sigma_next)
+    eye = jnp.eye(sigma.shape[0], dtype=jnp.float32)
+    back = lax.linalg.triangular_solve(factor, eye, left_side=True, lower=True).T
+    top = sigma[:, None] * hdot(total, back)
+    bottom = hdot(hdot(coeffs, total) + hdot(gram, coeffs), back)
+    sigma_next = jnp.sqrt(jnp.sum(top * top, axis=0) + jnp.sum(bottom * bottom, axis=0))
+    on_basis = hdot(square + hdot((coeffs - rounded).T, coeffs), back)
+    on_snaps = hdot(coeffs, back)
+    return on_basis, on_snaps, sigma_next
+
+
+def small_algebra(uu, su, ss, sigma):
+    half = su.shape[0] // 2
+    s00, s10, s11 = ss[:half, :half], ss[half:, :half], ss[half:, half:]
+
+    def gram_first(c, r):
+        cr = hdot(c, r.T)
+        return s00 - cr - cr.T + hdot(r, hdot(uu, r.T))
+
+    wu, ws, sigma1 = batch_update(su[:half], gram_first, sigma)
+    coeffs1 = hdot(su[half:], wu) + hdot(s10, ws)
+
+    def gram_second(c, r):
+        cr = hdot(c, r.T)
+        yu, ys = hdot(wu, r.T), hdot(ws, r.T)
+        mixed = hdot(ys.T, hdot(su[:half], yu))
+        own = hdot(yu.T, hdot(uu, yu)) + mixed + mixed.T + hdot(ys.T, hdot(s00, ys))
+        return s11 - cr - cr.T + own
+
+    wu1, ws1, sigma2 = batch_update(coeffs1, gram_second, sigma1)
+    return hdot(wu, wu1), hdot(ws, wu1), ws1, sigma2
 
 
 def body(state_init, rock_type, perm_table, well_cells, well_rate, basis_in, singular):
@@ -136,9 +140,8 @@
     source_full = jnp.concatenate([source, jnp.zeros_like(source)], -1)
     local_rows = basis_in.shape[0] * basis_in.shape[1] * basis_in.shape[2]
     rows_total = local_rows * lax.axis_size("gx") * sec_count
-    basis_now = basis_in
-    sigma = singular
     finals = []
+    snaps = []
     for group in range(GROUPS):
         fields = state_init[group * MG : (group + 1) * MG]
         inflow = source_full[group * MG : (group + 1) * MG]
@@ -162,7 +165,23 @@
         finals.append(fields)
         stacked = jnp.concatenate(saved, 0)
         stacked = lax.all_to_all(stacked, "sec", split_axis=1, concat_axis=2, tiled=True)
-        basis_now, sigma = compress(stacked, basis_now, sigma, rows_total)
+        snaps.append(stacked.reshape(stacked.shape[0], -1))
+    both = jnp.concatenate(snaps, 0)
+    basis = basis_in.reshape(both.shape[1], basis_in.shape[-1])
+    count = basis.shape[1]
+    uu = lax.dot_general(basis, basis, (((0,), (0,)), ((), ())), preferred_element_type=jnp.float32)
+    su = jnp.dot(both, basis, preferred_element_type=jnp.float32)
+    ss = lax.dot_general(both, both, (((1,), (1,)), ((), ())), preferred_element_type=jnp.float32)
+    local = jnp.concatenate([jnp.concatenate([uu, su], 0), jnp.pad(jnp.concatenate([jnp.zeros((count, both.shape[0]), jnp.float32), ss], 0), ((0, 0), (0, 64)))], 1)
+    whole = lax.psum(local, ("gx", "sec")) / rows_total
+    w0, w1, w2, sigma = small_algebra(
+        whole[:count, :count], whole[count:, :count], whole[count:, count : count + both.shape[0]], singular
+    )
+    fresh = jnp.dot(basis, w0.astype(jnp.bfloat16), preferred_element_type=jnp.float32)
+    fresh = fresh + lax.dot_general(
+        both, jnp.concatenate([w1, w2], 0).astype(jnp.bfloat16), (((0,), (0,)), ((), ())), preferred_element_type=jnp.float32
+    )
+    basis_now = fresh.astype(jnp.bfloat16).reshape(basis_in.shape)
     return (jnp.concatenate(finals, 0), basis_now, sigma)
 
 

time: 688 us -> 635 us (0.923)
  blocking collectives: 312 us -> 0 us
  waiting for transfers between devices: 17.6 us -> 289 us
  matrix products: 47.9 us -> 30.2 us
  other arithmetic: 146 us -> 131 us
  between operations: 5.16 us -> 18.6 us
  local copies, waits for them, and re-layouts: 19.7 us -> 27.9 us
    psum x4 -> x0, blocking collectives: 312 us -> none  [the longest x2 163 us: compress(): coeffs = lax.psum(local_proj, ('gx', 'sec')) / rows_total]
    psum x0 -> x1, waiting for transfers between devices: none -> 262 us  [body(): whole = lax.psum(local, ('gx', 'sec')) / rows_total]
    dot_general x16 -> x41, matrix products: 40.1 us -> 24.4 us  [the longest x36 10.9 us: hdot(): return jnp.dot(a, b, precision=HIGH)]
    another operation x31 -> x21, other arithmetic: 123 us -> 109 us  [the longest x14 69.7 us: batch_update(): factor = jnp.linalg.cholesky(inner)]
    all_to_all x2, waiting for transfers between devices: 5.36 us -> 13.5 us  [body(): lax.all_to_all(stacked, 'sec', split_axis=1, concat_axis=2, tiled=True)]
    unnamed x37 -> x31, local copies, waits for them, and re-layouts: 1.65 us -> 8.88 us
  transfers between devices with their start and end apart: 38 -> 39, of which waited for: 8 -> 9; matrix products, arithmetic and copies ran while one was open for 18% -> 5% of each run, Pallas kernels for 0% -> 0%
where the time goes in v1:
time: 635 us; the launch traced here: 625 us
  waiting for transfers between devices  289 us (46%)
  other arithmetic  131 us (21%)
  starting transfers between devices  129 us (20%)
  matrix products  30.2 us (5%)
  local copies, waits for them, and re-layouts  27.9 us (4%)
  between operations  18.6 us (3%)
    psum x1, waiting for transfers between devices, body(): whole = lax.psum(local, ('gx', 'sec')) / rows_total  262 us
    ppermute x18, starting transfers between devices, with_halo(): lax.ppermute(lax.slice_in_dim(block, block.shape[dim] - width, None, axis...  87.2 us
    another operation x14, other arithmetic, batch_update(): factor = jnp.linalg.cholesky(inner)  69.7 us
    another operation x5, other arithmetic, batch_update(): lax.linalg.triangular_solve(factor, eye, left_side=True, lower=True)  39.4 us
    ppermute x18, starting transfers between devices, with_halo(): lax.ppermute(lax.slice_in_dim(block, 0, width, axis=dim), axis, backward)  29.1 us
    all_to_all x2, waiting for transfers between devices, body(): lax.all_to_all(stacked, 'sec', split_axis=1, concat_axis=2, tiled=True)  13.5 us
    ppermute x18, waiting for transfers between devices, with_halo(): lax.ppermute(lax.slice_in_dim(block, 0, width, axis=dim), axis, backward)  12.9 us
  transfers between devices with their start and end apart: 39, of which 9 were waited for; matrix products, arithmetic and copies ran while one was open for 5% of the time, Pallas kernels for 0%

profile of v1, /device:TPU:1, one launch (start us, length us, event | category | flops | bytes accessed | tf_op | source)
XLA Modules:
  0.0 625.5 jit_solution(13930910843129405325)
XLA Ops:
  9.1 6.3 %collective-permute-start = (bf16[1,8,128]{2,1,0:T(8,128)(2,1)}, bf16[1,8,128]{2,1,0:T(8,128)(2,1)}, u32[]{:S(2)}, u32[]{:S(2)}) collective-permute-start(bf16[1,8,128]{2,1,0:T(8,128)(2,1)} %get-tuple-element.185), channel_id=1, source_target_pairs={{0,8},{8,16},{16,24},{24,32},{32,40},{40,48},{48,56},{56,64},{64,7... | collective-permute-start | bytes 6152 | tf_op jit(solution)/shard_map/ppermute | solution.py:21
  15.4 1.9 collective-permute-start.1
  19.0 4.5 collective-permute-start.4
  23.6 1.9 collective-permute-start.5
  26.1 4.5 collective-permute-start.20
  30.6 2.2 fusion.153
  33.5 5.5 fusion.8
  40.5 2.1 convolution_bitcast_fusion.1
  43.5 3.2 collective-permute-start.2
  46.7 1.3 collective-permute-start.3
  49.8 1.9 collective-permute-start.21
  53.7 4.0 collective-permute-start.6
  57.7 1.3 collective-permute-start.7
  59.0 4.0 collective-permute-start.22
  63.0 1.3 collective-permute-start.23
  65.4 2.0 fusion.139
  70.1 6.9 %collective-permute-start.8 = (bf16[8,1,8,128]{3,2,0,1:T(8,128)(2,1)S(1)}, bf16[8,1,8,128]{3,2,0,1:T(8,128)(2,1)S(1)}, u32[]{:S(2)}, u32[]{:S(2)}) collective-permute-start(bf16[8,1,8,128]{3,2,0,1:T(8,128)(2,1)S(1)} %get-tuple-element.157), channel_id=1, source_target_pairs={{0,8},{8,16},{16,24},{24,32},{32,40},{40,48},{48,56},{56,64},{64,7... | collective-permute-start | bytes 49160 | tf_op jit(solution)/shard_map/ppermute | solution.py:21
  77.0 1.9 collective-permute-start.9
  79.1 4.5 collective-permute-start.24
  83.6 1.9 collective-permute-start.25
  85.8 3.3 collective-permute-start.10
  89.0 1.3 collective-permute-start.11
  91.5 5.3 collective-permute-start.26
  96.8 1.5 collective-permute-start.27
  99.9 4.0 collective-permute-done.27
  105.6 7.8 %collective-permute-start.12 = (bf16[8,1,8,128]{3,2,0,1:T(8,128)(2,1)S(1)}, bf16[8,1,8,128]{3,2,0,1:T(8,128)(2,1)S(1)}, u32[]{:S(2)}, u32[]{:S(2)}) collective-permute-start(bf16[8,1,8,128]{3,2,0,1:T(8,128)(2,1)S(1)} %get-tuple-element.155), channel_id=1, source_target_pairs={{0,8},{8,16},{16,24},{24,32},{32,40},{40,48},{48,56},{56,64},{64,7... | collective-permute-start | bytes 49160 | tf_op jit(solution)/shard_map/ppermute | solution.py:21
  113.4 1.9 collective-permute-start.13
  115.5 4.5 collective-permute-start.28
  120.0 1.9 collective-permute-start.29
  122.2 3.6 collective-permute-start.14
  125.8 1.3 collective-permute-start.15
  128.5 4.5 collective-permute-start.30
  133.0 1.3 collective-permute-start.31
  135.9 4.2 collective-permute-done.31
  141.7 8.4 %collective-permute-start.16 = (bf16[8,1,8,128]{3,2,0,1:T(8,128)(2,1)S(1)}, bf16[8,1,8,128]{3,2,0,1:T(8,128)(2,1)S(1)}, u32[]{:S(2)}, u32[]{:S(2)}) collective-permute-start(bf16[8,1,8,128]{3,2,0,1:T(8,128)(2,1)S(1)} %get-tuple-element.153), channel_id=1, source_target_pairs={{0,8},{8,16},{16,24},{24,32},{32,40},{40,48},{48,56},{56,64},{64,7... | collective-permute-start | bytes 49160 | tf_op jit(solution)/shard_map/ppermute | solution.py:21
  150.1 1.9 collective-permute-start.17
  152.2 4.5 collective-permute-start.32
  156.8 1.9 collective-permute-start.33
  158.8 3.6 collective-permute-start.18
  162.4 1.3 collective-permute-start.19
  163.7 1.4 collective-permute-done.33
  165.2 3.6 collective-permute-start.34
  172.4 9.0 %all-to-all-start = ((bf16[32,8,8,128]{3,2,0,1:T(8,128)(2,1)}), bf16[32,8,8,128]{3,2,0,1:T(8,128)(2,1)S(1)}, u32[]{:S(2)}, u32[]{:S(2)}) async-start(bf16[32,8,8,128]{3,2,0,1:T(8,128)(2,1)} %pad_maximum_fusion.1), calls=%async_computation | async-start | bytes 1048576 | tf_op jit(solution)/shard_map/all_to_all | solution.py:167
  183.8 6.1 all-to-all-done
  189.9 3.5 all-to-all-start.1
  194.3 7.3 %all-to-all-done.1 = bf16[32,8,8,128]{3,2,0,1:T(8,128)(2,1)S(1)} async-done(((bf16[32,8,8,128]{3,2,0,1:T(8,128)(2,1)}), bf16[32,8,8,128]{3,2,0,1:T(8,128)(2,1)S(1)}, u32[]{:S(2)}, u32[]{:S(2)}) %all-to-all-start.1) | async-done | bytes 524320 | tf_op jit(solution)/shard_map/all_to_all | solution.py:167
  206.4 262.3 %all-reduce.23.cloned.1.call-done = f32[320,384]{1,0:T(8,128)} async-done(((f32[320,384]{1,0:T(8,128)}), f32[320,384]{1,0:T(8,128)}) %all-reduce.23.cloned.1.call-update) | async-done | bytes 491536 | tf_op jit(solution)/shard_map/psum | solution.py:176
  473.0 11.7 %cholesky.130 = f32[128,128]{1,0:T(8,128)S(1)} custom-call(f32[128,128]{1,0:T(8,128)S(1)} %cholesky.194), custom_call_target="Cholesky" | custom-call | tf_op jit(solution)/shard_map/jit(cholesky)/cholesky | solution.py:69
  485.4 9.8 %custom-call.13 = f32[1,128,128]{1,2,0:T(8,128)S(1)} custom-call(f32[1,128,128]{2,1,0:T(8,128)S(1)} %get-tuple-element.182), custom_call_target="InvertDiagBlocksLowerTriangular" | custom-call | tf_op jit(solution)/shard_map/jit(cholesky)/cholesky | solution.py:69
  495.7 11.9 %cholesky.147 = f32[128,128]{1,0:T(8,128)S(1)} custom-call(f32[128,128]{1,0:T(8,128)S(1)} %convolution_subtract_fusion.3), custom_call_target="Cholesky" | custom-call | tf_op jit(solution)/shard_map/jit(cholesky)/cholesky | solution.py:69
  509.8 4.1 while.4
  510.4 1.4 bitcast_dynamic-update-slice_fusion.6
  512.5 1.4 bitcast_dynamic-update-slice_fusion.6
  513.9 19.7 %custom-call.14 = f32[2,128,128]{1,2,0:T(8,128)S(1)} custom-call(f32[2,128,128]{2,1,0:T(8,128)S(1)} %get-tuple-element.19), custom_call_target="InvertDiagBlocksLowerTriangular" | custom-call | tf_op jit(solution)/shard_map/triangular_solve/custom-call.0 | solution.py:71
  540.9 11.7 %cholesky.164 = f32[128,128]{1,0:T(8,128)S(1)} custom-call(f32[128,128]{1,0:T(8,128)S(1)} %cholesky.197), custom_call_target="Cholesky" | custom-call | tf_op jit(solution)/shard_map/jit(cholesky)/cholesky | solution.py:69
  553.3 9.8 %custom-call.15 = f32[1,128,128]{1,2,0:T(8,128)S(1)} custom-call(f32[1,128,128]{2,1,0:T(8,128)S(1)} %get-tuple-element.178), custom_call_target="InvertDiagBlocksLowerTriangular" | custom-call | tf_op jit(solution)/shard_map/jit(cholesky)/cholesky | solution.py:69
  563.7 11.9 %cholesky.181 = f32[128,128]{1,0:T(8,128)S(1)} custom-call(f32[128,128]{1,0:T(8,128)S(1)} %convolution_subtract_fusion.2), custom_call_target="Cholesky" | custom-call | tf_op jit(solution)/shard_map/jit(cholesky)/cholesky | solution.py:69
  577.7 4.1 while.5
  578.4 1.4 bitcast_dynamic-update-slice_fusion.7
  580.4 1.4 bitcast_dynamic-update-slice_fusion.7
  581.8 19.7 %custom-call.16 = f32[2,128,128]{1,2,0:T(8,128)S(1)} custom-call(f32[2,128,128]{2,1,0:T(8,128)S(1)} %get-tuple-element.20), custom_call_target="InvertDiagBlocksLowerTriangular" | custom-call | tf_op jit(solution)/shard_map/triangular_solve/custom-call.0 | solution.py:71
  604.6 3.5 convolution_bitcast_fusion
  608.2 3.3 fusion
  611.5 6.4 %copy.82 = bf16[8192,256]{1,0:T(8,128)(2,1)} copy(bf16[8192,256]{0,1:T(8,128)(2,1)} %fusion) | data formatting | bytes 8388608
  (242 shorter events, 57.1 us)
Async XLA Ops:
  7.2 33.3 %copy-start = (f32[16,256]{1,0:T(8,128)S(1)}, f32[16,256]{1,0:T(8,128)}, u32[]{:S(2)}) copy-start(f32[16,256]{1,0:T(8,128)} %param.14) | copy-start | bytes 49156
  7.2 25.7 %copy-start.3 = (f32[16,8,8,128]{3,2,1,0:T(8,128)S(1)}, f32[16,8,8,128]{3,2,1,0:T(8,128)}, u32[]{:S(2)}) copy-start(f32[16,8,8,128]{3,2,1,0:T(8,128)} %param.10) | copy-start | bytes 1572868
  9.1 33.5 %collective-permute-start = (bf16[1,8,128]{2,1,0:T(8,128)(2,1)}, bf16[1,8,128]{2,1,0:T(8,128)(2,1)}, u32[]{:S(2)}, u32[]{:S(2)}) collective-permute-start(bf16[1,8,128]{2,1,0:T(8,128)(2,1)} %get-tuple-element.185), channel_id=1, source_target_pairs={{0,8},{8,16},{16,24},{24,32},{32,40},{40,48},{48,56},{56,64},{64,7... | collective-permute-start | bytes 6152 | tf_op jit(solution)/shard_map/ppermute | solution.py:21
  15.4 27.3 %collective-permute-start.1 = (bf16[1,8,128]{2,1,0:T(8,128)(2,1)}, bf16[1,8,128]{2,1,0:T(8,128)(2,1)}, u32[]{:S(2)}, u32[]{:S(2)}) collective-permute-start(bf16[1,8,128]{2,1,0:T(8,128)(2,1)} %get-tuple-element.186), channel_id=1, source_target_pairs={{8,0},{16,8},{24,16},{32,24},{40,32},{48,40},{56,48},{64,56},{72,6... | collective-permute-start | bytes 6152 | tf_op jit(solution)/shard_map/ppermute | solution.py:24
  19.0 33.8 %collective-permute-start.4 = (bf16[8,1,8,128]{3,2,0,1:T(8,128)(2,1)}, bf16[8,1,8,128]{3,2,0,1:T(8,128)(2,1)S(1)}, u32[]{:S(2)}, u32[]{:S(2)}) collective-permute-start(bf16[8,1,8,128]{3,2,0,1:T(8,128)(2,1)} %get-tuple-element.159), channel_id=1, source_target_pairs={{0,8},{8,16},{16,24},{24,32},{32,40},{40,48},{48,56},{56,64},{64,7... | collective-permute-start | bytes 49160 | tf_op jit(solution)/shard_map/ppermute | solution.py:21
  23.6 29.2 %collective-permute-start.5 = (bf16[8,1,8,128]{3,2,0,1:T(8,128)(2,1)}, bf16[8,1,8,128]{3,2,0,1:T(8,128)(2,1)}, u32[]{:S(2)}, u32[]{:S(2)}) collective-permute-start(bf16[8,1,8,128]{3,2,0,1:T(8,128)(2,1)} %get-tuple-element.160), channel_id=1, source_target_pairs={{8,0},{16,8},{24,16},{32,24},{40,32},{48,40},{56,48},{64,56},{72,6... | collective-permute-start | bytes 49160 | tf_op jit(solution)/shard_map/ppermute | solution.py:24
  26.1 32.9 %collective-permute-start.20 = (bf16[8,1,8,128]{3,2,0,1:T(8,128)(2,1)}, bf16[8,1,8,128]{3,2,0,1:T(8,128)(2,1)S(1)}, u32[]{:S(2)}, u32[]{:S(2)}) collective-permute-start(bf16[8,1,8,128]{3,2,0,1:T(8,128)(2,1)} %get-tuple-element.167), channel_id=1, source_target_pairs={{0,8},{8,16},{16,24},{24,32},{32,40},{40,48},{48,56},{56,64},{64,7... | collective-permute-start | bytes 49160 | tf_op jit(solution)/shard_map/ppermute | solution.py:21
  33.5 7.0 %copy-start.13 = (s32[256]{0:T(256)S(1)}, s32[256]{0:T(256)}, u32[]{:S(2)}) copy-start(s32[256]{0:T(256)} %param.13) | copy-start | bytes 3076
  40.5 24.9 %copy-start.4 = (f32[8,8,8,128]{3,2,1,0:T(8,128)S(1)}, f32[8,8,8,128]{3,2,1,0:T(8,128)}, u32[]{:S(2)}) copy-start(f32[8,8,8,128]{3,2,1,0:T(8,128)} %get-tuple-element.193) | copy-start | bytes 786436
  40.5 24.9 %copy-start.5 = (f32[8,8,8,128]{3,2,1,0:T(8,128)S(1)}, f32[8,8,8,128]{3,2,1,0:T(8,128)}, u32[]{:S(2)}) copy-start(f32[8,8,8,128]{3,2,1,0:T(8,128)} %get-tuple-element.194) | copy-start | bytes 786436
  43.5 6.3 %collective-permute-start.2 = (bf16[10,1,128]{2,1,0:T(2,128)(2,1)S(1)}, bf16[10,1,128]{2,1,0:T(2,128)(2,1)S(1)}, u32[]{:S(2)}, u32[]{:S(2)}) collective-permute-start(bf16[10,1,128]{2,1,0:T(2,128)(2,1)S(1)} %get-tuple-element.183), channel_id=1, source_target_pairs={{0,1},{1,2},{2,3},{3,4},{4,5},{5,6},{6,7},{8,9},{9,10},{10,11},{11... | collective-permute-start | bytes 7688 | tf_op jit(solution)/shard_map/ppermute | solution.py:21
  46.7 5.0 collective-permute-start.3
  49.8 15.6 %copy-start.8 = (f32[128]{0:T(128)S(1)}, f32[128]{0:T(128)}, u32[]{:S(2)}) copy-start(f32[128]{0:T(128)} %get-tuple-element.203) | copy-start | bytes 1540
  49.8 15.6 %copy-start.10 = (f32[128]{0:T(128)S(1)}, f32[128]{0:T(128)}, u32[]{:S(2)}) copy-start(f32[128]{0:T(128)} %get-tuple-element.204) | copy-start | bytes 1540
  49.8 9.2 %collective-permute-start.21 = (bf16[8,1,8,128]{3,2,0,1:T(8,128)(2,1)}, bf16[8,1,8,128]{3,2,0,1:T(8,128)(2,1)S(1)}, u32[]{:S(2)}, u32[]{:S(2)}) collective-permute-start(bf16[8,1,8,128]{3,2,0,1:T(8,128)(2,1)} %get-tuple-element.168), channel_id=1, source_target_pairs={{8,0},{16,8},{24,16},{32,24},{40,32},{48,40},{56,48},{64,56},{72,6... | collective-permute-start | bytes 49160 | tf_op jit(solution)/shard_map/ppermute | solution.py:24
  53.7 10.7 %collective-permute-start.6 = (bf16[8,10,1,128]{3,2,0,1:T(2,128)(2,1)S(1)}, bf16[8,10,1,128]{3,2,0,1:T(2,128)(2,1)S(1)}, u32[]{:S(2)}, u32[]{:S(2)}) collective-permute-start(bf16[8,10,1,128]{3,2,0,1:T(2,128)(2,1)S(1)} %get-tuple-element.143), channel_id=1, source_target_pairs={{0,1},{1,2},{2,3},{3,4},{4,5},{5,6},{6,7},{8,9},{9,10},{10,11},{11... | collective-permute-start | bytes 61448 | tf_op jit(solution)/shard_map/ppermute | solution.py:21
  57.7 6.7 %collective-permute-start.7 = (bf16[8,10,1,128]{3,2,0,1:T(2,128)(2,1)S(1)}, bf16[8,10,1,128]{3,2,0,1:T(2,128)(2,1)S(1)}, u32[]{:S(2)}, u32[]{:S(2)}) collective-permute-start(bf16[8,10,1,128]{3,2,0,1:T(2,128)(2,1)S(1)} %get-tuple-element.144), channel_id=1, source_target_pairs={{1,0},{2,1},{3,2},{4,3},{5,4},{6,5},{7,6},{9,8},{10,9},{11,10},{12... | collective-permute-start | bytes 61448 | tf_op jit(solution)/shard_map/ppermute | solution.py:24
  59.0 8.6 %collective-permute-start.22 = (bf16[8,10,1,128]{3,2,0,1:T(2,128)(2,1)S(1)}, bf16[8,10,1,128]{3,2,0,1:T(2,128)(2,1)S(1)}, u32[]{:S(2)}, u32[]{:S(2)}) collective-permute-start(bf16[8,10,1,128]{3,2,0,1:T(2,128)(2,1)S(1)} %get-tuple-element.151), channel_id=1, source_target_pairs={{0,1},{1,2},{2,3},{3,4},{4,5},{5,6},{6,7},{8,9},{9,10},{10,11},{11... | collective-permute-start | bytes 61448 | tf_op jit(solution)/shard_map/ppermute | solution.py:21
  63.0 5.5 collective-permute-start.23
  65.4 3.5 copy-start.6
  70.1 15.6 %collective-permute-start.8 = (bf16[8,1,8,128]{3,2,0,1:T(8,128)(2,1)S(1)}, bf16[8,1,8,128]{3,2,0,1:T(8,128)(2,1)S(1)}, u32[]{:S(2)}, u32[]{:S(2)}) collective-permute-start(bf16[8,1,8,128]{3,2,0,1:T(8,128)(2,1)S(1)} %get-tuple-element.157), channel_id=1, source_target_pairs={{0,8},{8,16},{16,24},{24,32},{32,40},{40,48},{48,56},{56,64},{64,7... | collective-permute-start | bytes 49160 | tf_op jit(solution)/shard_map/ppermute | solution.py:21
  77.0 8.7 %collective-permute-start.9 = (bf16[8,1,8,128]{3,2,0,1:T(8,128)(2,1)S(1)}, bf16[8,1,8,128]{3,2,0,1:T(8,128)(2,1)S(1)}, u32[]{:S(2)}, u32[]{:S(2)}) collective-permute-start(bf16[8,1,8,128]{3,2,0,1:T(8,128)(2,1)S(1)} %get-tuple-element.158), channel_id=1, source_target_pairs={{8,0},{16,8},{24,16},{32,24},{40,32},{48,40},{56,48},{64,56},{72,6... | collective-permute-start | bytes 49160 | tf_op jit(solution)/shard_map/ppermute | solution.py:24
  79.1 11.3 %collective-permute-start.24 = (bf16[8,1,8,128]{3,2,0,1:T(8,128)(2,1)S(1)}, bf16[8,1,8,128]{3,2,0,1:T(8,128)(2,1)S(1)}, u32[]{:S(2)}, u32[]{:S(2)}) collective-permute-start(bf16[8,1,8,128]{3,2,0,1:T(8,128)(2,1)S(1)} %get-tuple-element.165), channel_id=1, source_target_pairs={{0,8},{8,16},{16,24},{24,32},{32,40},{40,48},{48,56},{56,64},{64,7... | collective-permute-start | bytes 49160 | tf_op jit(solution)/shard_map/ppermute | solution.py:21
  83.6 7.8 %collective-permute-start.25 = (bf16[8,1,8,128]{3,2,0,1:T(8,128)(2,1)S(1)}, bf16[8,1,8,128]{3,2,0,1:T(8,128)(2,1)S(1)}, u32[]{:S(2)}, u32[]{:S(2)}) collective-permute-start(bf16[8,1,8,128]{3,2,0,1:T(8,128)(2,1)S(1)} %get-tuple-element.166), channel_id=1, source_target_pairs={{8,0},{16,8},{24,16},{32,24},{40,32},{48,40},{56,48},{64,56},{72,6... | collective-permute-start | bytes 49160 | tf_op jit(solution)/shard_map/ppermute | solution.py:24
  85.8 12.5 %collective-permute-start.10 = (bf16[8,10,1,128]{3,2,0,1:T(2,128)(2,1)S(1)}, bf16[8,10,1,128]{3,2,0,1:T(2,128)(2,1)S(1)}, u32[]{:S(2)}, u32[]{:S(2)}) collective-permute-start(bf16[8,10,1,128]{3,2,0,1:T(2,128)(2,1)S(1)} %get-tuple-element.141), channel_id=1, source_target_pairs={{0,1},{1,2},{2,3},{3,4},{4,5},{5,6},{6,7},{8,9},{9,10},{10,11},{11... | collective-permute-start | bytes 61448 | tf_op jit(solution)/shard_map/ppermute | solution.py:21
  89.0 9.3 %collective-permute-start.11 = (bf16[8,10,1,128]{3,2,0,1:T(2,128)(2,1)S(1)}, bf16[8,10,1,128]{3,2,0,1:T(2,128)(2,1)S(1)}, u32[]{:S(2)}, u32[]{:S(2)}) collective-permute-start(bf16[8,10,1,128]{3,2,0,1:T(2,128)(2,1)S(1)} %get-tuple-element.142), channel_id=1, source_target_pairs={{1,0},{2,1},{3,2},{4,3},{5,4},{6,5},{7,6},{9,8},{10,9},{11,10},{12... | collective-permute-start | bytes 61448 | tf_op jit(solution)/shard_map/ppermute | solution.py:24
  91.5 8.4 %collective-permute-start.26 = (bf16[8,10,1,128]{3,2,0,1:T(2,128)(2,1)S(1)}, bf16[8,10,1,128]{3,2,0,1:T(2,128)(2,1)S(1)}, u32[]{:S(2)}, u32[]{:S(2)}) collective-permute-start(bf16[8,10,1,128]{3,2,0,1:T(2,128)(2,1)S(1)} %get-tuple-element.149), channel_id=1, source_target_pairs={{0,1},{1,2},{2,3},{3,4},{4,5},{5,6},{6,7},{8,9},{9,10},{10,11},{11... | collective-permute-start | bytes 61448 | tf_op jit(solution)/shard_map/ppermute | solution.py:21
  96.8 7.1 %collective-permute-start.27 = (bf16[8,10,1,128]{3,2,0,1:T(2,128)(2,1)S(1)}, bf16[8,10,1,128]{3,2,0,1:T(2,128)(2,1)S(1)}, u32[]{:S(2)}, u32[]{:S(2)}) collective-permute-start(bf16[8,10,1,128]{3,2,0,1:T(2,128)(2,1)S(1)} %get-tuple-element.150), channel_id=1, source_target_pairs={{1,0},{2,1},{3,2},{4,3},{5,4},{6,5},{7,6},{9,8},{10,9},{11,10},{12... | collective-permute-start | bytes 61448 | tf_op jit(solution)/shard_map/ppermute | solution.py:24
  105.6 16.5 %collective-permute-start.12 = (bf16[8,1,8,128]{3,2,0,1:T(8,128)(2,1)S(1)}, bf16[8,1,8,128]{3,2,0,1:T(8,128)(2,1)S(1)}, u32[]{:S(2)}, u32[]{:S(2)}) collective-permute-start(bf16[8,1,8,128]{3,2,0,1:T(8,128)(2,1)S(1)} %get-tuple-element.155), channel_id=1, source_target_pairs={{0,8},{8,16},{16,24},{24,32},{32,40},{40,48},{48,56},{56,64},{64,7... | collective-permute-start | bytes 49160 | tf_op jit(solution)/shard_map/ppermute | solution.py:21
  113.4 8.7 %collective-permute-start.13 = (bf16[8,1,8,128]{3,2,0,1:T(8,128)(2,1)S(1)}, bf16[8,1,8,128]{3,2,0,1:T(8,128)(2,1)S(1)}, u32[]{:S(2)}, u32[]{:S(2)}) collective-permute-start(bf16[8,1,8,128]{3,2,0,1:T(8,128)(2,1)S(1)} %get-tuple-element.156), channel_id=1, source_target_pairs={{8,0},{16,8},{24,16},{32,24},{40,32},{48,40},{56,48},{64,56},{72,6... | collective-permute-start | bytes 49160 | tf_op jit(solution)/shard_map/ppermute | solution.py:24
  115.5 11.6 %collective-permute-start.28 = (bf16[8,1,8,128]{3,2,0,1:T(8,128)(2,1)S(1)}, bf16[8,1,8,128]{3,2,0,1:T(8,128)(2,1)S(1)}, u32[]{:S(2)}, u32[]{:S(2)}) collective-permute-start(bf16[8,1,8,128]{3,2,0,1:T(8,128)(2,1)S(1)} %get-tuple-element.163), channel_id=1, source_target_pairs={{0,8},{8,16},{16,24},{24,32},{32,40},{40,48},{48,56},{56,64},{64,7... | collective-permute-start | bytes 49160 | tf_op jit(solution)/shard_map/ppermute | solution.py:21
  120.0 8.4 %collective-permute-start.29 = (bf16[8,1,8,128]{3,2,0,1:T(8,128)(2,1)S(1)}, bf16[8,1,8,128]{3,2,0,1:T(8,128)(2,1)S(1)}, u32[]{:S(2)}, u32[]{:S(2)}) collective-permute-start(bf16[8,1,8,128]{3,2,0,1:T(8,128)(2,1)S(1)} %get-tuple-element.164), channel_id=1, source_target_pairs={{8,0},{16,8},{24,16},{32,24},{40,32},{48,40},{56,48},{64,56},{72,6... | collective-permute-start | bytes 49160 | tf_op jit(solution)/shard_map/ppermute | solution.py:24
  122.2 12.1 %collective-permute-start.14 = (bf16[8,10,1,128]{3,2,0,1:T(2,128)(2,1)S(1)}, bf16[8,10,1,128]{3,2,0,1:T(2,128)(2,1)S(1)}, u32[]{:S(2)}, u32[]{:S(2)}) collective-permute-start(bf16[8,10,1,128]{3,2,0,1:T(2,128)(2,1)S(1)} %get-tuple-element.139), channel_id=1, source_target_pairs={{0,1},{1,2},{2,3},{3,4},{4,5},{5,6},{6,7},{8,9},{9,10},{10,11},{11... | collective-permute-start | bytes 61448 | tf_op jit(solution)/shard_map/ppermute | solution.py:21
  125.8 8.5 %collective-permute-start.15 = (bf16[8,10,1,128]{3,2,0,1:T(2,128)(2,1)S(1)}, bf16[8,10,1,128]{3,2,0,1:T(2,128)(2,1)S(1)}, u32[]{:S(2)}, u32[]{:S(2)}) collective-permute-start(bf16[8,10,1,128]{3,2,0,1:T(2,128)(2,1)S(1)} %get-tuple-element.140), channel_id=1, source_target_pairs={{1,0},{2,1},{3,2},{4,3},{5,4},{6,5},{7,6},{9,8},{10,9},{11,10},{12... | collective-permute-start | bytes 61448 | tf_op jit(solution)/shard_map/ppermute | solution.py:24
  128.5 7.4 %collective-permute-start.30 = (bf16[8,10,1,128]{3,2,0,1:T(2,128)(2,1)S(1)}, bf16[8,10,1,128]{3,2,0,1:T(2,128)(2,1)S(1)}, u32[]{:S(2)}, u32[]{:S(2)}) collective-permute-start(bf16[8,10,1,128]{3,2,0,1:T(2,128)(2,1)S(1)} %get-tuple-element.147), channel_id=1, source_target_pairs={{0,1},{1,2},{2,3},{3,4},{4,5},{5,6},{6,7},{8,9},{9,10},{10,11},{11... | collective-permute-start | bytes 61448 | tf_op jit(solution)/shard_map/ppermute | solution.py:21
  133.0 7.1 %collective-permute-start.31 = (bf16[8,10,1,128]{3,2,0,1:T(2,128)(2,1)S(1)}, bf16[8,10,1,128]{3,2,0,1:T(2,128)(2,1)S(1)}, u32[]{:S(2)}, u32[]{:S(2)}) collective-permute-start(bf16[8,10,1,128]{3,2,0,1:T(2,128)(2,1)S(1)} %get-tuple-element.148), channel_id=1, source_target_pairs={{1,0},{2,1},{3,2},{4,3},{5,4},{6,5},{7,6},{9,8},{10,9},{11,10},{12... | collective-permute-start | bytes 61448 | tf_op jit(solution)/shard_map/ppermute | solution.py:24
  141.7 17.0 %collective-permute-start.16 = (bf16[8,1,8,128]{3,2,0,1:T(8,128)(2,1)S(1)}, bf16[8,1,8,128]{3,2,0,1:T(8,128)(2,1)S(1)}, u32[]{:S(2)}, u32[]{:S(2)}) collective-permute-start(bf16[8,1,8,128]{3,2,0,1:T(8,128)(2,1)S(1)} %get-tuple-element.153), channel_id=1, source_target_pairs={{0,8},{8,16},{16,24},{24,32},{32,40},{40,48},{48,56},{56,64},{64,7... | collective-permute-start | bytes 49160 | tf_op jit(solution)/shard_map/ppermute | solution.py:21
  150.1 8.6 %collective-permute-start.17 = (bf16[8,1,8,128]{3,2,0,1:T(8,128)(2,1)S(1)}, bf16[8,1,8,128]{3,2,0,1:T(8,128)(2,1)S(1)}, u32[]{:S(2)}, u32[]{:S(2)}) collective-permute-start(bf16[8,1,8,128]{3,2,0,1:T(8,128)(2,1)S(1)} %get-tuple-element.154), channel_id=1, source_target_pairs={{8,0},{16,8},{24,16},{32,24},{40,32},{48,40},{56,48},{64,56},{72,6... | collective-permute-start | bytes 49160 | tf_op jit(solution)/shard_map/ppermute | solution.py:24
  152.2 11.5 %collective-permute-start.32 = (bf16[8,1,8,128]{3,2,0,1:T(8,128)(2,1)S(1)}, bf16[8,1,8,128]{3,2,0,1:T(8,128)(2,1)S(1)}, u32[]{:S(2)}, u32[]{:S(2)}) collective-permute-start(bf16[8,1,8,128]{3,2,0,1:T(8,128)(2,1)S(1)} %get-tuple-element.161), channel_id=1, source_target_pairs={{0,8},{8,16},{16,24},{24,32},{32,40},{40,48},{48,56},{56,64},{64,7... | collective-permute-start | bytes 49160 | tf_op jit(solution)/shard_map/ppermute | solution.py:21
  156.8 8.4 %collective-permute-start.33 = (bf16[8,1,8,128]{3,2,0,1:T(8,128)(2,1)S(1)}, bf16[8,1,8,128]{3,2,0,1:T(8,128)(2,1)S(1)}, u32[]{:S(2)}, u32[]{:S(2)}) collective-permute-start(bf16[8,1,8,128]{3,2,0,1:T(8,128)(2,1)S(1)} %get-tuple-element.162), channel_id=1, source_target_pairs={{8,0},{16,8},{24,16},{32,24},{40,32},{48,40},{56,48},{64,56},{72,6... | collective-permute-start | bytes 49160 | tf_op jit(solution)/shard_map/ppermute | solution.py:24
  158.8 11.4 %collective-permute-start.18 = (bf16[8,10,1,128]{3,2,0,1:T(2,128)(2,1)S(1)}, bf16[8,10,1,128]{3,2,0,1:T(2,128)(2,1)S(1)}, u32[]{:S(2)}, u32[]{:S(2)}) collective-permute-start(bf16[8,10,1,128]{3,2,0,1:T(2,128)(2,1)S(1)} %get-tuple-element.137), channel_id=1, source_target_pairs={{0,1},{1,2},{2,3},{3,4},{4,5},{5,6},{6,7},{8,9},{9,10},{10,11},{11... | collective-permute-start | bytes 61448 | tf_op jit(solution)/shard_map/ppermute | solution.py:21
  162.4 7.7 %collective-permute-start.19 = (bf16[8,10,1,128]{3,2,0,1:T(2,128)(2,1)S(1)}, bf16[8,10,1,128]{3,2,0,1:T(2,128)(2,1)S(1)}, u32[]{:S(2)}, u32[]{:S(2)}) collective-permute-start(bf16[8,10,1,128]{3,2,0,1:T(2,128)(2,1)S(1)} %get-tuple-element.138), channel_id=1, source_target_pairs={{1,0},{2,1},{3,2},{4,3},{5,4},{6,5},{7,6},{9,8},{10,9},{11,10},{12... | collective-permute-start | bytes 61448 | tf_op jit(solution)/shard_map/ppermute | solution.py:24
  165.2 16.3 %collective-permute-start.34 = (bf16[8,10,1,128]{3,2,0,1:T(2,128)(2,1)S(1)}, bf16[8,10,1,128]{3,2,0,1:T(2,128)(2,1)S(1)}, u32[]{:S(2)}, u32[]{:S(2)}) collective-permute-start(bf16[8,10,1,128]{3,2,0,1:T(2,128)(2,1)S(1)} %get-tuple-element.145), channel_id=1, source_target_pairs={{0,1},{1,2},{2,3},{3,4},{4,5},{5,6},{6,7},{8,9},{9,10},{10,11},{11... | collective-permute-start | bytes 61448 | tf_op jit(solution)/shard_map/ppermute | solution.py:21
  168.9 12.7 %collective-permute-start.35 = (bf16[8,10,1,128]{3,2,0,1:T(2,128)(2,1)S(1)}, bf16[8,10,1,128]{3,2,0,1:T(2,128)(2,1)S(1)}, u32[]{:S(2)}, u32[]{:S(2)}) collective-permute-start(bf16[8,10,1,128]{3,2,0,1:T(2,128)(2,1)S(1)} %get-tuple-element.146), channel_id=1, source_target_pairs={{1,0},{2,1},{3,2},{4,3},{5,4},{6,5},{7,6},{9,8},{10,9},{11,10},{12... | collective-permute-start | bytes 61448 | tf_op jit(solution)/shard_map/ppermute | solution.py:24
  170.5 11.4 %copy-start.9 = (f32[128]{0:T(128)S(1)}, f32[128]{0:T(128)}, u32[]{:S(2)}) copy-start(f32[128]{0:T(128)} %get-tuple-element.203) | copy-start | bytes 1540
  170.5 11.4 %copy-start.11 = (f32[128]{0:T(128)S(1)}, f32[128]{0:T(128)}, u32[]{:S(2)}) copy-start(f32[128]{0:T(128)} %get-tuple-element.204) | copy-start | bytes 1540
  172.4 17.5 %all-to-all-start = ((bf16[32,8,8,128]{3,2,0,1:T(8,128)(2,1)}), bf16[32,8,8,128]{3,2,0,1:T(8,128)(2,1)S(1)}, u32[]{:S(2)}, u32[]{:S(2)}) async-start(bf16[32,8,8,128]{3,2,0,1:T(8,128)(2,1)} %pad_maximum_fusion.1), calls=%async_computation | async-start | bytes 1048576 | tf_op jit(solution)/shard_map/all_to_all | solution.py:167
  189.9 11.8 %all-to-all-start.1 = ((bf16[32,8,8,128]{3,2,0,1:T(8,128)(2,1)}), bf16[32,8,8,128]{3,2,0,1:T(8,128)(2,1)S(1)}, u32[]{:S(2)}, u32[]{:S(2)}) async-start(bf16[32,8,8,128]{3,2,0,1:T(8,128)(2,1)} %pad_maximum_fusion.2), calls=%async_computation.1 | async-start | bytes 1048576 | tf_op jit(solution)/shard_map/all_to_all | solution.py:167
  193.4 275.4 %all-reduce.23.cloned.1.call-start = ((), (), s32[]{:S(2)}) async-start(), calls=%async_computation.2 | async-start | bytes 983040 | tf_op jit(solution)/shard_map/psum | solution.py:176
  201.7 2.2 copy-start.2
  201.8 2.9 copy-start.7
  202.1 3.4 copy-start.12
  608.1 10.3 %copy-start.1 = (f32[16,256]{1,0:T(8,128)S(1)}, f32[16,256]{1,0:T(8,128)}, u32[]{:S(2)}) copy-start(f32[16,256]{1,0:T(8,128)} %param.14) | copy-start | bytes 49156
Sparse Core Ops, SparseCore 0:
  205.6 263.1 all-reduce.22

commit v2 on v1

v2 whole, which is shorter than its diff:
```python
import jax
import jax.numpy as jnp
from jax import lax
from jax.experimental import pallas as pl
from jax.experimental.pallas import tpu as pltpu
from jax.sharding import PartitionSpec as P

MG = 8
STEPS = 4
GROUPS = 2
MEMB = MG * GROUPS

DT_PRESSURE = 0.12
DT_SATURATION = 0.06
DT_ADVECT = 0.15

MESH = pl.DeviceIdType.MESH
VMEM = pltpu.VMEM
F32 = jnp.float32
BF16 = jnp.bfloat16


def harmonic(left, right):
    return 2.0 * left * right / (left + right)


def remote(src, dst, send_sem, recv_sem, device):
    return pltpu.make_async_remote_copy(
        src_ref=src, dst_ref=dst, send_sem=send_sem, recv_sem=recv_sem, device_id=device, device_id_type=MESH
    )


def flux_kernel(
    table_ref, state_ref, rock_ref, inflow_ref, out_ref, snaps_ref,
    perm_send, perm_recv, x_send, x_recv, y_send, y_recv, y_wide, weights, turned, packed,
    ps_sem, pr_sem, hs_sem, hr_sem, ss_sem, sr_sem, own_sem,
):
    gx_count, sec_count = lax.axis_size("gx"), lax.axis_size("sec")
    gx, sec = lax.axis_index("gx"), lax.axis_index("sec")
    beside = (
        {"gx": lax.rem(gx + gx_count - 1, gx_count)},
        {"gx": lax.rem(gx + 1, gx_count)},
        {"sec": lax.rem(sec + sec_count - 1, sec_count)},
        {"sec": lax.rem(sec + 1, sec_count)},
    )
    barrier = pltpu.get_barrier_semaphore()
    for device in beside[:2]:
        pl.semaphore_signal(barrier, inc=1, device_id=device, device_id_type=MESH)
    for ahead in range(1, sec_count):
        pl.semaphore_signal(
            barrier, inc=1, device_id={"sec": lax.rem(sec + ahead, sec_count)}, device_id_type=MESH
        )

    lane = lax.broadcasted_iota(jnp.int32, (8, 128), 1)
    row = lax.broadcasted_iota(jnp.int32, (8, 128), 0)

    perm = [[], [], []]
    for x in range(8):
        kind = rock_ref[x]
        for d in range(3):
            value = jnp.full((8, 128), table_ref[d, 0], F32)
            for r in range(1, 16):
                value = jnp.where(kind == r, table_ref[d, r], value)
            perm[d].append(value)
    perm_send[0] = perm[0][0]
    perm_send[1] = perm[0][7]
    for x in range(8):
        perm_send[2, pl.ds(x, 1), :] = perm[1][x][0:1]
        perm_send[3, pl.ds(x, 1), :] = perm[1][x][7:8]

    def halo_copies(step):
        pairs = []
        for d in range(4):
            send = (x_send if d < 2 else y_send).at[step, d % 2]
            recv = (x_recv if d < 2 else y_recv).at[step, 1 - d % 2]
            pairs.append(remote(send, recv, hs_sem.at[step, d], hr_sem.at[step, d ^ 1], beside[d]))
        return pairs

    def stage_y(step):
        y_send[step, 0] = out_ref[pl.ds(0, 128, stride=8), :].astype(BF16)
        y_send[step, 1] = out_ref[pl.ds(7, 128, stride=8), :].astype(BF16)

    def first(m, carry):
        x_send[0, 0, m] = state_ref[m, 0].astype(BF16)
        x_send[0, 1, m] = state_ref[m, 7].astype(BF16)
        for x in range(8):
            out_ref[pl.ds(pl.multiple_of(m * 64 + x * 8, 8), 8), :] = state_ref[m, x]
        return carry

    lax.fori_loop(0, MEMB, first, 0)
    stage_y(0)
    pl.semaphore_wait(barrier, 1 + sec_count)
    perm_copies = [
        remote(perm_send.at[d], perm_recv.at[d ^ 1], ps_sem.at[d], pr_sem.at[d ^ 1], beside[d]) for d in range(4)
    ]
    for copy in perm_copies:
        copy.start()
    flying = halo_copies(0)
    for copy in flying:
        copy.start()

    z_up = jnp.where((lane & 63) == 63, 0.0, 1.0)
    z_down = jnp.where((lane & 63) == 0, 0.0, 1.0)
    for x in range(8):
        weights[4, x] = z_up * harmonic(perm[2][x], pltpu.roll(perm[2][x], 127, 1))
        weights[5, x] = z_down * harmonic(perm[2][x], pltpu.roll(perm[2][x], 1, 1))
    for copy in perm_copies:
        copy.wait()
    not_first_x = jnp.where(gx == 0, 0.0, 1.0)
    not_last_x = jnp.where(gx == gx_count - 1, 0.0, 1.0)
    not_first_y = jnp.where(sec == 0, 0.0, 1.0)
    not_last_y = jnp.where(sec == sec_count - 1, 0.0, 1.0)
    for x in range(8):
        above = perm[0][x + 1] if x < 7 else perm_recv[1] * not_last_x
        below = perm[0][x - 1] if x > 0 else perm_recv[0] * not_first_x
        weights[0, x] = harmonic(perm[0][x], above)
        weights[1, x] = harmonic(below, perm[0][x])
        right = jnp.broadcast_to(perm_recv[3, pl.ds(x, 1), :] * not_last_y, (8, 128))
        left = jnp.broadcast_to(perm_recv[2, pl.ds(x, 1), :] * not_first_y, (8, 128))
        weights[2, x] = harmonic(perm[1][x], jnp.where(row == 7, right, pltpu.roll(perm[1][x], 7, 0)))
        weights[3, x] = harmonic(jnp.where(row == 0, left, pltpu.roll(perm[1][x], 1, 0)), perm[1][x])

    step_sizes = jnp.where(lane < 64, DT_PRESSURE, DT_SATURATION)
    advect = jnp.where(lane < 64, 0.0, DT_ADVECT)
    sent = []
    for step in range(STEPS):
        for copy in flying:
            copy.wait()
        y_wide[0] = y_recv[step, 0].astype(F32)
        y_wide[1] = y_recv[step, 1].astype(F32)

        def member(m, carry):
            base = pl.multiple_of(m * 64, 64)
            old = [out_ref[pl.ds(base + x * 8, 8), :] for x in range(8)]
            old_below = x_recv[step, 0, m].astype(F32)
            old_above = x_recv[step, 1, m].astype(F32)
            for x in range(8):
                here = old[x]
                left = jnp.broadcast_to(y_wide[0, pl.ds(m * 8 + x, 1), :], (8, 128))
                right = jnp.broadcast_to(y_wide[1, pl.ds(m * 8 + x, 1), :], (8, 128))
                besides = (
                    old[x + 1] if x < 7 else old_above,
                    old[x - 1] if x > 0 else old_below,
                    jnp.where(row == 7, right, pltpu.roll(here, 7, 0)),
                    jnp.where(row == 0, left, pltpu.roll(here, 1, 0)),
                    pltpu.roll(here, 127, 1),
                    pltpu.roll(here, 1, 1),
                )
                spread = carried = None
                for d in range(6):
                    flow = weights[d, x] * (besides[d] - here)
                    pushed = pltpu.roll(flow, 64, 1)
                    moved = pushed * jnp.where(pushed > 0.0, besides[d], here)
                    spread = flow if spread is None else spread + flow
                    carried = moved if carried is None else carried + moved
                fresh = here + step_sizes * spread + advect * carried + DT_PRESSURE * inflow_ref[m, x]
                out_ref[pl.ds(base + x * 8, 8), :] = fresh
                turned[x, pl.ds(m, 8, stride=MEMB), :] = fresh
                if step + 1 < STEPS and x in (0, 7):
                    x_send[step + 1, x // 7, m] = fresh.astype(BF16)
            return carry

        lax.fori_loop(0, MEMB, member, 0)
        if step + 1 < STEPS:
            stage_y(step + 1)
            flying = halo_copies(step + 1)
            for copy in flying:
                copy.start()
        for x in range(8):
            packed[step, x] = turned[x].reshape(8, MEMB, 128).astype(BF16)
        mine = pltpu.make_async_copy(
            packed.at[step, sec], snaps_ref.at[step, pl.ds(sec * 8, 8)], own_sem.at[step]
        )
        mine.start()
        sent.append(mine)
        for ahead in range(1, sec_count):
            target = lax.rem(sec + ahead, sec_count)
            copy = remote(
                packed.at[step, target], snaps_ref.at[step, pl.ds(sec * 8, 8)],
                ss_sem.at[step, ahead], sr_sem.at[step, ahead], {"sec": target},
            )
            copy.start()
            sent.append(copy)
    for copy in sent:
        copy.wait()


def flux(table, state, rock, inflow):
    sec_count = lax.axis_size("sec")
    dma = pltpu.SemaphoreType.DMA
    return pl.pallas_call(
        flux_kernel,
        out_shape=(
            jax.ShapeDtypeStruct((MEMB * 64, 128), F32),
            jax.ShapeDtypeStruct((STEPS, 8 * sec_count, MEMB, 128), BF16),
        ),
        in_specs=[
            pl.BlockSpec(memory_space=pltpu.SMEM),
            pl.BlockSpec(memory_space=VMEM),
            pl.BlockSpec(memory_space=VMEM),
            pl.BlockSpec(memory_space=VMEM),
        ],
        out_specs=(pl.BlockSpec(memory_space=VMEM), pl.BlockSpec(memory_space=VMEM)),
        scratch_shapes=[
            VMEM((4, 8, 128), F32),
            VMEM((4, 8, 128), F32),
            VMEM((STEPS, 2, MEMB, 8, 128), BF16),
            VMEM((STEPS, 2, MEMB, 8, 128), BF16),
            VMEM((STEPS, 2, MEMB * 8, 128), BF16),
            VMEM((STEPS, 2, MEMB * 8, 128), BF16),
            VMEM((2, MEMB * 8, 128), F32),
            VMEM((6, 8, 8, 128), F32),
            VMEM((8, 8 * MEMB, 128), F32),
            VMEM((STEPS, 8, 8, MEMB, 128), BF16),
            dma((4,)), dma((4,)), dma((STEPS, 4)), dma((STEPS, 4)),
            dma((STEPS, sec_count)), dma((STEPS, sec_count)), dma((STEPS,)),
        ],
        compiler_params=pltpu.CompilerParams(
            collective_id=0, has_side_effects=True, vmem_limit_bytes=32 * 1024 * 1024
        ),
        name="flux",
    )(table, state, rock, inflow)


PLANE = 32
COLUMN = 8


def reduce_kernel(x_ref, out_ref, slots, partial, column, send1, recv1, send2, recv2, send3, recv3):
    gx, sec = lax.axis_index("gx"), lax.axis_index("sec")
    z_hi, z_lo = lax.rem(gx // 2, 4), sec // 4
    me = (gx // 8) * 8 + lax.rem(gx, 2) * 4 + lax.rem(sec, 4)
    me_z = z_hi * 2 + z_lo

    def in_plane(p):
        return {"gx": (p // 8) * 8 + z_hi * 2 + lax.rem(p // 4, 2), "sec": z_lo * 4 + lax.rem(p, 4)}

    def in_column(q):
        return {"gx": (gx // 8) * 8 + (q // 2) * 2 + lax.rem(gx, 2), "sec": lax.rem(q, 2) * 4 + lax.rem(sec, 4)}

    barrier = pltpu.get_barrier_semaphore()
    for k in range(1, PLANE):
        pl.semaphore_signal(barrier, inc=1, device_id=in_plane(lax.rem(me + k, PLANE)), device_id_type=MESH)
    for k in range(1, COLUMN):
        pl.semaphore_signal(barrier, inc=1, device_id=in_column(lax.rem(me_z + k, COLUMN)), device_id_type=MESH)
    slots[me] = x_ref[me]
    pl.semaphore_wait(barrier, PLANE + COLUMN - 2)

    def scatter(k):
        p = lax.rem(me + k, PLANE)
        return remote(x_ref.at[p], slots.at[me], send1.at[k], recv1.at[k], in_plane(p))

    for k in range(1, PLANE):
        scatter(k).start()
    for k in range(1, PLANE):
        scatter(k).wait()
    total = slots[0]
    for k in range(1, PLANE):
        total = total + slots[k]
    partial[...] = total
    column[me_z] = total

    def across(k):
        q = lax.rem(me_z + k, COLUMN)
        return remote(partial, column.at[me_z], send2.at[k], recv2.at[k], in_column(q))

    for k in range(1, COLUMN):
        across(k).start()
    for k in range(1, COLUMN):
        across(k).wait()
    total = column[0]
    for k in range(1, COLUMN):
        total = total + column[k]
    out_ref[me] = total

    def gather(k):
        p = lax.rem(me + k, PLANE)
        return remote(out_ref.at[me], out_ref.at[me], send3.at[k], recv3.at[k], in_plane(p))

    for k in range(1, PLANE):
        gather(k).start()
    for k in range(1, PLANE):
        gather(k).wait()


def all_sum(x):
    rows = x.shape[0] // PLANE
    dma = pltpu.SemaphoreType.DMA
    out = pl.pallas_call(
        reduce_kernel,
        out_shape=jax.ShapeDtypeStruct((PLANE, rows, 128), F32),
        in_specs=[pl.BlockSpec(memory_space=VMEM)],
        out_specs=pl.BlockSpec(memory_space=VMEM),
        scratch_shapes=[
            VMEM((PLANE, rows, 128), F32), VMEM((rows, 128), F32), VMEM((COLUMN, rows, 128), F32),
            dma((PLANE,)), dma((PLANE,)), dma((COLUMN,)), dma((COLUMN,)), dma((PLANE,)), dma((PLANE,)),
        ],
        compiler_params=pltpu.CompilerParams(
            collective_id=1, has_side_effects=True, vmem_limit_bytes=16 * 1024 * 1024
        ),
        name="all_sum",
    )(x.reshape(PLANE, rows, 128))
    return out.reshape(x.shape)


HIGH = lax.Precision.HIGHEST


def hdot(a, b):
    return jnp.dot(a, b, precision=HIGH)


def batch_update(coeffs, gram_of, sigma):
    rounded = coeffs.astype(jnp.bfloat16).astype(jnp.float32)
    gram = gram_of(coeffs, rounded)
    square = jnp.diag(sigma * sigma)
    total = square + hdot(coeffs.T, coeffs)
    inner = hdot(total, total) + hdot(coeffs.T, hdot(gram, coeffs))
    factor = jnp.linalg.cholesky(inner)
    eye = jnp.eye(sigma.shape[0], dtype=jnp.float32)
    back = lax.linalg.triangular_solve(factor, eye, left_side=True, lower=True).T
    top = sigma[:, None] * hdot(total, back)
    bottom = hdot(hdot(coeffs, total) + hdot(gram, coeffs), back)
    sigma_next = jnp.sqrt(jnp.sum(top * top, axis=0) + jnp.sum(bottom * bottom, axis=0))
    on_basis = hdot(square + hdot((coeffs - rounded).T, coeffs), back)
    on_snaps = hdot(coeffs, back)
    return on_basis, on_snaps, sigma_next


def small_algebra(uu, su, ss, sigma):
    half = su.shape[0] // 2
    s00, s10, s11 = ss[:half, :half], ss[half:, :half], ss[half:, half:]

    def gram_first(c, r):
        cr = hdot(c, r.T)
        return s00 - cr - cr.T + hdot(r, hdot(uu, r.T))

    wu, ws, sigma1 = batch_update(su[:half], gram_first, sigma)
    coeffs1 = hdot(su[half:], wu) + hdot(s10, ws)

    def gram_second(c, r):
        cr = hdot(c, r.T)
        yu, ys = hdot(wu, r.T), hdot(ws, r.T)
        mixed = hdot(ys.T, hdot(su[:half], yu))
        own = hdot(yu.T, hdot(uu, yu)) + mixed + mixed.T + hdot(ys.T, hdot(s00, ys))
        return s11 - cr - cr.T + own

    wu1, ws1, sigma2 = batch_update(coeffs1, gram_second, sigma1)
    return hdot(wu, wu1), hdot(ws, wu1), ws1, sigma2


def body(state_init, rock_type, perm_table, well_cells, well_rate, basis_in, singular):
    members, across, along, width = state_init.shape
    layers = width // 2
    sec_count = lax.axis_size("sec")
    rock = rock_type.reshape(across, along, layers)
    rock = jnp.concatenate([rock, rock], -1)
    x_start = lax.axis_index("gx") * across
    y_start = lax.axis_index("sec") * along
    total_y = along * sec_count
    x_pos = lax.broadcasted_iota(jnp.int32, (across, along, layers), 0)
    y_pos = lax.broadcasted_iota(jnp.int32, (across, along, layers), 1)
    z_pos = lax.broadcasted_iota(jnp.int32, (across, along, layers), 2)
    cell_ids = ((x_start + x_pos) * total_y + y_start + y_pos) * layers + z_pos
    hits = (well_cells[:, None] == cell_ids.reshape(1, -1)).astype(jnp.float32)
    source = jnp.dot(well_rate, hits, precision=HIGH).reshape(members, across, along, layers)
    source_full = jnp.concatenate([source, jnp.zeros_like(source)], -1)
    rows_total = basis_in.size // basis_in.shape[-1] * lax.axis_size("gx") * sec_count

    final, snaps = flux(perm_table, state_init, rock, source_full)
    state_out = final.reshape(state_init.shape)

    both = snaps.reshape(STEPS, -1, GROUPS, MG, width).transpose(2, 0, 3, 1, 4).reshape(GROUPS * STEPS * MG, -1)
    basis = basis_in.reshape(both.shape[1], basis_in.shape[-1])
    count = basis.shape[1]
    taken = both.shape[0]
    uu = lax.dot_general(basis, basis, (((0,), (0,)), ((), ())), preferred_element_type=jnp.float32)
    su = jnp.dot(both, basis, preferred_element_type=jnp.float32)
    ss = lax.dot_general(both, both, (((1,), (1,)), ((), ())), preferred_element_type=jnp.float32)
    local = jnp.concatenate(
        [
            su[:, :128],
            su[:, 128:],
            uu[:64, :128],
            uu[:64, 128:],
            uu[64:128, 128:],
            uu[128:192, 128:],
            jnp.concatenate([uu[64:128, 64:128], uu[192:, 192:]], 1),
            jnp.pad(ss, ((0, 0), (0, 64))),
        ],
        0,
    )
    whole = all_sum(local) / rows_total
    part = [whole[64 * i : 64 * (i + 1)] for i in range(8)]
    su = jnp.concatenate([part[0], part[1]], 1)
    row0 = jnp.concatenate([part[2], part[3]], 1)
    row1 = jnp.concatenate([row0[:, 64:128].T, part[6][:, :64], part[4]], 1)
    row2 = jnp.concatenate([row0[:, 128:192].T, row1[:, 128:192].T, part[5]], 1)
    row3 = jnp.concatenate([row0[:, 192:].T, row1[:, 192:].T, row2[:, 192:].T, part[6][:, 64:]], 1)
    uu = jnp.concatenate([row0, row1, row2, row3], 0)
    ss = part[7][:, :64]
    w0, w1, w2, sigma = small_algebra(uu, su, ss, singular)
    fresh = jnp.dot(basis, w0.astype(jnp.bfloat16), preferred_element_type=jnp.float32)
    fresh = fresh + lax.dot_general(
        both, jnp.concatenate([w1, w2], 0).astype(jnp.bfloat16), (((0,), (0,)), ((), ())), preferred_element_type=jnp.float32
    )
    return (state_out, fresh.astype(jnp.bfloat16).reshape(basis_in.shape), sigma)


def solution(mesh):
    return jax.shard_map(
        body,
        mesh=mesh,
        in_specs=(
            P(None, "gx", "sec", None),
            P("gx", "sec"),
            P(),
            P(),
            P(),
            P(("gx", "sec"), None, None, None),
            P(),
        ),
        out_specs=(P(None, "gx", "sec", None), P(("gx", "sec"), None, None, None), P()),
        check_vma=False,
    )
```

time: 635 us -> 245 us (0.39)
  waiting for transfers between devices: 289 us -> 0 us
  starting transfers between devices: 129 us -> 0 us
  Pallas kernels: 0 us -> 68.6 us
  other arithmetic: 131 us -> 111 us
  between operations: 18.6 us -> 4.13 us
    psum x1 -> x0, waiting for transfers between devices: 262 us -> none  [body(): whole = lax.psum(local, ('gx', 'sec')) / rows_total]
    ppermute x36 -> x0, starting transfers between devices: 116 us -> none  [the longest x18 87.2 us: with_halo(): lax.ppermute(lax.slice_in_dim(block, block.shape[dim] - width, None, axis...]
    pallas_call x0 -> x2, Pallas kernels: none -> 68.6 us  [the longest x1 41.4 us: flux(): pl.pallas_call(flux_kernel, out_shape=(jax.ShapeDtypeStruct((MEMB * 64, 1...]
    all_to_all x2 -> x0, waiting for transfers between devices: 13.5 us -> none  [body(): lax.all_to_all(stacked, 'sec', split_axis=1, concat_axis=2, tiled=True)]
    ppermute x36 -> x0, waiting for transfers between devices: 12.9 us -> none  [the longest x18 12.9 us: with_halo(): lax.ppermute(lax.slice_in_dim(block, 0, width, axis=dim), axis, backward)]
    all_to_all x2 -> x0, starting transfers between devices: 12.5 us -> none  [body(): lax.all_to_all(stacked, 'sec', split_axis=1, concat_axis=2, tiled=True)]
    convert_element_type x17 -> x0, other arithmetic: 12.1 us -> none  [the longest x6 7.16 us: body(): fields.astype(jnp.bfloat16)]
    slice x40 -> x3, local copies, waits for them, and re-layouts: 8.3 us -> 0.16 us  [the longest x1 0.08 us: body(): uu[64:128, 64:128]]
  transfers between devices with their start and end apart: 39 -> 0, of which waited for: 9 -> 0; matrix products, arithmetic and copies ran while one was open for 5% -> 0% of each run, Pallas kernels for 0% -> 0%
where the time goes in v2:
time: 245 us; the launch traced here: 240 us
  other arithmetic  111 us (45%)
  Pallas kernels  68.6 us (28%)
  matrix products  33.5 us (14%)
  local copies, waits for them, and re-layouts  22.7 us (9%)
  between operations  4.13 us (2%)
    another operation x13, other arithmetic, batch_update(): factor = jnp.linalg.cholesky(inner)  69 us
    pallas_call x1, Pallas kernels, flux(): pl.pallas_call(flux_kernel, out_shape=(jax.ShapeDtypeStruct((MEMB * 64, 1...  41.4 us
    another operation x5, other arithmetic, batch_update(): lax.linalg.triangular_solve(factor, eye, left_side=True, lower=True)  39.8 us
    pallas_call x1, Pallas kernels, all_sum(): pl.pallas_call(reduce_kernel, out_shape=jax.ShapeDtypeStruct((PLANE, rows...  27.2 us
    dot_general x36, matrix products, hdot(): return jnp.dot(a, b, precision=HIGH)  13.3 us
    another operation x15, local copies, waits for them, and re-layouts, batch_update(): lax.linalg.triangular_solve(factor, eye, left_side=True, lower=True)  11.4 us
    unnamed x22, local copies, waits for them, and re-layouts  8.66 us

profile of v2, /device:TPU:1, one launch (start us, length us, event | category | flops | bytes accessed | tf_op | source)
XLA Modules:
  0.0 240.3 jit_solution(156968632205842867)
XLA Ops:
  0.7 0.6 broadcast.138
  1.3 0.8 mul.68
  2.2 0.8 reshape.105
  3.1 2.0 convolution_bitcast_fusion.1
  5.2 4.8 %fusion.8 = f32[256,256]{1,0:T(8,128)S(1)} fusion(bf16[1,64,128,256]{3,2,1,0:T(8,128)(2,1)} %param.15), kind=kOutput, calls=%fused_computation.23 | convolution fusion | flops 1073741824 | bytes 4456448 | tf_op jit(solution)/shard_map/dot_general | solution.py:377
  10.3 41.4 %flux.1 = (f32[1024,128]{1,0:T(8,128)S(1)}, bf16[4,64,16,128]{3,2,1,0:T(8,128)(2,1)S(1)}) custom-call(f32[3,16]{1,0:T(4,128)S(1)} %copy-done.2, f32[16,8,8,128]{3,2,1,0:T(8,128)S(1)} %copy-done.1, s32[8,8,128]{2,1,0:T(8,128)S(1)} %pad_add_fusion.rock_ref, f32[16,8,8,128]{3,2,1,0:T(8,128)S(1)} %concatenate.39.inflow_ref), custom_call_target="tpu_custom_call" | custom-call | tf_op jit(solution)/shard_map/flux/pallas_call | solution.py:191
  52.0 1.2 fusion.18
  53.2 0.9 fusion.20
  54.3 27.2 %all_sum.1 = f32[32,16,128]{2,1,0:T(8,128)S(1)} custom-call(f32[32,16,128]{2,1,0:T(8,128)S(1)} %bitcast.176), custom_call_target="tpu_custom_call" | custom-call | tf_op jit(solution)/shard_map/all_sum/pallas_call | solution.py:289
  81.6 0.7 copy.59
  82.6 0.4 convolution_add_fusion.5
  83.0 0.4 convolution_add_fusion.6
  84.9 0.9 convolution_add_fusion.9
  85.8 0.4 fusion.88
  86.2 0.6 convolution_add_fusion.2
  87.0 0.7 copy-done.4
  87.7 11.7 %cholesky.130 = f32[128,128]{1,0:T(8,128)S(1)} custom-call(f32[128,128]{1,0:T(8,128)S(1)} %cholesky.194), custom_call_target="Cholesky" | custom-call | tf_op jit(solution)/shard_map/jit(cholesky)/cholesky | solution.py:319
  99.5 10.0 %custom-call.13 = f32[1,128,128]{1,2,0:T(8,128)S(1)} custom-call(f32[1,128,128]{2,1,0:T(8,128)S(1)} %get-tuple-element.78), custom_call_target="InvertDiagBlocksLowerTriangular" | custom-call | tf_op jit(solution)/shard_map/jit(cholesky)/cholesky | solution.py:319
  109.5 1.0 constant_dynamic-update-slice_fusion.3
  110.6 1.1 convolution_subtract_fusion.3
  111.7 11.7 %cholesky.147 = f32[128,128]{1,0:T(8,128)S(1)} custom-call(f32[128,128]{1,0:T(8,128)S(1)} %convolution_subtract_fusion.3), custom_call_target="Cholesky" | custom-call | tf_op jit(solution)/shard_map/jit(cholesky)/cholesky | solution.py:319
  123.4 0.7 compare_reduce_fusion.2
  125.5 5.3 %while.4 = (s32[]{:T(128)}, f32[256,256]{1,0:T(8,128)S(1)}, s32[2,2]{1,0:T(2,128)}, f32[2,128,128]{2,1,0:T(8,128)S(1)}, s32[]{:T(128)}) while((s32[]{:T(128)}, f32[256,256]{1,0:T(8,128)S(1)}, s32[2,2]{1,0:T(2,128)}, f32[2,128,128]{2,1,0:T(8,128)S(1)}, s32[]{:T(128)}) %tuple.64), condition=%wide.while_cond, body=%wide.while_body.sunk | while | flops 2 | bytes 131189 | solution.py:321
  125.5 0.7 constant_dynamic-slice_fusion.4
  126.2 0.6 fusion.161
  126.8 1.4 bitcast_dynamic-update-slice_fusion.4
  128.1 0.7 constant_dynamic-slice_fusion.4
  128.8 0.6 fusion.161
  129.4 1.4 bitcast_dynamic-update-slice_fusion.4
  130.8 20.1 %custom-call.14 = f32[2,128,128]{1,2,0:T(8,128)S(1)} custom-call(f32[2,128,128]{2,1,0:T(8,128)S(1)} %get-tuple-element.23), custom_call_target="InvertDiagBlocksLowerTriangular" | custom-call | tf_op jit(solution)/shard_map/triangular_solve/custom-call.0 | solution.py:321
  151.8 1.1 fusion.11
  152.9 0.4 fusion.13
  153.3 0.4 fusion.34
  153.7 0.3 fusion.33
  154.5 0.6 fusion.81
  155.8 0.4 fusion.89
  156.6 0.4 fusion.16
  157.5 0.4 convolution_add_fusion.3
  158.1 0.4 fusion.93
  158.6 0.6 convolution_add_fusion.1
  159.2 0.4 convolution_add_fusion.4
  159.8 11.7 %cholesky.164 = f32[128,128]{1,0:T(8,128)S(1)} custom-call(f32[128,128]{1,0:T(8,128)S(1)} %cholesky.197), custom_call_target="Cholesky" | custom-call | tf_op jit(solution)/shard_map/jit(cholesky)/cholesky | solution.py:319
  171.5 0.6 compare_reduce_fusion.1
  172.2 9.8 %custom-call.15 = f32[1,128,128]{1,2,0:T(8,128)S(1)} custom-call(f32[1,128,128]{2,1,0:T(8,128)S(1)} %get-tuple-element.74), custom_call_target="InvertDiagBlocksLowerTriangular" | custom-call | tf_op jit(solution)/shard_map/jit(cholesky)/cholesky | solution.py:319
  182.5 11.9 %cholesky.181 = f32[128,128]{1,0:T(8,128)S(1)} custom-call(f32[128,128]{1,0:T(8,128)S(1)} %convolution_subtract_fusion.2), custom_call_target="Cholesky" | custom-call | tf_op jit(solution)/shard_map/jit(cholesky)/cholesky | solution.py:319
  194.4 0.7 compare_reduce_fusion
  196.5 5.5 %while.5 = (s32[]{:T(128)}, f32[256,256]{1,0:T(8,128)S(1)}, s32[2,2]{1,0:T(2,128)}, f32[2,128,128]{2,1,0:T(8,128)S(1)}, s32[]{:T(128)}) while((s32[]{:T(128)}, f32[256,256]{1,0:T(8,128)S(1)}, s32[2,2]{1,0:T(2,128)}, f32[2,128,128]{2,1,0:T(8,128)S(1)}, s32[]{:T(128)}) %tuple.72), condition=%wide.while_cond.clone, body=%wide.while_body.clone.sunk | while | flops 2 | bytes 131189 | solution.py:321
  196.5 0.7 constant_dynamic-slice_fusion.5
  197.2 0.6 fusion.162
  197.8 1.4 bitcast_dynamic-update-slice_fusion.5
  199.3 0.7 constant_dynamic-slice_fusion.5
  199.9 0.6 fusion.162
  200.5 1.4 bitcast_dynamic-update-slice_fusion.5
  202.0 19.7 %custom-call.16 = f32[2,128,128]{1,2,0:T(8,128)S(1)} custom-call(f32[2,128,128]{2,1,0:T(8,128)S(1)} %get-tuple-element.24), custom_call_target="InvertDiagBlocksLowerTriangular" | custom-call | tf_op jit(solution)/shard_map/triangular_solve/custom-call.0 | solution.py:321
  222.6 1.1 fusion.12
  223.7 0.4 fusion.14
  224.0 0.3 convolution_convert_fusion.1
  224.4 0.4 fusion.32
  224.8 0.4 convolution_convert_fusion
  225.4 0.6 add_sqrt_fusion
  226.0 3.5 %convolution_bitcast_fusion = f32[8192,256]{0,1:T(8,128)S(1)} fusion(bf16[256,256]{1,0:T(8,128)(2,1)S(1)} %convolution_convert_fusion, bf16[8192,256]{1,0:T(8,128)(2,1)} %bitcast.177), kind=kOutput, calls=%fused_computation.5 | convolution fusion | flops 1073741824 | bytes 12713984 | tf_op jit(solution)/shard_map/dot_general | solution.py:403
  229.5 3.4 %fusion = bf16[8192,256]{0,1:T(8,128)(2,1)} fusion(f32[8192,256]{0,1:T(8,128)S(1)} %convolution_bitcast_fusion, bf16[8,8,64,128]{3,2,1,0:T(8,128)(2,1)S(1)} %bitcast.181, bf16[32,256]{1,0:T(8,128)(2,1)S(1)} %convolution_convert_fusion.1, bf16[32,256]{1,0:T(8,128)(2,1)S(1)} %convolution_convert_fusion.2), kind=kOutput, calls=%fused_computation.6 | convolution fusion | flops 272695296 | bytes 13664256 | tf_op jit(solution)/shard_map/dot_general | solution.py:404
  232.9 6.4 %copy.57 = bf16[8192,256]{1,0:T(8,128)(2,1)} copy(bf16[8192,256]{0,1:T(8,128)(2,1)} %fusion) | data formatting | bytes 8388608
  239.3 0.8 copy.102
  (85 shorter events, 8.2 us)
Async XLA Ops:
  0.6 2.5 %copy-start = (f32[16,256]{1,0:T(8,128)S(1)}, f32[16,256]{1,0:T(8,128)}, u32[]{:S(2)}) copy-start(f32[16,256]{1,0:T(8,128)} %param.14) | copy-start | bytes 49156
  5.1 5.2 %copy-start.1 = (f32[16,8,8,128]{3,2,1,0:T(8,128)S(1)}, f32[16,8,8,128]{3,2,1,0:T(8,128)}, u32[]{:S(2)}) copy-start(f32[16,8,8,128]{3,2,1,0:T(8,128)} %state_ref.1) | copy-start | bytes 1572868
  5.1 5.2 %copy-start.2 = (f32[3,16]{1,0:T(4,128)S(1)}, f32[3,16]{1,0:T(4,128)}, u32[]{:S(2)}) copy-start(f32[3,16]{1,0:T(4,128)} %table_ref.1) | copy-start | bytes 580
  10.3 42.9 %copy-start.3 = (bf16[1,64,128,256]{3,2,1,0:T(8,128)(2,1)S(1)}, bf16[1,64,128,256]{3,2,1,0:T(8,128)(2,1)}, u32[]{:S(2)}) copy-start(bf16[1,64,128,256]{3,2,1,0:T(8,128)(2,1)} %param.15) | copy-start | bytes 12582916
  86.2 66.7 %copy-start.5 = (f32[32,256]{1,0:T(8,128)S(1)}, f32[32,256]{1,0:T(8,128)}, u32[]{:S(2)}) copy-start(f32[32,256]{1,0:T(8,128)} %convolution_add_fusion.9) | copy-start | bytes 98308
  87.0 0.7 copy-start.4
  150.9 6.1 %copy-start.6 = (f32[32,32]{0,1:T(8,128)S(1)}, f32[32,32]{0,1:T(8,128)}, u32[]{:S(2)}) copy-start(f32[32,32]{0,1:T(8,128)} %copy.59) | copy-start | bytes 12292

commit v3 on v2

--- a/solution.py
+++ b/solution.py
@@ -306,47 +306,260 @@
 HIGH = lax.Precision.HIGHEST
 
 
-def hdot(a, b):
-    return jnp.dot(a, b, precision=HIGH)
-
-
-def batch_update(coeffs, gram_of, sigma):
-    rounded = coeffs.astype(jnp.bfloat16).astype(jnp.float32)
-    gram = gram_of(coeffs, rounded)
-    square = jnp.diag(sigma * sigma)
-    total = square + hdot(coeffs.T, coeffs)
-    inner = hdot(total, total) + hdot(coeffs.T, hdot(gram, coeffs))
-    factor = jnp.linalg.cholesky(inner)
-    eye = jnp.eye(sigma.shape[0], dtype=jnp.float32)
-    back = lax.linalg.triangular_solve(factor, eye, left_side=True, lower=True).T
-    top = sigma[:, None] * hdot(total, back)
-    bottom = hdot(hdot(coeffs, total) + hdot(gram, coeffs), back)
-    sigma_next = jnp.sqrt(jnp.sum(top * top, axis=0) + jnp.sum(bottom * bottom, axis=0))
-    on_basis = hdot(square + hdot((coeffs - rounded).T, coeffs), back)
-    on_snaps = hdot(coeffs, back)
-    return on_basis, on_snaps, sigma_next
-
-
-def small_algebra(uu, su, ss, sigma):
-    half = su.shape[0] // 2
-    s00, s10, s11 = ss[:half, :half], ss[half:, :half], ss[half:, half:]
-
-    def gram_first(c, r):
-        cr = hdot(c, r.T)
-        return s00 - cr - cr.T + hdot(r, hdot(uu, r.T))
-
-    wu, ws, sigma1 = batch_update(su[:half], gram_first, sigma)
-    coeffs1 = hdot(su[half:], wu) + hdot(s10, ws)
-
-    def gram_second(c, r):
-        cr = hdot(c, r.T)
-        yu, ys = hdot(wu, r.T), hdot(ws, r.T)
-        mixed = hdot(ys.T, hdot(su[:half], yu))
-        own = hdot(yu.T, hdot(uu, yu)) + mixed + mixed.T + hdot(ys.T, hdot(s00, ys))
-        return s11 - cr - cr.T + own
-
-    wu1, ws1, sigma2 = batch_update(coeffs1, gram_second, sigma1)
-    return hdot(wu, wu1), hdot(ws, wu1), ws1, sigma2
+def dot(a, b, contract=((1,), (0,))):
+    return lax.dot_general(a, b, (contract, ((), ())), precision=HIGH, preferred_element_type=F32)
+
+
+ROWS_BASIS = 256
+RANK = 32
+BLOCK = 8
+STRIDE = RANK + BLOCK
+
+
+def spread_row(ref, at):
+    return jnp.broadcast_to(ref[pl.ds(at, 1), :], (8, 128))
+
+
+def factor(c, gram, sigma, mx, ct, first, second, coef, yy, nat):
+    lane = lax.broadcasted_iota(jnp.int32, (8, 128), 1)
+    row = lax.broadcasted_iota(jnp.int32, (8, 128), 0)
+    group = lane // 32
+    g0, g1, g2 = group == 0, group == 1, group == 2
+
+    def wide(mask, rows):
+        return jnp.concatenate([mask] * (rows // 8), 0)
+
+    def turn(x, by):
+        return pltpu.roll(x, by, 1)
+
+    padded = jnp.concatenate([c, jnp.broadcast_to(sigma, (96, ROWS_BASIS))], 0)
+    ct[...] = padded.T
+    sig_col = turn(ct[...], 96)
+    sig_col = jnp.where(wide(lane, ROWS_BASIS) < 96, sig_col, turn(sig_col, 32))
+    inv2 = 1.0 / (sig_col * sig_col)
+
+    at = lax.broadcasted_iota(jnp.int32, (ROWS_BASIS, 128), 0)
+    over = lax.broadcasted_iota(jnp.int32, (ROWS_BASIS, 128), 1)
+    before = at < BLOCK * (over & 31)
+    pick = over // 32
+    masks = jnp.where(
+        pick == 0, jnp.where(before, inv2 * inv2, 0.0),
+        jnp.where(pick == 1, jnp.where(before, inv2, 0.0), jnp.where((pick == 2) & ~before, 1.0, 0.0)),
+    )
+    low = lax.broadcasted_iota(jnp.int32, (RANK, 128), 0)
+    lanes = wide(group, RANK)
+    for chunk in range(4):
+        pairs = jnp.concatenate([c * c[a : a + 1] for a in range(chunk * 8, chunk * 8 + 8)], 0)
+        sums = dot(pairs, masks)
+        for i in range(8):
+            a = chunk * 8 + i
+            mx[a * STRIDE : a * STRIDE + RANK, :] = (
+                sums[i * RANK : (i + 1) * RANK]
+                + jnp.where((lanes == 1) & (low == a), 1.0, 0.0)
+                + jnp.where(lanes == 2, jnp.broadcast_to(gram[:, a : a + 1], (RANK, 128)), 0.0)
+            )
+    fourth = []
+    for half in range(2):
+        mixed = jnp.concatenate([ct[pl.ds(half * 4 + t, 32, stride=8), :] for t in range(4)], 0).T
+        for t in range(4):
+            here = mixed if t == 0 else turn(mixed, 128 - 32 * t)
+            r1 = here[:RANK]
+            sig = here[RANK : 2 * RANK]
+            r2 = sig * sig * r1
+            mx[pl.ds(RANK + half * 4 + t, RANK, stride=STRIDE), :] = jnp.where(
+                lanes == 0, r1, jnp.where(lanes == 2, -turn(r2, 64), 0.0)
+            )
+            sq = sig[:8] * sig[:8]
+            fourth.append(sq * sq)
+
+    acc = tuple(jnp.zeros((8, 128), F32) for _ in range(BLOCK))
+    for part in range(4):
+        skip = part * 8
+        count = RANK - skip
+        w0, w1, w2 = wide(g0, count), wide(g1, count), wide(g2, count)
+
+        def step(k, acc):
+            base = pl.multiple_of(k * STRIDE, 8)
+            rk = mx[pl.ds(base + skip, count), :]
+            ck = mx[pl.ds(skip * STRIDE + k, count, stride=STRIDE), :]
+            pivot = spread_row(mx, base + k)
+            up, down, across = turn(pivot, 32), turn(pivot, 96), turn(pivot, 64)
+            p = jnp.where(g0, pivot, jnp.where(g1, up, across))
+            e = jnp.where(g0, down, jnp.where(g1, pivot, up))
+            q = jnp.where(g0, across, jnp.where(g1, down, pivot))
+            det = 1.0 / (p * q + e * e)
+            p, e, q = p * det, e * det, q * det
+            pw, ew, qw = (jnp.concatenate([z] * (count // 8), 0) for z in (p, e, q))
+            rk_up, rk_down, ck_down = turn(rk, 32), turn(rk, 96), turn(ck, 96)
+            u = jnp.where(w2, rk_up, jnp.where(w1, rk, rk))
+            v = jnp.where(w0, ck_down, jnp.where(w1, -rk_down, -rk))
+            fa = qw * u + ew * v
+            sa = ew * u - pw * v
+            first[pl.ds(pl.multiple_of(k * RANK, 8) + skip, count), :] = fa
+            second[pl.ds(pl.multiple_of(k * RANK, 8) + skip, count), :] = sa
+            coef[0, skip:RANK, :] = jnp.where(w0, rk, jnp.where(w1, rk_up, -rk_up))
+            coef[1, skip:RANK, :] = jnp.where(w0, ck_down, ck)
+            right = mx[pl.ds(base + RANK, 8), :]
+            swapped = turn(right, 64)
+            u = jnp.where(g0, right, swapped)
+            v = jnp.where(g0, -swapped, -right)
+            fr = q * u + e * v
+            sr = e * u - p * v
+            yy[pl.ds(pl.multiple_of(k * 8, 8), 8), :] = jnp.where(g0, fr, turn(sr, 32))
+            acc = tuple(
+                acc[t]
+                + jnp.broadcast_to(u[t : t + 1], (8, 128)) * fr
+                + jnp.broadcast_to(v[t : t + 1], (8, 128)) * sr
+                for t in range(BLOCK)
+            )
+            fall = jnp.concatenate([fa, fr], 0)
+            sall = jnp.concatenate([sa, sr], 0)
+            for i in range(skip, RANK):
+                f = jnp.broadcast_to(coef[0, i : i + 1, :], (8, 128))
+                s = jnp.broadcast_to(coef[1, i : i + 1, :], (8, 128))
+                for part8 in range(count // 8 + 1):
+                    where = i * STRIDE + skip + part8 * 8
+                    mx[where : where + 8, :] = mx[where : where + 8, :] - (
+                        f * fall[part8 * 8 : part8 * 8 + 8] + s * sall[part8 * 8 : part8 * 8 + 8]
+                    )
+            return acc
+
+        acc = lax.fori_loop(skip, skip + 8, step, acc)
+
+    ys = [None] * RANK
+    for k in range(RANK - 1, -1, -1):
+        y = yy[k * 8 : k * 8 + 8, :]
+        if k < RANK - 1:
+            a1 = a2 = None
+            for l in range(RANK - 1, k, -1):
+                m1 = spread_row(first, k * RANK + l) * ys[l]
+                m2 = spread_row(second, k * RANK + l) * ys[l]
+                a1 = m1 if a1 is None else a1 + m1
+                a2 = m2 if a2 is None else a2 + m2
+            y = y - jnp.where(g0, a1 + turn(a1, 96), a2 + turn(a2, 32))
+        ys[k] = y
+
+    block = [acc[t] + jnp.where(row == t, fourth[t], 0.0) for t in range(BLOCK)]
+    scale = jnp.zeros((8, 128), F32)
+    steps = []
+    for s in range(BLOCK):
+        d = jnp.broadcast_to(block[s][s : s + 1], (8, 128))
+        scale = jnp.where(row == s, lax.rsqrt(d), scale)
+        ratio = jnp.where(row > s, block[s] / d, 0.0)
+        steps.append(ratio)
+        for t in range(s + 1, BLOCK):
+            block[t] = block[t] - jnp.broadcast_to(block[s][t : t + 1], (8, 128)) * ratio
+    for index in range(2 * RANK + BLOCK):
+        if index < RANK:
+            value = ys[index]
+        elif index < 2 * RANK:
+            value = turn(ys[index - RANK], 96)
+        else:
+            value = jnp.where(row == index - 2 * RANK, 1.0, 0.0)
+        for s in range(BLOCK - 1):
+            value = value - steps[s] * jnp.broadcast_to(value[s : s + 1], (8, 128))
+        yy[index * 8 : index * 8 + 8, :] = value * scale
+    for half in range(2):
+        mixed = None
+        for t in range(4):
+            part = yy[pl.ds(half * 4 + t, 128, stride=8), :]
+            part = part if t == 0 else turn(part, 32 * t)
+            mixed = part if t == 0 else jnp.where(wide(group, 128) == t, part, mixed)
+        mixed = mixed.T
+        for t in range(4):
+            nat[pl.ds(half * 4 + t, 32, stride=8), :] = mixed[32 * t : 32 * t + 32]
+
+    inv_row = 1.0 / (sigma * sigma)
+    weighed = jnp.concatenate([c * (inv_row * inv_row), c * inv_row], 0)
+    across = lax.broadcasted_iota(jnp.int32, (ROWS_BASIS, ROWS_BASIS), 1)
+    down = lax.broadcasted_iota(jnp.int32, (ROWS_BASIS, ROWS_BASIS), 0)
+    tile = jnp.where(
+        (lax.broadcasted_iota(jnp.int32, (BLOCK, ROWS_BASIS), 1) & 7)
+        == lax.broadcasted_iota(jnp.int32, (BLOCK, ROWS_BASIS), 0), 1.0, 0.0
+    )
+    natural = nat[...]
+    below = -dot(natural[:, : 2 * RANK], weighed)
+    own = dot(natural[:, 2 * RANK : 2 * RANK + BLOCK], tile)
+    inverse = jnp.where(across // 8 < down // 8, below, jnp.where(across // 8 == down // 8, own, 0.0))
+    return inverse, sig_col
+
+
+def batch_update(c, rounded, gram, sigma, *scratch):
+    inverse, sig_col = factor(c, gram, sigma, *scratch)
+    sig = jnp.concatenate([sig_col, sig_col], 1)
+    on_snaps = dot(c, inverse, ((1,), (1,)))
+    scaled = sig * sig * inverse.T
+    total = scaled + dot(c, on_snaps, ((0,), (0,)))
+    on_basis = scaled + dot(c - rounded, on_snaps, ((0,), (0,)))
+    top = sig * total
+    bottom = dot(c, total) + dot(gram, on_snaps)
+    energy = jnp.sum(top * top, axis=0, keepdims=True) + jnp.sum(bottom * bottom, axis=0, keepdims=True)
+    return on_basis, on_snaps, jnp.sqrt(energy)
+
+
+def small_kernel(rows_total, whole_ref, sigma_ref, mix_ref, sigma_out_ref, half_uu, *scratch):
+    scale = 1.0 / rows_total
+
+    def piece(index):
+        return whole_ref[64 * index : 64 * (index + 1), :] * scale
+
+    high = lax.broadcasted_iota(jnp.int32, (64, 128), 1) >= 64
+    last = piece(6)
+    half_uu[...] = jnp.zeros((256, 256), F32)
+    half_uu[0:64, 0:128] = jnp.where(high, 1.0, 0.5) * piece(2)
+    half_uu[0:64, 128:256] = piece(3)
+    half_uu[64:128, 0:128] = jnp.where(high, 0.5 * last, 0.0)
+    half_uu[64:128, 128:256] = piece(4)
+    half_uu[128:192, 128:256] = jnp.where(high, 1.0, 0.5) * piece(5)
+    half_uu[192:256, 128:256] = jnp.where(high, 0.5 * pltpu.roll(last, 64, 1), 0.0)
+    su = jnp.concatenate([piece(0), piece(1)], 1)
+    ss = piece(7)
+    s00, s10, s11 = ss[:32, :32], ss[32:, :32], ss[32:, 32:64]
+
+    def of_basis(x):
+        part = dot(dot(x, half_uu[...]), x, ((1,), (1,)))
+        return part + part.T
+
+    def twice(c, r):
+        part = dot(c, r, ((1,), (1,)))
+        return part + part.T
+
+    c0 = su[:32]
+    r0 = c0.astype(BF16).astype(F32)
+    gram0 = s00 - twice(c0, r0) + of_basis(r0)
+    wu, ws, sigma1 = batch_update(c0, r0, gram0, sigma_ref[...], *scratch)
+    c1 = dot(su[32:], wu) + dot(s10, ws)
+    r1 = c1.astype(BF16).astype(F32)
+    yu = dot(r1, wu, ((1,), (1,)))
+    ys = dot(r1, ws, ((1,), (1,)))
+    cross = dot(dot(ys, c0), yu, ((1,), (1,)))
+    gram1 = s11 - twice(c1, r1) + of_basis(yu) + cross + cross.T + dot(dot(ys, s00), ys, ((1,), (1,)))
+    wu1, ws1, sigma2 = batch_update(c1, r1, gram1, sigma1, *scratch)
+    mix_ref[0:256, :] = dot(wu, wu1).astype(BF16)
+    mix_ref[256:288, :] = dot(ws, wu1).astype(BF16)
+    mix_ref[288:320, :] = ws1.astype(BF16)
+    sigma_out_ref[...] = sigma2
+
+
+def small_algebra(whole, sigma, rows_total):
+    return pl.pallas_call(
+        lambda *refs: small_kernel(float(rows_total), *refs),
+        out_shape=(jax.ShapeDtypeStruct((320, 256), BF16), jax.ShapeDtypeStruct((1, 256), F32)),
+        in_specs=[pl.BlockSpec(memory_space=VMEM)] * 2,
+        out_specs=(pl.BlockSpec(memory_space=VMEM),) * 2,
+        scratch_shapes=[
+            VMEM((256, 256), F32),
+            VMEM((RANK * STRIDE, 128), F32),
+            VMEM((256, 128), F32),
+            VMEM((RANK * RANK, 128), F32),
+            VMEM((RANK * RANK, 128), F32),
+            VMEM((2, RANK, 128), F32),
+            VMEM((128 * 8, 128), F32),
+            VMEM((256, 128), F32),
+        ],
+        compiler_params=pltpu.CompilerParams(vmem_limit_bytes=32 * 1024 * 1024),
+        name="small_algebra",
+    )(whole, sigma.reshape(1, -1))
 
 
 def body(state_init, rock_type, perm_table, well_cells, well_rate, basis_in, singular):
@@ -385,26 +598,15 @@
             uu[:64, 128:],
             uu[64:128, 128:],
             uu[128:192, 128:],
-            jnp.concatenate([uu[64:128, 64:128], uu[192:, 192:]], 1),
+            jnp.concatenate([uu[192:, 192:], uu[64:128, 64:128]], 1),
             jnp.pad(ss, ((0, 0), (0, 64))),
         ],
         0,
     )
-    whole = all_sum(local) / rows_total
-    part = [whole[64 * i : 64 * (i + 1)] for i in range(8)]
-    su = jnp.concatenate([part[0], part[1]], 1)
-    row0 = jnp.concatenate([part[2], part[3]], 1)
-    row1 = jnp.concatenate([row0[:, 64:128].T, part[6][:, :64], part[4]], 1)
-    row2 = jnp.concatenate([row0[:, 128:192].T, row1[:, 128:192].T, part[5]], 1)
-    row3 = jnp.concatenate([row0[:, 192:].T, row1[:, 192:].T, row2[:, 192:].T, part[6][:, 64:]], 1)
-    uu = jnp.concatenate([row0, row1, row2, row3], 0)
-    ss = part[7][:, :64]
-    w0, w1, w2, sigma = small_algebra(uu, su, ss, singular)
-    fresh = jnp.dot(basis, w0.astype(jnp.bfloat16), preferred_element_type=jnp.float32)
-    fresh = fresh + lax.dot_general(
-        both, jnp.concatenate([w1, w2], 0).astype(jnp.bfloat16), (((0,), (0,)), ((), ())), preferred_element_type=jnp.float32
-    )
-    return (state_out, fresh.astype(jnp.bfloat16).reshape(basis_in.shape), sigma)
+    mix, sigma = small_algebra(all_sum(local), singular, rows_total)
+    fresh = jnp.dot(basis, mix[:count], preferred_element_type=jnp.float32)
+    fresh = fresh + lax.dot_general(both, mix[count:], (((0,), (0,)), ((), ())), preferred_element_type=jnp.float32)
+    return (state_out, fresh.astype(jnp.bfloat16).reshape(basis_in.shape), sigma.reshape(-1))
 
 
 def solution(mesh):

time: 245 us -> 116 us (0.47); the launches traced: 240 us -> 116 us
  other arithmetic: 111 us -> 0.24 us
  Pallas kernels: 68.6 us -> 92.7 us
  matrix products: 33.5 us -> 13.7 us
  local copies, waits for them, and re-layouts: 22.7 us -> 8.69 us
  between operations: 4.13 us -> 0.81 us
    another operation x18 -> x0, other arithmetic: 109 us -> none  [the longest x13 69 us: batch_update(): factor = jnp.linalg.cholesky(inner)]
    pallas_call x0 -> x1, Pallas kernels: none -> 24.2 us  [small_algebra(): pl.pallas_call(lambda *refs: small_kernel(float(rows_total), *refs), out_...]
    dot_general x38 -> x2, matrix products: 20.2 us -> 4.67 us  [the longest x1 3.33 us: body(): lax.dot_general(both, mix[count:], (((0,), (0,)), ((), ())), preferred_el...]
    another operation x19 -> x0, local copies, waits for them, and re-layouts: 11.4 us -> none  [the longest x15 11.4 us: batch_update(): lax.linalg.triangular_solve(factor, eye, left_side=True, lower=True)]
    another operation x10 -> x0, matrix products: 4.39 us -> none  [the longest x4 2.62 us: batch_update(): factor = jnp.linalg.cholesky(inner)]
    unnamed x22 -> x16, local copies, waits for them, and re-layouts: 8.66 us -> 7.2 us
where the time goes in v3:
time: 116 us
  Pallas kernels  92.7 us (80%)
  matrix products  13.7 us (12%)
  local copies, waits for them, and re-layouts  8.69 us (7%)
    pallas_call x1, Pallas kernels, flux(): pl.pallas_call(flux_kernel, out_shape=(jax.ShapeDtypeStruct((MEMB * 64, 1...  41.2 us
    pallas_call x1, Pallas kernels, all_sum(): pl.pallas_call(reduce_kernel, out_shape=jax.ShapeDtypeStruct((PLANE, rows...  27.3 us
    pallas_call x1, Pallas kernels, small_algebra(): pl.pallas_call(lambda *refs: small_kernel(float(rows_total), *refs), out_...  24.2 us
    unnamed x16, local copies, waits for them, and re-layouts  7.2 us
    dot_general x1, matrix products, body(): lax.dot_general(basis, basis, (((0,), (0,)), ((), ())), preferred_element...  4.79 us
    dot_general x1, matrix products, body(): lax.dot_general(both, mix[count:], (((0,), (0,)), ((), ())), preferred_el...  3.33 us

profile of v3, /device:TPU:1, one launch (start us, length us, event | category | flops | bytes accessed | tf_op | source)
XLA Modules:
  0.0 116.1 jit_solution(3129177820332468864)
XLA Ops:
  0.6 0.0 copy-start
  0.7 0.1 iota_add_fusion
  0.7 0.1 reshape.87
  0.8 0.8 reshape.75
  1.6 0.1 pad_add_fusion.rock_ref
  1.7 0.0 copy-done
  1.7 2.0 %convolution_bitcast_fusion.1 = f32[16,4096]{1,0:T(8,128)S(1)} fusion(f32[16,256]{1,0:T(8,128)S(1)} %copy-done, s32[4096]{0:T(1024)S(1)} %reshape.87, s32[256]{0:T(256)} %param.10), kind=kOutput, calls=%fused_computation.3 | convolution fusion | flops 202375168 | bytes 295936 | tf_op jit(solution)/shard_map/dot_general | solution.py:579
  3.7 0.0 copy-start.1
  3.7 0.0 copy-start.2
  3.7 4.8 %fusion.6 = f32[256,256]{1,0:T(8,128)S(1)} fusion(bf16[1,64,128,256]{3,2,1,0:T(8,128)(2,1)} %param.12), kind=kOutput, calls=%fused_computation.9 | convolution fusion | flops 1073741824 | bytes 4456448 | tf_op jit(solution)/shard_map/dot_general | solution.py:590
  8.5 0.1 fusion.19
  8.6 0.2 reshape.76
  8.8 0.0 copy-start.4
  8.9 0.0 copy-done.1
  8.9 0.0 copy-done.2
  8.9 41.2 %flux.1 = (f32[1024,128]{1,0:T(8,128)S(1)}, bf16[4,64,16,128]{3,2,1,0:T(8,128)(2,1)S(1)}) custom-call(f32[3,16]{1,0:T(4,128)S(1)} %copy-done.2, f32[16,8,8,128]{3,2,1,0:T(8,128)S(1)} %copy-done.1, s32[8,8,128]{2,1,0:T(8,128)S(1)} %pad_add_fusion.rock_ref, f32[16,8,8,128]{3,2,1,0:T(8,128)S(1)} %concatenate.14.inflow_ref), custom_call_target="tpu_custom_call" | custom-call | tf_op jit(solution)/shard_map/flux/pallas_call | solution.py:191
  50.1 0.3 copy.13
  50.4 0.0 copy-start.3
  50.4 1.2 %fusion.10 = f32[64,64]{1,0:T(8,128)S(1)} fusion(bf16[8,8,64,128]{3,2,1,0:T(8,128)(2,1)S(1)} %bitcast.39), kind=kOutput, calls=%fused_computation.11 | convolution fusion | flops 67108864 | bytes 1064960 | tf_op jit(solution)/shard_map/dot_general | solution.py:592
  51.6 0.0 copy-done.4
  51.6 1.0 fusion.12
  52.6 0.1 maximum_dynamic-update-slice_fusion
  52.7 27.3 %all_sum.1 = f32[32,16,128]{2,1,0:T(8,128)S(1)} custom-call(f32[32,16,128]{2,1,0:T(8,128)S(1)} %bitcast.35), custom_call_target="tpu_custom_call" | custom-call | tf_op jit(solution)/shard_map/all_sum/pallas_call | solution.py:289
  80.0 0.0 copy-done.3
  80.0 24.2 %small_algebra.1 = (bf16[320,256]{1,0:T(8,128)(2,1)S(1)}, f32[1,256]{1,0:T(1,128)}) custom-call(f32[512,128]{1,0:T(8,128)S(1)} %bitcast.33, f32[1,256]{1,0:T(1,128)S(1)} %bitcast.36), custom_call_target="tpu_custom_call" | custom-call | tf_op jit(solution)/shard_map/small_algebra/pallas_call | solution.py:545
  104.3 1.3 %convolution_bitcast_fusion = f32[8192,256]{0,1:T(8,128)S(1)} fusion(bf16[8192,256]{1,0:T(8,128)(2,1)S(1)} %bitcast.38, bf16[320,256]{1,0:T(8,128)(2,1)S(1)} %get-tuple-element.9), kind=kOutput, calls=%fused_computation.1 | convolution fusion | flops 1073741824 | bytes 12713984 | tf_op jit(solution)/shard_map/dot_general | solution.py:607
  105.6 3.3 %fusion = bf16[8192,256]{0,1:T(8,128)(2,1)} fusion(f32[8192,256]{0,1:T(8,128)S(1)} %convolution_bitcast_fusion, bf16[8,8,64,128]{3,2,1,0:T(8,128)(2,1)S(1)} %bitcast.41, bf16[320,256]{1,0:T(8,128)(2,1)S(1)} %get-tuple-element.9), kind=kOutput, calls=%fused_computation.2 | convolution fusion | flops 272629760 | bytes 13664256 | tf_op jit(solution)/shard_map/dot_general | solution.py:608
  109.0 6.4 %copy.19 = bf16[8192,256]{1,0:T(8,128)(2,1)} copy(bf16[8192,256]{0,1:T(8,128)(2,1)} %fusion) | data formatting | bytes 8388608
  115.3 0.8 copy.39
  (7 shorter events, 0.1 us)
Async XLA Ops:
  0.6 1.1 copy-start
  3.7 5.2 %copy-start.1 = (f32[16,8,8,128]{3,2,1,0:T(8,128)S(1)}, f32[16,8,8,128]{3,2,1,0:T(8,128)}, u32[]{:S(2)}) copy-start(f32[16,8,8,128]{3,2,1,0:T(8,128)} %state_ref.1) | copy-start | bytes 1572868
  3.7 5.2 %copy-start.2 = (f32[3,16]{1,0:T(4,128)S(1)}, f32[3,16]{1,0:T(4,128)}, u32[]{:S(2)}) copy-start(f32[3,16]{1,0:T(4,128)} %table_ref.1) | copy-start | bytes 580
  8.8 42.7 %copy-start.4 = (bf16[1,64,128,256]{3,2,1,0:T(8,128)(2,1)S(1)}, bf16[1,64,128,256]{3,2,1,0:T(8,128)(2,1)}, u32[]{:S(2)}) copy-start(bf16[1,64,128,256]{3,2,1,0:T(8,128)(2,1)} %param.12) | copy-start | bytes 12582916
  50.4 29.7 %copy-start.3 = (f32[256]{0:T(256)S(1)}, f32[256]{0:T(256)}, u32[]{:S(2)}) copy-start(f32[256]{0:T(256)} %param.13) | copy-start | bytes 3076

commit v4 on v3

--- a/solution.py
+++ b/solution.py
@@ -30,10 +30,19 @@
     )
 
 
-def flux_kernel(
-    table_ref, state_ref, rock_ref, inflow_ref, out_ref, snaps_ref,
-    perm_send, perm_recv, x_send, x_recv, y_send, y_recv, y_wide, weights, turned, packed,
-    ps_sem, pr_sem, hs_sem, hr_sem, ss_sem, sr_sem, own_sem,
+PLANE = 32
+COLUMN = 8
+
+
+SHARE = 16
+CHUNKS = 8
+
+
+def slab_kernel(
+    table_ref, state_ref, rock_ref, cells_ref, rate_ref, basis_hbm, out_ref, snaps_ref, sum_ref,
+    basis, uu, inflow, kinds, perm_send, perm_recv, x_send, x_recv, y_send, y_recv, y_wide, weights, turned, packed,
+    local, slots, partial, column,
+    load_sem, ps_sem, pr_sem, hs_sem, hr_sem, ss_sem, sr_sem, own_sem, send1, recv1, send2, recv2, send3, recv3,
 ):
     gx_count, sec_count = lax.axis_size("gx"), lax.axis_size("sec")
     gx, sec = lax.axis_index("gx"), lax.axis_index("sec")
@@ -43,20 +52,85 @@
         {"sec": lax.rem(sec + sec_count - 1, sec_count)},
         {"sec": lax.rem(sec + 1, sec_count)},
     )
+    z_hi, z_lo = lax.rem(gx // 2, 4), sec // 4
+    me = (gx // 8) * 8 + lax.rem(gx, 2) * 4 + lax.rem(sec, 4)
+    me_z = z_hi * 2 + z_lo
+
+    def in_plane(p):
+        return {"gx": (p // 8) * 8 + z_hi * 2 + lax.rem(p // 4, 2), "sec": z_lo * 4 + lax.rem(p, 4)}
+
+    def in_column(q):
+        return {"gx": (gx // 8) * 8 + (q // 2) * 2 + lax.rem(gx, 2), "sec": lax.rem(q, 2) * 4 + lax.rem(sec, 4)}
+
     barrier = pltpu.get_barrier_semaphore()
-    for device in beside[:2]:
+
+    def greet(device):
         pl.semaphore_signal(barrier, inc=1, device_id=device, device_id_type=MESH)
+
+    greet(beside[0])
+    greet(beside[1])
     for ahead in range(1, sec_count):
-        pl.semaphore_signal(
-            barrier, inc=1, device_id={"sec": lax.rem(sec + ahead, sec_count)}, device_id_type=MESH
-        )
+        greet({"sec": lax.rem(sec + ahead, sec_count)})
+    for k in range(1, COLUMN):
+        greet(in_column(lax.rem(me_z + k, COLUMN)))
+    for k in range(1, PLANE):
+        greet(in_plane(lax.rem(me + k, PLANE)))
+
+    def load(c):
+        rows = pl.ds(pl.multiple_of(c * 1024, 1024), 1024)
+        return pltpu.make_async_copy(basis_hbm.at[rows], basis.at[rows], load_sem.at[c])
+
+    for c in range(CHUNKS):
+        load(c).start()
 
     lane = lax.broadcasted_iota(jnp.int32, (8, 128), 1)
     row = lax.broadcasted_iota(jnp.int32, (8, 128), 0)
 
+    def uu_chunk(c, carry):
+        load(c).wait()
+        part = basis[pl.ds(pl.multiple_of(c * 1024, 1024), 1024), :]
+        tn = (((0,), (0,)), ((), ()))
+        uu[0:128, :] += lax.dot_general(part[:, :128], part, tn, preferred_element_type=F32)
+        uu[128:256, 128:256] += lax.dot_general(part[:, 128:], part[:, 128:], tn, preferred_element_type=F32)
+        return carry
+
+    def halo_copies(step, g):
+        copies = []
+        for d in range(4):
+            if d < 2:
+                src = x_send.at[step, d, pl.ds(g * MG, MG)]
+                dst = x_recv.at[step, 1 - d, pl.ds(g * MG, MG)]
+            else:
+                rows = pl.ds(pl.multiple_of(g * 8 * MG, 8 * MG), 8 * MG)
+                src = y_send.at[step, d - 2, rows]
+                dst = y_recv.at[step, 3 - d, rows]
+            copies.append(remote(src, dst, hs_sem.at[step, g, d], hr_sem.at[step, g, d ^ 1], beside[d]))
+        return copies
+
+    def stage_y(step, g):
+        for side, y in ((0, 0), (1, 7)):
+            rows = pl.ds(pl.multiple_of(g * 8 * MG, 8 * MG), 8 * MG)
+            y_send[step, side, rows, :] = out_ref[pl.ds(g * 64 * MG + y, 8 * MG, stride=8), :].astype(BF16)
+
+    def first(m, carry):
+        x_send[0, 0, m] = state_ref[m, 0].astype(BF16)
+        x_send[0, 1, m] = state_ref[m, 7].astype(BF16)
+        for x in range(8):
+            out_ref[pl.ds(pl.multiple_of(m * 64 + x * 8, 8), 8), :] = state_ref[m, x]
+        return carry
+
+    lax.fori_loop(0, MEMB, first, 0)
+    stage_y(0, 0)
+    stage_y(0, 1)
+
+    for pair in range(4):
+        both = rock_ref[:, pair * 128 : pair * 128 + 128]
+        other = pltpu.roll(both, 64, 1)
+        kinds[pl.ds(2 * pair, 8, stride=8), :] = jnp.where(lane < 64, both, other)
+        kinds[pl.ds(2 * pair + 1, 8, stride=8), :] = jnp.where(lane < 64, other, both)
     perm = [[], [], []]
     for x in range(8):
-        kind = rock_ref[x]
+        kind = kinds[x * 8 : x * 8 + 8, :]
         for d in range(3):
             value = jnp.full((8, 128), table_ref[d, 0], F32)
             for r in range(1, 16):
@@ -68,36 +142,38 @@
         perm_send[2, pl.ds(x, 1), :] = perm[1][x][0:1]
         perm_send[3, pl.ds(x, 1), :] = perm[1][x][7:8]
 
-    def halo_copies(step):
-        pairs = []
-        for d in range(4):
-            send = (x_send if d < 2 else y_send).at[step, d % 2]
-            recv = (x_recv if d < 2 else y_recv).at[step, 1 - d % 2]
-            pairs.append(remote(send, recv, hs_sem.at[step, d], hr_sem.at[step, d ^ 1], beside[d]))
-        return pairs
-
-    def stage_y(step):
-        y_send[step, 0] = out_ref[pl.ds(0, 128, stride=8), :].astype(BF16)
-        y_send[step, 1] = out_ref[pl.ds(7, 128, stride=8), :].astype(BF16)
-
-    def first(m, carry):
-        x_send[0, 0, m] = state_ref[m, 0].astype(BF16)
-        x_send[0, 1, m] = state_ref[m, 7].astype(BF16)
-        for x in range(8):
-            out_ref[pl.ds(pl.multiple_of(m * 64 + x * 8, 8), 8), :] = state_ref[m, x]
-        return carry
-
-    lax.fori_loop(0, MEMB, first, 0)
-    stage_y(0)
-    pl.semaphore_wait(barrier, 1 + sec_count)
+    uu[...] = jnp.zeros((256, 256), F32)
+    pl.semaphore_wait(barrier, 2 + (sec_count - 1) + (COLUMN - 1) + (PLANE - 1))
     perm_copies = [
         remote(perm_send.at[d], perm_recv.at[d ^ 1], ps_sem.at[d], pr_sem.at[d ^ 1], beside[d]) for d in range(4)
     ]
     for copy in perm_copies:
         copy.start()
-    flying = halo_copies(0)
-    for copy in flying:
-        copy.start()
+    for g in range(GROUPS):
+        for copy in halo_copies(0, g):
+            copy.start()
+
+    rate = rate_ref[...]
+    top = rate.astype(BF16)
+    rest = rate - top.astype(F32)
+    middle = rest.astype(BF16)
+    parts = jnp.concatenate([top, middle, (rest - middle.astype(F32)).astype(BF16)], 0)
+    wells = cells_ref[...]
+    cell = lax.broadcasted_iota(jnp.int32, (512, 256), 0)
+
+    def place(x, carry):
+        ids = ((gx * 8 + x) * (8 * sec_count) + sec * 8) * 64 + cell
+        hits = jnp.where(ids == wells, 1.0, 0.0).astype(BF16)
+        found = lax.dot_general(parts, hits, (((1,), (1,)), ((), ())), preferred_element_type=F32)
+        found = found[:MEMB] + found[MEMB : 2 * MEMB] + found[2 * MEMB :]
+        for y in range(8):
+            pair = found[:, (y // 2) * 128 : (y // 2) * 128 + 128]
+            pair = pair if y % 2 == 0 else pltpu.roll(pair, 64, 1)
+            half = lax.broadcasted_iota(jnp.int32, (MEMB, 128), 1) < 64
+            inflow[pl.ds(x * 8 + y, MEMB, stride=64), :] = jnp.where(half, DT_PRESSURE * pair, 0.0)
+        return carry
+
+    lax.fori_loop(0, 8, place, 0)
 
     z_up = jnp.where((lane & 63) == 63, 0.0, 1.0)
     z_down = jnp.where((lane & 63) == 0, 0.0, 1.0)
@@ -122,86 +198,164 @@
 
     step_sizes = jnp.where(lane < 64, DT_PRESSURE, DT_SATURATION)
     advect = jnp.where(lane < 64, 0.0, DT_ADVECT)
-    sent = []
+
+    def snap_copies(step):
+        copies = [
+            pltpu.make_async_copy(packed.at[step, sec], snaps_ref.at[step, pl.ds(sec * 8, 8)], own_sem.at[step])
+        ]
+        for ahead in range(1, sec_count):
+            target = lax.rem(sec + ahead, sec_count)
+            copies.append(
+                remote(
+                    packed.at[step, target], snaps_ref.at[step, pl.ds(sec * 8, 8)],
+                    ss_sem.at[step, ahead], sr_sem.at[step, ahead], {"sec": target},
+                )
+            )
+        return copies
+
     for step in range(STEPS):
-        for copy in flying:
-            copy.wait()
-        y_wide[0] = y_recv[step, 0].astype(F32)
-        y_wide[1] = y_recv[step, 1].astype(F32)
-
-        def member(m, carry):
-            base = pl.multiple_of(m * 64, 64)
-            old = [out_ref[pl.ds(base + x * 8, 8), :] for x in range(8)]
-            old_below = x_recv[step, 0, m].astype(F32)
-            old_above = x_recv[step, 1, m].astype(F32)
-            for x in range(8):
-                here = old[x]
-                left = jnp.broadcast_to(y_wide[0, pl.ds(m * 8 + x, 1), :], (8, 128))
-                right = jnp.broadcast_to(y_wide[1, pl.ds(m * 8 + x, 1), :], (8, 128))
-                besides = (
-                    old[x + 1] if x < 7 else old_above,
-                    old[x - 1] if x > 0 else old_below,
-                    jnp.where(row == 7, right, pltpu.roll(here, 7, 0)),
-                    jnp.where(row == 0, left, pltpu.roll(here, 1, 0)),
-                    pltpu.roll(here, 127, 1),
-                    pltpu.roll(here, 1, 1),
-                )
-                spread = carried = None
-                for d in range(6):
-                    flow = weights[d, x] * (besides[d] - here)
-                    pushed = pltpu.roll(flow, 64, 1)
-                    moved = pushed * jnp.where(pushed > 0.0, besides[d], here)
-                    spread = flow if spread is None else spread + flow
-                    carried = moved if carried is None else carried + moved
-                fresh = here + step_sizes * spread + advect * carried + DT_PRESSURE * inflow_ref[m, x]
-                out_ref[pl.ds(base + x * 8, 8), :] = fresh
-                turned[x, pl.ds(m, 8, stride=MEMB), :] = fresh
-                if step + 1 < STEPS and x in (0, 7):
-                    x_send[step + 1, x // 7, m] = fresh.astype(BF16)
+
+        def half_step(g, carry):
+            for copy in halo_copies(step, g):
+                copy.wait()
+            rows = pl.ds(pl.multiple_of(g * 8 * MG, 8 * MG), 8 * MG)
+            y_wide[0, rows, :] = y_recv[step, 0, rows, :].astype(F32)
+            y_wide[1, rows, :] = y_recv[step, 1, rows, :].astype(F32)
+
+            def member(index, carry):
+                m = g * MG + index
+                base = pl.multiple_of(m * 64, 64)
+                old = [out_ref[pl.ds(base + x * 8, 8), :] for x in range(8)]
+                old_below = x_recv[step, 0, m].astype(F32)
+                old_above = x_recv[step, 1, m].astype(F32)
+                for x in range(8):
+                    here = old[x]
+                    left = jnp.broadcast_to(y_wide[0, pl.ds(m * 8 + x, 1), :], (8, 128))
+                    right = jnp.broadcast_to(y_wide[1, pl.ds(m * 8 + x, 1), :], (8, 128))
+                    besides = (
+                        old[x + 1] if x < 7 else old_above,
+                        old[x - 1] if x > 0 else old_below,
+                        jnp.where(row == 7, right, pltpu.roll(here, 7, 0)),
+                        jnp.where(row == 0, left, pltpu.roll(here, 1, 0)),
+                        pltpu.roll(here, 127, 1),
+                        pltpu.roll(here, 1, 1),
+                    )
+                    spread = carried = None
+                    for d in range(6):
+                        flow = weights[d, x] * (besides[d] - here)
+                        pushed = pltpu.roll(flow, 64, 1)
+                        moved = pushed * jnp.where(pushed > 0.0, besides[d], here)
+                        spread = flow if spread is None else spread + flow
+                        carried = moved if carried is None else carried + moved
+                    fresh = here + step_sizes * spread + advect * carried + inflow[pl.ds(base + x * 8, 8), :]
+                    out_ref[pl.ds(base + x * 8, 8), :] = fresh
+                    turned[x, pl.ds(m, 8, stride=MEMB), :] = fresh
+                    if step + 1 < STEPS and x in (0, 7):
+                        x_send[step + 1, x // 7, m] = fresh.astype(BF16)
+                return carry
+
+            lax.fori_loop(0, MG, member, 0)
+            if step + 1 < STEPS:
+                stage_y(step + 1, g)
+                for copy in halo_copies(step + 1, g):
+                    copy.start()
             return carry
 
-        lax.fori_loop(0, MEMB, member, 0)
-        if step + 1 < STEPS:
-            stage_y(step + 1)
-            flying = halo_copies(step + 1)
-            for copy in flying:
-                copy.start()
+        lax.fori_loop(0, GROUPS, half_step, 0)
         for x in range(8):
             packed[step, x] = turned[x].reshape(8, MEMB, 128).astype(BF16)
-        mine = pltpu.make_async_copy(
-            packed.at[step, sec], snaps_ref.at[step, pl.ds(sec * 8, 8)], own_sem.at[step]
+        for copy in snap_copies(step):
+            copy.start()
+        lax.fori_loop(2 * step, 2 * step + 2, uu_chunk, 0)
+    for step in range(STEPS):
+        for copy in snap_copies(step):
+            copy.wait()
+
+    def gram(pair, carry):
+        su, ss = carry
+        lhs = jnp.concatenate(
+            [snaps_ref[:, 2 * pair].reshape(64, 128), snaps_ref[:, 2 * pair + 1].reshape(64, 128)], 1
         )
-        mine.start()
-        sent.append(mine)
-        for ahead in range(1, sec_count):
-            target = lax.rem(sec + ahead, sec_count)
-            copy = remote(
-                packed.at[step, target], snaps_ref.at[step, pl.ds(sec * 8, 8)],
-                ss_sem.at[step, ahead], sr_sem.at[step, ahead], {"sec": target},
-            )
-            copy.start()
-            sent.append(copy)
-    for copy in sent:
-        copy.wait()
-
-
-def flux(table, state, rock, inflow):
+        rhs = basis[pl.ds(pl.multiple_of(pair * 256, 256), 256), :]
+        su = su + jnp.dot(lhs, rhs, preferred_element_type=F32)
+        ss = ss + lax.dot_general(lhs, lhs, (((1,), (1,)), ((), ())), preferred_element_type=F32)
+        return su, ss
+
+    su, ss = lax.fori_loop(
+        0, 4 * sec_count, gram, (jnp.zeros((64, 256), F32), jnp.zeros((64, 64), F32)), unroll=4
+    )
+    zero = jnp.zeros((64, 64), F32)
+    for index, block in enumerate(
+        (
+            su[:, :128],
+            su[:, 128:],
+            uu[0:64, 0:128],
+            uu[0:64, 128:256],
+            uu[64:128, 128:256],
+            uu[128:192, 128:256],
+            jnp.concatenate([uu[192:256, 192:256], uu[64:128, 64:128]], 1),
+            jnp.concatenate([ss, zero], 1),
+        )
+    ):
+        local[4 * index : 4 * index + 4] = block.reshape(4, SHARE, 128)
+
+    slots[me] = local[me]
+
+    def scatter(k):
+        p = lax.rem(me + k, PLANE)
+        return remote(local.at[p], slots.at[me], send1.at[k], recv1.at[k], in_plane(p))
+
+    for k in range(1, PLANE):
+        scatter(k).start()
+    for k in range(1, PLANE):
+        scatter(k).wait()
+    total = slots[0]
+    for k in range(1, PLANE):
+        total = total + slots[k]
+    partial[...] = total
+    column[me_z] = total
+
+    def across(k):
+        q = lax.rem(me_z + k, COLUMN)
+        return remote(partial, column.at[me_z], send2.at[k], recv2.at[k], in_column(q))
+
+    for k in range(1, COLUMN):
+        across(k).start()
+    for k in range(1, COLUMN):
+        across(k).wait()
+    total = column[0]
+    for k in range(1, COLUMN):
+        total = total + column[k]
+    sum_ref[me] = total
+
+    def gather(k):
+        p = lax.rem(me + k, PLANE)
+        return remote(sum_ref.at[me], sum_ref.at[me], send3.at[k], recv3.at[k], in_plane(p))
+
+    for k in range(1, PLANE):
+        gather(k).start()
+    for k in range(1, PLANE):
+        gather(k).wait()
+
+
+def slab(table, state, rock, cells, rate, basis):
     sec_count = lax.axis_size("sec")
     dma = pltpu.SemaphoreType.DMA
+    in_vmem = pl.BlockSpec(memory_space=VMEM)
     return pl.pallas_call(
-        flux_kernel,
+        slab_kernel,
         out_shape=(
             jax.ShapeDtypeStruct((MEMB * 64, 128), F32),
             jax.ShapeDtypeStruct((STEPS, 8 * sec_count, MEMB, 128), BF16),
+            jax.ShapeDtypeStruct((PLANE, SHARE, 128), F32),
         ),
-        in_specs=[
-            pl.BlockSpec(memory_space=pltpu.SMEM),
-            pl.BlockSpec(memory_space=VMEM),
-            pl.BlockSpec(memory_space=VMEM),
-            pl.BlockSpec(memory_space=VMEM),
-        ],
-        out_specs=(pl.BlockSpec(memory_space=VMEM), pl.BlockSpec(memory_space=VMEM)),
+        in_specs=[pl.BlockSpec(memory_space=pltpu.SMEM)] + [in_vmem] * 4 + [pl.BlockSpec(memory_space=pltpu.HBM)],
+        out_specs=(in_vmem,) * 3,
         scratch_shapes=[
+            VMEM(basis.shape, BF16),
+            VMEM((256, 256), F32),
+            VMEM((MEMB * 64, 128), F32),
+            VMEM((64, 128), jnp.int32),
             VMEM((4, 8, 128), F32),
             VMEM((4, 8, 128), F32),
             VMEM((STEPS, 2, MEMB, 8, 128), BF16),
@@ -212,95 +366,42 @@
             VMEM((6, 8, 8, 128), F32),
             VMEM((8, 8 * MEMB, 128), F32),
             VMEM((STEPS, 8, 8, MEMB, 128), BF16),
-            dma((4,)), dma((4,)), dma((STEPS, 4)), dma((STEPS, 4)),
+            VMEM((PLANE, SHARE, 128), F32),
+            VMEM((PLANE, SHARE, 128), F32),
+            VMEM((SHARE, 128), F32),
+            VMEM((COLUMN, SHARE, 128), F32),
+            dma((CHUNKS,)), dma((4,)), dma((4,)), dma((STEPS, GROUPS, 4)), dma((STEPS, GROUPS, 4)),
             dma((STEPS, sec_count)), dma((STEPS, sec_count)), dma((STEPS,)),
-        ],
-        compiler_params=pltpu.CompilerParams(
-            collective_id=0, has_side_effects=True, vmem_limit_bytes=32 * 1024 * 1024
-        ),
-        name="flux",
-    )(table, state, rock, inflow)
-
-
-PLANE = 32
-COLUMN = 8
-
-
-def reduce_kernel(x_ref, out_ref, slots, partial, column, send1, recv1, send2, recv2, send3, recv3):
-    gx, sec = lax.axis_index("gx"), lax.axis_index("sec")
-    z_hi, z_lo = lax.rem(gx // 2, 4), sec // 4
-    me = (gx // 8) * 8 + lax.rem(gx, 2) * 4 + lax.rem(sec, 4)
-    me_z = z_hi * 2 + z_lo
-
-    def in_plane(p):
-        return {"gx": (p // 8) * 8 + z_hi * 2 + lax.rem(p // 4, 2), "sec": z_lo * 4 + lax.rem(p, 4)}
-
-    def in_column(q):
-        return {"gx": (gx // 8) * 8 + (q // 2) * 2 + lax.rem(gx, 2), "sec": lax.rem(q, 2) * 4 + lax.rem(sec, 4)}
-
-    barrier = pltpu.get_barrier_semaphore()
-    for k in range(1, PLANE):
-        pl.semaphore_signal(barrier, inc=1, device_id=in_plane(lax.rem(me + k, PLANE)), device_id_type=MESH)
-    for k in range(1, COLUMN):
-        pl.semaphore_signal(barrier, inc=1, device_id=in_column(lax.rem(me_z + k, COLUMN)), device_id_type=MESH)
-    slots[me] = x_ref[me]
-    pl.semaphore_wait(barrier, PLANE + COLUMN - 2)
-
-    def scatter(k):
-        p = lax.rem(me + k, PLANE)
-        return remote(x_ref.at[p], slots.at[me], send1.at[k], recv1.at[k], in_plane(p))
-
-    for k in range(1, PLANE):
-        scatter(k).start()
-    for k in range(1, PLANE):
-        scatter(k).wait()
-    total = slots[0]
-    for k in range(1, PLANE):
-        total = total + slots[k]
-    partial[...] = total
-    column[me_z] = total
-
-    def across(k):
-        q = lax.rem(me_z + k, COLUMN)
-        return remote(partial, column.at[me_z], send2.at[k], recv2.at[k], in_column(q))
-
-    for k in range(1, COLUMN):
-        across(k).start()
-    for k in range(1, COLUMN):
-        across(k).wait()
-    total = column[0]
-    for k in range(1, COLUMN):
-        total = total + column[k]
-    out_ref[me] = total
-
-    def gather(k):
-        p = lax.rem(me + k, PLANE)
-        return remote(out_ref.at[me], out_ref.at[me], send3.at[k], recv3.at[k], in_plane(p))
-
-    for k in range(1, PLANE):
-        gather(k).start()
-    for k in range(1, PLANE):
-        gather(k).wait()
-
-
-def all_sum(x):
-    rows = x.shape[0] // PLANE
-    dma = pltpu.SemaphoreType.DMA
-    out = pl.pallas_call(
-        reduce_kernel,
-        out_shape=jax.ShapeDtypeStruct((PLANE, rows, 128), F32),
-        in_specs=[pl.BlockSpec(memory_space=VMEM)],
-        out_specs=pl.BlockSpec(memory_space=VMEM),
-        scratch_shapes=[
-            VMEM((PLANE, rows, 128), F32), VMEM((rows, 128), F32), VMEM((COLUMN, rows, 128), F32),
             dma((PLANE,)), dma((PLANE,)), dma((COLUMN,)), dma((COLUMN,)), dma((PLANE,)), dma((PLANE,)),
         ],
         compiler_params=pltpu.CompilerParams(
-            collective_id=1, has_side_effects=True, vmem_limit_bytes=16 * 1024 * 1024
+            collective_id=0, has_side_effects=True, vmem_limit_bytes=40 * 1024 * 1024
         ),
-        name="all_sum",
-    )(x.reshape(PLANE, rows, 128))
-    return out.reshape(x.shape)
+        name="slab",
+    )(table, state, rock, cells, rate, basis)
+
+
+def rotate_kernel(basis_ref, snaps_ref, mix_ref, out_ref):
+    taken = jnp.concatenate([snaps_ref[:, y].reshape(64, 128).T for y in range(8)], 0)
+    lhs = jnp.concatenate([basis_ref[...], taken], 1)
+    out_ref[...] = jnp.dot(lhs, mix_ref[...], preferred_element_type=F32).astype(BF16)
+
+
+def rotate(basis, snaps, mix):
+    rows = basis.shape[0]
+    return pl.pallas_call(
+        rotate_kernel,
+        grid=(rows // 1024,),
+        out_shape=jax.ShapeDtypeStruct(basis.shape, BF16),
+        in_specs=[
+            pl.BlockSpec((1024, 256), lambda i: (i, 0)),
+            pl.BlockSpec((STEPS, 8, MEMB, 128), lambda i: (0, i, 0, 0)),
+            pl.BlockSpec((320, 256), lambda i: (0, 0)),
+        ],
+        out_specs=pl.BlockSpec((1024, 256), lambda i: (i, 0)),
+        compiler_params=pltpu.CompilerParams(vmem_limit_bytes=24 * 1024 * 1024),
+        name="rotate",
+    )(basis, snaps, mix)
 
 
 HIGH = lax.Precision.HIGHEST
@@ -497,6 +598,10 @@
     return on_basis, on_snaps, jnp.sqrt(energy)
 
 
+def by_batch(x):
+    return jnp.concatenate([x[16 * step + 8 * g : 16 * step + 8 * g + 8] for g in range(2) for step in range(4)], 0)
+
+
 def small_kernel(rows_total, whole_ref, sigma_ref, mix_ref, sigma_out_ref, half_uu, *scratch):
     scale = 1.0 / rows_total
 
@@ -512,9 +617,12 @@
     half_uu[64:128, 128:256] = piece(4)
     half_uu[128:192, 128:256] = jnp.where(high, 1.0, 0.5) * piece(5)
     half_uu[192:256, 128:256] = jnp.where(high, 0.5 * pltpu.roll(last, 64, 1), 0.0)
-    su = jnp.concatenate([piece(0), piece(1)], 1)
-    ss = piece(7)
-    s00, s10, s11 = ss[:32, :32], ss[32:, :32], ss[32:, 32:64]
+    su = by_batch(jnp.concatenate([piece(0), piece(1)], 1))
+    source = lax.broadcasted_iota(jnp.int32, (64, 64), 0)
+    target = lax.broadcasted_iota(jnp.int32, (64, 64), 1)
+    wanted = (target // 8 % 4) * 16 + (target // 32) * 8 + (target & 7)
+    ss = dot(by_batch(piece(7)[:, :64]), jnp.where(source == wanted, 1.0, 0.0))
+    s00, s10, s11 = ss[:32, :32], ss[32:, :32], ss[32:, 32:]
 
     def of_basis(x):
         part = dot(dot(x, half_uu[...]), x, ((1,), (1,)))
@@ -536,8 +644,10 @@
     gram1 = s11 - twice(c1, r1) + of_basis(yu) + cross + cross.T + dot(dot(ys, s00), ys, ((1,), (1,)))
     wu1, ws1, sigma2 = batch_update(c1, r1, gram1, sigma1, *scratch)
     mix_ref[0:256, :] = dot(wu, wu1).astype(BF16)
-    mix_ref[256:288, :] = dot(ws, wu1).astype(BF16)
-    mix_ref[288:320, :] = ws1.astype(BF16)
+    w0, w1 = dot(ws, wu1), ws1
+    mix_ref[256:320, :] = jnp.concatenate(
+        [w[8 * step : 8 * step + 8] for step in range(4) for w in (w0, w1)], 0
+    ).astype(BF16)
     sigma_out_ref[...] = sigma2
 
 
@@ -563,50 +673,12 @@
 
 
 def body(state_init, rock_type, perm_table, well_cells, well_rate, basis_in, singular):
-    members, across, along, width = state_init.shape
-    layers = width // 2
-    sec_count = lax.axis_size("sec")
-    rock = rock_type.reshape(across, along, layers)
-    rock = jnp.concatenate([rock, rock], -1)
-    x_start = lax.axis_index("gx") * across
-    y_start = lax.axis_index("sec") * along
-    total_y = along * sec_count
-    x_pos = lax.broadcasted_iota(jnp.int32, (across, along, layers), 0)
-    y_pos = lax.broadcasted_iota(jnp.int32, (across, along, layers), 1)
-    z_pos = lax.broadcasted_iota(jnp.int32, (across, along, layers), 2)
-    cell_ids = ((x_start + x_pos) * total_y + y_start + y_pos) * layers + z_pos
-    hits = (well_cells[:, None] == cell_ids.reshape(1, -1)).astype(jnp.float32)
-    source = jnp.dot(well_rate, hits, precision=HIGH).reshape(members, across, along, layers)
-    source_full = jnp.concatenate([source, jnp.zeros_like(source)], -1)
-    rows_total = basis_in.size // basis_in.shape[-1] * lax.axis_size("gx") * sec_count
-
-    final, snaps = flux(perm_table, state_init, rock, source_full)
-    state_out = final.reshape(state_init.shape)
-
-    both = snaps.reshape(STEPS, -1, GROUPS, MG, width).transpose(2, 0, 3, 1, 4).reshape(GROUPS * STEPS * MG, -1)
-    basis = basis_in.reshape(both.shape[1], basis_in.shape[-1])
-    count = basis.shape[1]
-    taken = both.shape[0]
-    uu = lax.dot_general(basis, basis, (((0,), (0,)), ((), ())), preferred_element_type=jnp.float32)
-    su = jnp.dot(both, basis, preferred_element_type=jnp.float32)
-    ss = lax.dot_general(both, both, (((1,), (1,)), ((), ())), preferred_element_type=jnp.float32)
-    local = jnp.concatenate(
-        [
-            su[:, :128],
-            su[:, 128:],
-            uu[:64, :128],
-            uu[:64, 128:],
-            uu[64:128, 128:],
-            uu[128:192, 128:],
-            jnp.concatenate([uu[192:, 192:], uu[64:128, 64:128]], 1),
-            jnp.pad(ss, ((0, 0), (0, 64))),
-        ],
-        0,
-    )
-    mix, sigma = small_algebra(all_sum(local), singular, rows_total)
-    fresh = jnp.dot(basis, mix[:count], preferred_element_type=jnp.float32)
-    fresh = fresh + lax.dot_general(both, mix[count:], (((0,), (0,)), ((), ())), preferred_element_type=jnp.float32)
-    return (state_out, fresh.astype(jnp.bfloat16).reshape(basis_in.shape), sigma.reshape(-1))
+    basis = basis_in.reshape(-1, basis_in.shape[-1])
+    rows_total = basis.shape[0] * lax.axis_size("gx") * lax.axis_size("sec")
+    final, snaps, whole = slab(perm_table, state_init, rock_type, well_cells.reshape(1, -1), well_rate, basis)
+    mix, sigma = small_algebra(whole.reshape(-1, 128), singular, rows_total)
+    fresh = rotate(basis, snaps, mix)
+    return (final.reshape(state_init.shape), fresh.reshape(basis_in.shape), sigma.reshape(-1))
 
 
 def solution(mesh):

time: 116 us -> 99.9 us (0.86)
  matrix products: 13.7 us -> 0 us
  local copies, waits for them, and re-layouts: 8.69 us -> 6.82 us
    dot_general x6 -> x0, matrix products: 13.7 us -> none  [the longest x1 4.79 us: body(): lax.dot_general(basis, basis, (((0,), (0,)), ((), ())), preferred_element...]
    reshape x3 -> x0, local copies, waits for them, and re-layouts: 1.29 us -> none  [the longest x1 0.79 us: body(): rock = rock_type.reshape(across, along, layers)]
    unnamed x16 -> x15, local copies, waits for them, and re-layouts: 7.2 us -> 6.82 us
where the time goes in v4:
time: 99.9 us; the launch traced here: 99.6 us
  Pallas kernels  92.1 us (92%)
  local copies, waits for them, and re-layouts  6.82 us (7%)
    pallas_call x1, Pallas kernels, slab(): pl.pallas_call(slab_kernel, out_shape=(jax.ShapeDtypeStruct((MEMB * 64, 1...  62.5 us
    pallas_call x1, Pallas kernels, small_algebra(): pl.pallas_call(lambda *refs: small_kernel(float(rows_total), *refs), out_...  24.1 us
    unnamed x15, local copies, waits for them, and re-layouts  6.82 us
    pallas_call x1, Pallas kernels, rotate(): pl.pallas_call(rotate_kernel, grid=(rows // 1024,), out_shape=jax.ShapeDt...  5.52 us

profile of v4, /device:TPU:1, one launch (start us, length us, event | category | flops | bytes accessed | tf_op | source)
XLA Modules:
  0.0 99.6 jit_solution(8539969299852491047)
XLA Ops:
  0.6 0.0 copy-start.6
  0.6 0.0 copy-start
  0.7 2.2 %copy-done = bf16[1,64,128,256]{3,2,1,0:T(8,128)(2,1)S(1)} copy-done((bf16[1,64,128,256]{3,2,1,0:T(8,128)(2,1)S(1)}, bf16[1,64,128,256]{3,2,1,0:T(8,128)(2,1)}, u32[]{:S(2)}) %copy-start) | copy-done | bytes 4194328
  2.8 0.0 copy-start.1
  2.8 1.0 %copy-done.1 = f32[16,8,8,128]{3,2,1,0:T(8,128)S(1)} copy-done((f32[16,8,8,128]{3,2,1,0:T(8,128)S(1)}, f32[16,8,8,128]{3,2,1,0:T(8,128)}, u32[]{:S(2)}) %copy-start.1) | copy-done | bytes 524312
  3.9 0.0 copy-start.2
  3.9 0.7 copy-done.2
  4.6 0.0 copy-start.3
  4.6 0.7 copy-done.3
  5.3 0.0 copy-start.4
  5.3 0.7 copy-done.4
  6.0 0.0 copy-start.5
  6.0 0.7 copy-done.5
  6.7 62.5 %slab.1 = (f32[1024,128]{1,0:T(8,128)S(1)}, bf16[4,64,16,128]{3,2,1,0:T(8,128)(2,1)S(1)}, f32[32,16,128]{2,1,0:T(8,128)S(1)}) custom-call(f32[3,16]{1,0:T(4,128)S(1)} %copy-done.4, f32[16,8,8,128]{3,2,1,0:T(8,128)S(1)} %copy-done.1, s32[8,512]{1,0:T(8,128)S(1)} %copy-done.2, s32[1,256]{1,0:T(1,128)S(1)} %bitcast.11, f32[16,256]{1,0:T(8,128)S(1)} %copy-done.3, ...), custom_call_target="tpu_custom_call" | custom-call | tf_op jit(solution)/shard_map/slab/pallas_call | solution.py:345
  69.2 0.0 copy-done.6
  69.2 24.1 %small_algebra.1 = (bf16[320,256]{1,0:T(8,128)(2,1)S(1)}, f32[1,256]{1,0:T(1,128)}) custom-call(f32[512,128]{1,0:T(8,128)S(1)} %bitcast.10, f32[1,256]{1,0:T(1,128)S(1)} %bitcast.12), custom_call_target="tpu_custom_call" | custom-call | tf_op jit(solution)/shard_map/small_algebra/pallas_call | solution.py:655
  93.3 5.5 %rotate.1 = bf16[8192,256]{1,0:T(8,128)(2,1)} custom-call(bf16[8192,256]{1,0:T(8,128)(2,1)S(1)} %bitcast.8, bf16[4,64,16,128]{3,2,1,0:T(8,128)(2,1)S(1)} %get-tuple-element.9.snaps_ref, bf16[320,256]{1,0:T(8,128)(2,1)S(1)} %get-tuple-element.11.mix_ref), custom_call_target="tpu_custom_call" | custom-call | tf_op jit(solution)/shard_map/rotate/pallas_call | solution.py:392
  98.8 0.8 copy.11
Async XLA Ops:
  0.6 68.6 %copy-start.6 = (f32[256]{0:T(256)S(1)}, f32[256]{0:T(256)}, u32[]{:S(2)}) copy-start(f32[256]{0:T(256)} %param.13) | copy-start | bytes 3076
  0.6 2.2 %copy-start = (bf16[1,64,128,256]{3,2,1,0:T(8,128)(2,1)S(1)}, bf16[1,64,128,256]{3,2,1,0:T(8,128)(2,1)}, u32[]{:S(2)}) copy-start(bf16[1,64,128,256]{3,2,1,0:T(8,128)(2,1)} %param.12) | copy-start | bytes 12582916
  2.8 1.0 %copy-start.1 = (f32[16,8,8,128]{3,2,1,0:T(8,128)S(1)}, f32[16,8,8,128]{3,2,1,0:T(8,128)}, u32[]{:S(2)}) copy-start(f32[16,8,8,128]{3,2,1,0:T(8,128)} %state_ref.1) | copy-start | bytes 1572868
  3.9 0.7 copy-start.2
  4.6 0.7 copy-start.3
  5.3 0.7 copy-start.4
  6.0 0.7 copy-start.5

commit v5 on v4

--- a/solution.py
+++ b/solution.py
@@ -36,13 +36,15 @@
 
 SHARE = 16
 CHUNKS = 8
+TEAMS = 4
+TEAM = MEMB // TEAMS
 
 
 def slab_kernel(
-    table_ref, state_ref, rock_ref, cells_ref, rate_ref, basis_hbm, out_ref, snaps_ref, sum_ref,
-    basis, uu, inflow, kinds, perm_send, perm_recv, x_send, x_recv, y_send, y_recv, y_wide, weights, turned, packed,
+    table_hbm, state_hbm, rock_hbm, cells_hbm, rate_hbm, basis_hbm, out_ref, snaps_ref, sum_ref,
+    table_ref, rock_ref, cells_ref, rate_ref, basis, uu, inflow, kinds, perm_send, perm_recv, x_send, x_recv, y_send, y_recv, y_wide, weights, turned, packed,
     local, slots, partial, column,
-    load_sem, ps_sem, pr_sem, hs_sem, hr_sem, ss_sem, sr_sem, own_sem, send1, recv1, send2, recv2, send3, recv3,
+    load_sem, in_sem, ps_sem, pr_sem, hs_sem, hr_sem, ss_sem, sr_sem, own_sem, send1, recv1, send2, recv2, send3, recv3,
 ):
     gx_count, sec_count = lax.axis_size("gx"), lax.axis_size("sec")
     gx, sec = lax.axis_index("gx"), lax.axis_index("sec")
@@ -80,6 +82,14 @@
         rows = pl.ds(pl.multiple_of(c * 1024, 1024), 1024)
         return pltpu.make_async_copy(basis_hbm.at[rows], basis.at[rows], load_sem.at[c])
 
+    arriving = [
+        pltpu.make_async_copy(src, dst, in_sem.at[i])
+        for i, (src, dst) in enumerate(
+            ((table_hbm, table_ref), (state_hbm, out_ref), (rock_hbm, rock_ref), (rate_hbm, rate_ref), (cells_hbm, cells_ref))
+        )
+    ]
+    for copy in arriving:
+        copy.start()
     for c in range(CHUNKS):
         load(c).start()
 
@@ -98,10 +108,10 @@
         copies = []
         for d in range(4):
             if d < 2:
-                src = x_send.at[step, d, pl.ds(g * MG, MG)]
-                dst = x_recv.at[step, 1 - d, pl.ds(g * MG, MG)]
+                src = x_send.at[step, d, pl.ds(g * TEAM, TEAM)]
+                dst = x_recv.at[step, 1 - d, pl.ds(g * TEAM, TEAM)]
             else:
-                rows = pl.ds(pl.multiple_of(g * 8 * MG, 8 * MG), 8 * MG)
+                rows = pl.ds(pl.multiple_of(g * 8 * TEAM, 8 * TEAM), 8 * TEAM)
                 src = y_send.at[step, d - 2, rows]
                 dst = y_recv.at[step, 3 - d, rows]
             copies.append(remote(src, dst, hs_sem.at[step, g, d], hr_sem.at[step, g, d ^ 1], beside[d]))
@@ -109,32 +119,33 @@
 
     def stage_y(step, g):
         for side, y in ((0, 0), (1, 7)):
-            rows = pl.ds(pl.multiple_of(g * 8 * MG, 8 * MG), 8 * MG)
-            y_send[step, side, rows, :] = out_ref[pl.ds(g * 64 * MG + y, 8 * MG, stride=8), :].astype(BF16)
+            rows = pl.ds(pl.multiple_of(g * 8 * TEAM, 8 * TEAM), 8 * TEAM)
+            y_send[step, side, rows, :] = out_ref[pl.ds(g * 64 * TEAM + y, 8 * TEAM, stride=8), :].astype(BF16)
 
     def first(m, carry):
-        x_send[0, 0, m] = state_ref[m, 0].astype(BF16)
-        x_send[0, 1, m] = state_ref[m, 7].astype(BF16)
-        for x in range(8):
-            out_ref[pl.ds(pl.multiple_of(m * 64 + x * 8, 8), 8), :] = state_ref[m, x]
+        x_send[0, 0, m] = out_ref[pl.ds(pl.multiple_of(m * 64, 8), 8), :].astype(BF16)
+        x_send[0, 1, m] = out_ref[pl.ds(pl.multiple_of(m * 64 + 56, 8), 8), :].astype(BF16)
         return carry
 
+    for copy in arriving:
+        copy.wait()
     lax.fori_loop(0, MEMB, first, 0)
-    stage_y(0, 0)
-    stage_y(0, 1)
+    for g in range(TEAMS):
+        stage_y(0, g)
 
     for pair in range(4):
         both = rock_ref[:, pair * 128 : pair * 128 + 128]
         other = pltpu.roll(both, 64, 1)
         kinds[pl.ds(2 * pair, 8, stride=8), :] = jnp.where(lane < 64, both, other)
         kinds[pl.ds(2 * pair + 1, 8, stride=8), :] = jnp.where(lane < 64, other, both)
+    table = [[jnp.broadcast_to(table_ref[d : d + 1, r : r + 1], (8, 128)) for r in range(16)] for d in range(3)]
     perm = [[], [], []]
     for x in range(8):
         kind = kinds[x * 8 : x * 8 + 8, :]
         for d in range(3):
-            value = jnp.full((8, 128), table_ref[d, 0], F32)
+            value = table[d][0]
             for r in range(1, 16):
-                value = jnp.where(kind == r, table_ref[d, r], value)
+                value = jnp.where(kind == r, table[d][r], value)
             perm[d].append(value)
     perm_send[0] = perm[0][0]
     perm_send[1] = perm[0][7]
@@ -143,13 +154,14 @@
         perm_send[3, pl.ds(x, 1), :] = perm[1][x][7:8]
 
     uu[...] = jnp.zeros((256, 256), F32)
+    lax.fori_loop(0, 3, uu_chunk, 0)
     pl.semaphore_wait(barrier, 2 + (sec_count - 1) + (COLUMN - 1) + (PLANE - 1))
     perm_copies = [
         remote(perm_send.at[d], perm_recv.at[d ^ 1], ps_sem.at[d], pr_sem.at[d ^ 1], beside[d]) for d in range(4)
     ]
     for copy in perm_copies:
         copy.start()
-    for g in range(GROUPS):
+    for g in range(TEAMS):
         for copy in halo_copies(0, g):
             copy.start()
 
@@ -174,6 +186,7 @@
         return carry
 
     lax.fori_loop(0, 8, place, 0)
+    lax.fori_loop(3, 5, uu_chunk, 0)
 
     z_up = jnp.where((lane & 63) == 63, 0.0, 1.0)
     z_down = jnp.where((lane & 63) == 0, 0.0, 1.0)
@@ -215,15 +228,15 @@
 
     for step in range(STEPS):
 
-        def half_step(g, carry):
+        def team_step(g, carry):
             for copy in halo_copies(step, g):
                 copy.wait()
-            rows = pl.ds(pl.multiple_of(g * 8 * MG, 8 * MG), 8 * MG)
+            rows = pl.ds(pl.multiple_of(g * 8 * TEAM, 8 * TEAM), 8 * TEAM)
             y_wide[0, rows, :] = y_recv[step, 0, rows, :].astype(F32)
             y_wide[1, rows, :] = y_recv[step, 1, rows, :].astype(F32)
 
             def member(index, carry):
-                m = g * MG + index
+                m = g * TEAM + index
                 base = pl.multiple_of(m * 64, 64)
                 old = [out_ref[pl.ds(base + x * 8, 8), :] for x in range(8)]
                 old_below = x_recv[step, 0, m].astype(F32)
@@ -254,19 +267,19 @@
                         x_send[step + 1, x // 7, m] = fresh.astype(BF16)
                 return carry
 
-            lax.fori_loop(0, MG, member, 0)
+            lax.fori_loop(0, TEAM, member, 0)
             if step + 1 < STEPS:
                 stage_y(step + 1, g)
                 for copy in halo_copies(step + 1, g):
                     copy.start()
             return carry
 
-        lax.fori_loop(0, GROUPS, half_step, 0)
+        lax.fori_loop(0, TEAMS, team_step, 0)
         for x in range(8):
             packed[step, x] = turned[x].reshape(8, MEMB, 128).astype(BF16)
         for copy in snap_copies(step):
             copy.start()
-        lax.fori_loop(2 * step, 2 * step + 2, uu_chunk, 0)
+    lax.fori_loop(5, CHUNKS, uu_chunk, 0)
     for step in range(STEPS):
         for copy in snap_copies(step):
             copy.wait()
@@ -349,9 +362,13 @@
             jax.ShapeDtypeStruct((STEPS, 8 * sec_count, MEMB, 128), BF16),
             jax.ShapeDtypeStruct((PLANE, SHARE, 128), F32),
         ),
-        in_specs=[pl.BlockSpec(memory_space=pltpu.SMEM)] + [in_vmem] * 4 + [pl.BlockSpec(memory_space=pltpu.HBM)],
+        in_specs=[pl.BlockSpec(memory_space=pltpu.HBM)] * 6,
         out_specs=(in_vmem,) * 3,
         scratch_shapes=[
+            VMEM(table.shape, F32),
+            VMEM(rock.shape, jnp.int32),
+            VMEM(cells.shape, jnp.int32),
+            VMEM(rate.shape, F32),
             VMEM(basis.shape, BF16),
             VMEM((256, 256), F32),
             VMEM((MEMB * 64, 128), F32),
@@ -370,7 +387,7 @@
             VMEM((PLANE, SHARE, 128), F32),
             VMEM((SHARE, 128), F32),
             VMEM((COLUMN, SHARE, 128), F32),
-            dma((CHUNKS,)), dma((4,)), dma((4,)), dma((STEPS, GROUPS, 4)), dma((STEPS, GROUPS, 4)),
+            dma((CHUNKS,)), dma((5,)), dma((4,)), dma((4,)), dma((STEPS, TEAMS, 4)), dma((STEPS, TEAMS, 4)),
             dma((STEPS, sec_count)), dma((STEPS, sec_count)), dma((STEPS,)),
             dma((PLANE,)), dma((PLANE,)), dma((COLUMN,)), dma((COLUMN,)), dma((PLANE,)), dma((PLANE,)),
         ],
@@ -378,7 +395,7 @@
             collective_id=0, has_side_effects=True, vmem_limit_bytes=40 * 1024 * 1024
         ),
         name="slab",
-    )(table, state, rock, cells, rate, basis)
+    )(*(pltpu.with_memory_space_constraint(x, pltpu.HBM) for x in (table, state.reshape(-1, 128), rock, cells, rate, basis)))
 
 
 def rotate_kernel(basis_ref, snaps_ref, mix_ref, out_ref):
@@ -404,11 +421,14 @@
     )(basis, snaps, mix)
 
 
-HIGH = lax.Precision.HIGHEST
-
-
 def dot(a, b, contract=((1,), (0,))):
-    return lax.dot_general(a, b, (contract, ((), ())), precision=HIGH, preferred_element_type=F32)
+    a1, b1 = a.astype(BF16), b.astype(BF16)
+    a2, b2 = (a - a1.astype(F32)).astype(BF16), (b - b1.astype(F32)).astype(BF16)
+
+    def one(x, y):
+        return lax.dot_general(x, y, (contract, ((), ())), preferred_element_type=F32)
+
+    return one(a1, b1) + (one(a1, b2) + one(a2, b1))
 
 
 ROWS_BASIS = 256
@@ -602,7 +622,11 @@
     return jnp.concatenate([x[16 * step + 8 * g : 16 * step + 8 * g + 8] for g in range(2) for step in range(4)], 0)
 
 
-def small_kernel(rows_total, whole_ref, sigma_ref, mix_ref, sigma_out_ref, half_uu, *scratch):
+def small_kernel(
+    rows_total, whole_ref, sigma_ref, fields_ref, mix_ref, sigma_out_ref, fields_out, half_uu, copy_sem, *scratch
+):
+    writing = pltpu.make_async_copy(fields_ref, fields_out, copy_sem)
+    writing.start()
     scale = 1.0 / rows_total
 
     def piece(index):
@@ -649,16 +673,18 @@
         [w[8 * step : 8 * step + 8] for step in range(4) for w in (w0, w1)], 0
     ).astype(BF16)
     sigma_out_ref[...] = sigma2
-
-
-def small_algebra(whole, sigma, rows_total):
+    writing.wait()
+
+
+def small_algebra(whole, sigma, fields, rows_total):
     return pl.pallas_call(
         lambda *refs: small_kernel(float(rows_total), *refs),
-        out_shape=(jax.ShapeDtypeStruct((320, 256), BF16), jax.ShapeDtypeStruct((1, 256), F32)),
-        in_specs=[pl.BlockSpec(memory_space=VMEM)] * 2,
-        out_specs=(pl.BlockSpec(memory_space=VMEM),) * 2,
+        out_shape=(jax.ShapeDtypeStruct((320, 256), BF16), jax.ShapeDtypeStruct((1, 256), F32), jax.ShapeDtypeStruct(fields.shape, F32)),
+        in_specs=[pl.BlockSpec(memory_space=VMEM)] * 3,
+        out_specs=(pl.BlockSpec(memory_space=VMEM),) * 2 + (pl.BlockSpec(memory_space=pltpu.HBM),),
         scratch_shapes=[
             VMEM((256, 256), F32),
+            pltpu.SemaphoreType.DMA,
             VMEM((RANK * STRIDE, 128), F32),
             VMEM((256, 128), F32),
             VMEM((RANK * RANK, 128), F32),
@@ -669,14 +695,14 @@
         ],
         compiler_params=pltpu.CompilerParams(vmem_limit_bytes=32 * 1024 * 1024),
         name="small_algebra",
-    )(whole, sigma.reshape(1, -1))
+    )(whole, sigma.reshape(1, -1), fields)
 
 
 def body(state_init, rock_type, perm_table, well_cells, well_rate, basis_in, singular):
     basis = basis_in.reshape(-1, basis_in.shape[-1])
     rows_total = basis.shape[0] * lax.axis_size("gx") * lax.axis_size("sec")
     final, snaps, whole = slab(perm_table, state_init, rock_type, well_cells.reshape(1, -1), well_rate, basis)
-    mix, sigma = small_algebra(whole.reshape(-1, 128), singular, rows_total)
+    mix, sigma, final = small_algebra(whole.reshape(-1, 128), singular, final, rows_total)
     fresh = rotate(basis, snaps, mix)
     return (final.reshape(state_init.shape), fresh.reshape(basis_in.shape), sigma.reshape(-1))
 

time: 99.9 us -> 87.8 us (0.88)
  local copies, waits for them, and re-layouts: 6.82 us -> 0.01 us
  Pallas kernels: 92.1 us -> 87 us
    unnamed x15 -> x4, local copies, waits for them, and re-layouts: 6.82 us -> 0.01 us
    pallas_call x1, Pallas kernels: 24.1 us -> 21.2 us  [small_algebra(): pl.pallas_call(lambda *refs: small_kernel(float(rows_total), *refs), out_...]
    pallas_call x1, Pallas kernels: 62.5 us -> 60.3 us  [slab(): pl.pallas_call(slab_kernel, out_shape=(jax.ShapeDtypeStruct((MEMB * 64, 1...]
where the time goes in v5:
time: 87.8 us; the launch traced here: 87.7 us
  Pallas kernels  87 us (99%)
    pallas_call x1, Pallas kernels, slab(): pl.pallas_call(slab_kernel, out_shape=(jax.ShapeDtypeStruct((MEMB * 64, 1...  60.3 us
    pallas_call x1, Pallas kernels, small_algebra(): pl.pallas_call(lambda *refs: small_kernel(float(rows_total), *refs), out_...  21.2 us
    pallas_call x1, Pallas kernels, rotate(): pl.pallas_call(rotate_kernel, grid=(rows // 1024,), out_shape=jax.ShapeDt...  5.52 us

profile of v5, /device:TPU:1, one launch (start us, length us, event | category | flops | bytes accessed | tf_op | source)
XLA Modules:
  0.0 87.7 jit_solution(13978713244797008019)
XLA Ops:
  0.6 0.0 copy-start.1
  0.6 0.0 copy-start
  0.7 60.3 %slab.1 = (f32[1024,128]{1,0:T(8,128)S(1)}, bf16[4,64,16,128]{3,2,1,0:T(8,128)(2,1)S(1)}, f32[32,16,128]{2,1,0:T(8,128)S(1)}) custom-call(f32[3,16]{1,0:T(4,128)} %table_hbm.1, f32[1024,128]{1,0:T(8,128)} %bitcast.13, s32[8,512]{1,0:T(8,128)} %rock_hbm.1, s32[1,256]{1,0:T(1,128)} %bitcast.14, f32[16,256]{1,0:T(8,128)} %rate_hbm.1, bf16[8192,256]{1,0:T(8,128)(2,1)} %bitcast.8), custom_call_target="tpu_custom_call" | custom-call | tf_op jit(solution)/shard_map/slab/pallas_call | solution.py:358
  61.0 0.0 copy-done.1
  61.0 21.2 %small_algebra.1 = (bf16[320,256]{1,0:T(8,128)(2,1)S(1)}, f32[1,256]{1,0:T(1,128)}, f32[1024,128]{1,0:T(8,128)}) custom-call(f32[512,128]{1,0:T(8,128)S(1)} %bitcast.10, f32[1,256]{1,0:T(1,128)S(1)} %bitcast.11, f32[1024,128]{1,0:T(8,128)S(1)} %get-tuple-element.10.refs_2_), custom_call_target="tpu_custom_call" | custom-call | tf_op jit(solution)/shard_map/small_algebra/pallas_call | solution.py:680
  82.2 0.0 copy-done
  82.2 5.5 %rotate.1 = bf16[8192,256]{1,0:T(8,128)(2,1)} custom-call(bf16[8192,256]{1,0:T(8,128)(2,1)S(1)} %bitcast.9, bf16[4,64,16,128]{3,2,1,0:T(8,128)(2,1)S(1)} %get-tuple-element.12.snaps_ref, bf16[320,256]{1,0:T(8,128)(2,1)S(1)} %get-tuple-element.13.mix_ref), custom_call_target="tpu_custom_call" | custom-call | tf_op jit(solution)/shard_map/rotate/pallas_call | solution.py:409
Async XLA Ops:
  0.6 60.4 %copy-start.1 = (f32[256]{0:T(256)S(1)}, f32[256]{0:T(256)}, u32[]{:S(2)}) copy-start(f32[256]{0:T(256)} %param.13) | copy-start | bytes 3076
  0.6 81.6 %copy-start = (bf16[1,64,128,256]{3,2,1,0:T(8,128)(2,1)S(1)}, bf16[1,64,128,256]{3,2,1,0:T(8,128)(2,1)}, u32[]{:S(2)}) copy-start(bf16[1,64,128,256]{3,2,1,0:T(8,128)(2,1)} %param.12) | copy-start | bytes 12582916

commit v6 on v5

--- a/solution.py
+++ b/solution.py
@@ -42,7 +42,7 @@
 
 def slab_kernel(
     table_hbm, state_hbm, rock_hbm, cells_hbm, rate_hbm, basis_hbm, out_ref, snaps_ref, sum_ref,
-    table_ref, rock_ref, cells_ref, rate_ref, basis, uu, inflow, kinds, perm_send, perm_recv, x_send, x_recv, y_send, y_recv, y_wide, weights, turned, packed,
+    table_ref, rock_ref, cells_ref, rate_ref, fields, basis, uu, inflow, kinds, perm_send, perm_recv, x_send, x_recv, y_send, y_recv, y_wide, weights, turned, packed,
     local, slots, partial, column,
     load_sem, in_sem, ps_sem, pr_sem, hs_sem, hr_sem, ss_sem, sr_sem, own_sem, send1, recv1, send2, recv2, send3, recv3,
 ):
@@ -120,16 +120,27 @@
     def stage_y(step, g):
         for side, y in ((0, 0), (1, 7)):
             rows = pl.ds(pl.multiple_of(g * 8 * TEAM, 8 * TEAM), 8 * TEAM)
-            y_send[step, side, rows, :] = out_ref[pl.ds(g * 64 * TEAM + y, 8 * TEAM, stride=8), :].astype(BF16)
-
-    def first(m, carry):
-        x_send[0, 0, m] = out_ref[pl.ds(pl.multiple_of(m * 64, 8), 8), :].astype(BF16)
-        x_send[0, 1, m] = out_ref[pl.ds(pl.multiple_of(m * 64 + 56, 8), 8), :].astype(BF16)
+            y_send[step, side, rows, :] = fields[pl.ds(g * 64 * TEAM + y, 8 * TEAM, stride=8), :].astype(BF16)
+
+    low_half = lane < 64
+
+    def first(q, carry):
+        base = pl.multiple_of(q * 128, 128)
+        for x in range(8):
+            a = out_ref[pl.ds(base + x * 8, 8), :]
+            b = out_ref[pl.ds(base + 64 + x * 8, 8), :]
+            p = jnp.where(low_half, a, pltpu.roll(b, 64, 1))
+            s = jnp.where(low_half, pltpu.roll(a, 64, 1), b)
+            fields[pl.ds(base + x * 8, 8), :] = p
+            fields[pl.ds(base + 64 + x * 8, 8), :] = s
+            if x in (0, 7):
+                x_send[0, x // 7, 2 * q] = p.astype(BF16)
+                x_send[0, x // 7, 2 * q + 1] = s.astype(BF16)
         return carry
 
     for copy in arriving:
         copy.wait()
-    lax.fori_loop(0, MEMB, first, 0)
+    lax.fori_loop(0, MEMB // 2, first, 0)
     for g in range(TEAMS):
         stage_y(0, g)
 
@@ -165,7 +176,7 @@
         for copy in halo_copies(0, g):
             copy.start()
 
-    rate = rate_ref[...]
+    rate = jnp.concatenate([rate_ref[m : m + 1, :] for start in range(2) for m in range(start, MEMB, 2)], 0)
     top = rate.astype(BF16)
     rest = rate - top.astype(F32)
     middle = rest.astype(BF16)
@@ -179,10 +190,13 @@
         found = lax.dot_general(parts, hits, (((1,), (1,)), ((), ())), preferred_element_type=F32)
         found = found[:MEMB] + found[MEMB : 2 * MEMB] + found[2 * MEMB :]
         for y in range(8):
-            pair = found[:, (y // 2) * 128 : (y // 2) * 128 + 128]
-            pair = pair if y % 2 == 0 else pltpu.roll(pair, 64, 1)
-            half = lax.broadcasted_iota(jnp.int32, (MEMB, 128), 1) < 64
-            inflow[pl.ds(x * 8 + y, MEMB, stride=64), :] = jnp.where(half, DT_PRESSURE * pair, 0.0)
+            columns = slice((y // 2) * 128, (y // 2) * 128 + 128)
+            even, odd = found[:8, columns], found[8:, columns]
+            if y % 2 == 0:
+                both = jnp.where(low_half, even, pltpu.roll(odd, 64, 1))
+            else:
+                both = jnp.where(low_half, pltpu.roll(even, 64, 1), odd)
+            inflow[pl.ds(x * 8 + y, 8, stride=64), :] = DT_PRESSURE * both
         return carry
 
     lax.fori_loop(0, 8, place, 0)
@@ -209,9 +223,6 @@
         weights[2, x] = harmonic(perm[1][x], jnp.where(row == 7, right, pltpu.roll(perm[1][x], 7, 0)))
         weights[3, x] = harmonic(jnp.where(row == 0, left, pltpu.roll(perm[1][x], 1, 0)), perm[1][x])
 
-    step_sizes = jnp.where(lane < 64, DT_PRESSURE, DT_SATURATION)
-    advect = jnp.where(lane < 64, 0.0, DT_ADVECT)
-
     def snap_copies(step):
         copies = [
             pltpu.make_async_copy(packed.at[step, sec], snaps_ref.at[step, pl.ds(sec * 8, 8)], own_sem.at[step])
@@ -235,39 +246,57 @@
             y_wide[0, rows, :] = y_recv[step, 0, rows, :].astype(F32)
             y_wide[1, rows, :] = y_recv[step, 1, rows, :].astype(F32)
 
-            def member(index, carry):
-                m = g * TEAM + index
-                base = pl.multiple_of(m * 64, 64)
-                old = [out_ref[pl.ds(base + x * 8, 8), :] for x in range(8)]
-                old_below = x_recv[step, 0, m].astype(F32)
-                old_above = x_recv[step, 1, m].astype(F32)
-                for x in range(8):
-                    here = old[x]
-                    left = jnp.broadcast_to(y_wide[0, pl.ds(m * 8 + x, 1), :], (8, 128))
-                    right = jnp.broadcast_to(y_wide[1, pl.ds(m * 8 + x, 1), :], (8, 128))
-                    besides = (
-                        old[x + 1] if x < 7 else old_above,
-                        old[x - 1] if x > 0 else old_below,
+            def pair_step(index, carry):
+                q = g * (TEAM // 2) + index
+                base = pl.multiple_of(q * 128, 128)
+                ps = [fields[pl.ds(base + x * 8, 8), :] for x in range(8)]
+                ss = [fields[pl.ds(base + 64 + x * 8, 8), :] for x in range(8)]
+                ends = [[x_recv[step, side, 2 * q + i].astype(F32) for side in range(2)] for i in range(2)]
+
+                def besides(all_x, x, i):
+                    here = all_x[x]
+                    at = (2 * q + i) * 8 + x
+                    left = jnp.broadcast_to(y_wide[0, pl.ds(at, 1), :], (8, 128))
+                    right = jnp.broadcast_to(y_wide[1, pl.ds(at, 1), :], (8, 128))
+                    return (
+                        all_x[x + 1] if x < 7 else ends[i][1],
+                        all_x[x - 1] if x > 0 else ends[i][0],
                         jnp.where(row == 7, right, pltpu.roll(here, 7, 0)),
                         jnp.where(row == 0, left, pltpu.roll(here, 1, 0)),
                         pltpu.roll(here, 127, 1),
                         pltpu.roll(here, 1, 1),
                     )
-                    spread = carried = None
+
+                for x in range(8):
+                    p, s = ps[x], ss[x]
+                    p_beside, s_beside = besides(ps, x, 0), besides(ss, x, 1)
+                    p_spread = s_spread = carried = None
                     for d in range(6):
-                        flow = weights[d, x] * (besides[d] - here)
-                        pushed = pltpu.roll(flow, 64, 1)
-                        moved = pushed * jnp.where(pushed > 0.0, besides[d], here)
-                        spread = flow if spread is None else spread + flow
+                        weight = weights[d, x]
+                        flow = weight * (p_beside[d] - p)
+                        spread = weight * (s_beside[d] - s)
+                        moved = flow * jnp.where(flow > 0.0, s_beside[d], s)
+                        p_spread = flow if p_spread is None else p_spread + flow
+                        s_spread = spread if s_spread is None else s_spread + spread
                         carried = moved if carried is None else carried + moved
-                    fresh = here + step_sizes * spread + advect * carried + inflow[pl.ds(base + x * 8, 8), :]
-                    out_ref[pl.ds(base + x * 8, 8), :] = fresh
-                    turned[x, pl.ds(m, 8, stride=MEMB), :] = fresh
-                    if step + 1 < STEPS and x in (0, 7):
-                        x_send[step + 1, x // 7, m] = fresh.astype(BF16)
+                    p = p + DT_PRESSURE * p_spread + inflow[pl.ds(pl.multiple_of(q * 64 + x * 8, 8), 8), :]
+                    s = s + DT_SATURATION * s_spread + DT_ADVECT * carried
+                    a = jnp.where(low_half, p, pltpu.roll(s, 64, 1))
+                    b = jnp.where(low_half, pltpu.roll(p, 64, 1), s)
+                    turned[x, pl.ds(2 * q, 8, stride=MEMB), :] = a
+                    turned[x, pl.ds(2 * q + 1, 8, stride=MEMB), :] = b
+                    if step + 1 < STEPS:
+                        fields[pl.ds(base + x * 8, 8), :] = p
+                        fields[pl.ds(base + 64 + x * 8, 8), :] = s
+                        if x in (0, 7):
+                            x_send[step + 1, x // 7, 2 * q] = p.astype(BF16)
+                            x_send[step + 1, x // 7, 2 * q + 1] = s.astype(BF16)
+                    else:
+                        out_ref[pl.ds(base + x * 8, 8), :] = a
+                        out_ref[pl.ds(base + 64 + x * 8, 8), :] = b
                 return carry
 
-            lax.fori_loop(0, TEAM, member, 0)
+            lax.fori_loop(0, TEAM // 2, pair_step, 0)
             if step + 1 < STEPS:
                 stage_y(step + 1, g)
                 for copy in halo_copies(step + 1, g):
@@ -369,9 +398,10 @@
             VMEM(rock.shape, jnp.int32),
             VMEM(cells.shape, jnp.int32),
             VMEM(rate.shape, F32),
+            VMEM((MEMB * 64, 128), F32),
             VMEM(basis.shape, BF16),
             VMEM((256, 256), F32),
-            VMEM((MEMB * 64, 128), F32),
+            VMEM((MEMB * 32, 128), F32),
             VMEM((64, 128), jnp.int32),
             VMEM((4, 8, 128), F32),
             VMEM((4, 8, 128), F32),
@@ -399,8 +429,9 @@
 
 
 def rotate_kernel(basis_ref, snaps_ref, mix_ref, out_ref):
-    taken = jnp.concatenate([snaps_ref[:, y].reshape(64, 128).T for y in range(8)], 0)
-    lhs = jnp.concatenate([basis_ref[...], taken], 1)
+    block = pl.program_id(0)
+    taken = jnp.concatenate([snaps_ref[:, block * 8 + y].reshape(64, 128).T for y in range(8)], 0)
+    lhs = jnp.concatenate([basis_ref[pl.ds(pl.multiple_of(block * 1024, 1024), 1024), :], taken], 1)
     out_ref[...] = jnp.dot(lhs, mix_ref[...], preferred_element_type=F32).astype(BF16)
 
 
@@ -411,9 +442,9 @@
         grid=(rows // 1024,),
         out_shape=jax.ShapeDtypeStruct(basis.shape, BF16),
         in_specs=[
-            pl.BlockSpec((1024, 256), lambda i: (i, 0)),
-            pl.BlockSpec((STEPS, 8, MEMB, 128), lambda i: (0, i, 0, 0)),
-            pl.BlockSpec((320, 256), lambda i: (0, 0)),
+            pl.BlockSpec(memory_space=VMEM),
+            pl.BlockSpec(memory_space=VMEM),
+            pl.BlockSpec(memory_space=VMEM),
         ],
         out_specs=pl.BlockSpec((1024, 256), lambda i: (i, 0)),
         compiler_params=pltpu.CompilerParams(vmem_limit_bytes=24 * 1024 * 1024),

time: 87.8 us -> 85.8 us (0.977)
  Pallas kernels: 87 us -> 85 us
    pallas_call x1, Pallas kernels: 60.3 us -> 58.4 us  [slab(): pl.pallas_call(slab_kernel, out_shape=(jax.ShapeDtypeStruct((MEMB * 64, 1...]
where the time goes in v6:
time: 85.8 us; the launch traced here: 85.7 us
  Pallas kernels  85 us (99%)
    pallas_call x1, Pallas kernels, slab(): pl.pallas_call(slab_kernel, out_shape=(jax.ShapeDtypeStruct((MEMB * 64, 1...  58.4 us
    pallas_call x1, Pallas kernels, small_algebra(): pl.pallas_call(lambda *refs: small_kernel(float(rows_total), *refs), out_...  21.2 us
    pallas_call x1, Pallas kernels, rotate(): pl.pallas_call(rotate_kernel, grid=(rows // 1024,), out_shape=jax.ShapeDt...  5.45 us

profile of v6, /device:TPU:1, one launch (start us, length us, event | category | flops | bytes accessed | tf_op | source)
XLA Modules:
  0.0 85.7 jit_solution(14447934869077195485)
XLA Ops:
  0.6 0.0 copy-start.1
  0.6 0.0 copy-start
  0.7 58.4 %slab.1 = (f32[1024,128]{1,0:T(8,128)S(1)}, bf16[4,64,16,128]{3,2,1,0:T(8,128)(2,1)S(1)}, f32[32,16,128]{2,1,0:T(8,128)S(1)}) custom-call(f32[3,16]{1,0:T(4,128)} %table_hbm.1, f32[1024,128]{1,0:T(8,128)} %bitcast.13, s32[8,512]{1,0:T(8,128)} %rock_hbm.1, s32[1,256]{1,0:T(1,128)} %bitcast.14, f32[16,256]{1,0:T(8,128)} %rate_hbm.1, bf16[8192,256]{1,0:T(8,128)(2,1)} %bitcast.8), custom_call_target="tpu_custom_call" | custom-call | tf_op jit(solution)/shard_map/slab/pallas_call | solution.py:387
  59.0 0.0 copy-done.1
  59.0 21.2 %small_algebra.1 = (bf16[320,256]{1,0:T(8,128)(2,1)S(1)}, f32[1,256]{1,0:T(1,128)}, f32[1024,128]{1,0:T(8,128)}) custom-call(f32[512,128]{1,0:T(8,128)S(1)} %bitcast.10, f32[1,256]{1,0:T(1,128)S(1)} %bitcast.11, f32[1024,128]{1,0:T(8,128)S(1)} %get-tuple-element.10.refs_2_), custom_call_target="tpu_custom_call" | custom-call | tf_op jit(solution)/shard_map/small_algebra/pallas_call | solution.py:711
  80.2 0.0 copy-done
  80.2 5.5 %rotate.1 = bf16[8192,256]{1,0:T(8,128)(2,1)} custom-call(bf16[8192,256]{1,0:T(8,128)(2,1)S(1)} %bitcast.9, bf16[4,64,16,128]{3,2,1,0:T(8,128)(2,1)S(1)} %get-tuple-element.12.snaps_ref, bf16[320,256]{1,0:T(8,128)(2,1)S(1)} %get-tuple-element.13.mix_ref), custom_call_target="tpu_custom_call" | custom-call | tf_op jit(solution)/shard_map/rotate/pallas_call | solution.py:440
Async XLA Ops:
  0.6 58.4 %copy-start.1 = (f32[256]{0:T(256)S(1)}, f32[256]{0:T(256)}, u32[]{:S(2)}) copy-start(f32[256]{0:T(256)} %param.13) | copy-start | bytes 3076
  0.6 79.6 %copy-start = (bf16[1,64,128,256]{3,2,1,0:T(8,128)(2,1)S(1)}, bf16[1,64,128,256]{3,2,1,0:T(8,128)(2,1)}, u32[]{:S(2)}) copy-start(bf16[1,64,128,256]{3,2,1,0:T(8,128)(2,1)} %param.12) | copy-start | bytes 12582916

commit v7 on v6

--- a/solution.py
+++ b/solution.py
@@ -525,8 +525,9 @@
             fourth.append(sq * sq)
 
     acc = tuple(jnp.zeros((8, 128), F32) for _ in range(BLOCK))
-    for part in range(4):
-        skip = part * 8
+    for part in range(8):
+        start = part * 4
+        skip = part // 2 * 8
         count = RANK - skip
         w0, w1, w2 = wide(g0, count), wide(g1, count), wide(g2, count)
 
@@ -566,7 +567,7 @@
             )
             fall = jnp.concatenate([fa, fr], 0)
             sall = jnp.concatenate([sa, sr], 0)
-            for i in range(skip, RANK):
+            for i in range(start, RANK):
                 f = jnp.broadcast_to(coef[0, i : i + 1, :], (8, 128))
                 s = jnp.broadcast_to(coef[1, i : i + 1, :], (8, 128))
                 for part8 in range(count // 8 + 1):
@@ -576,7 +577,7 @@
                     )
             return acc
 
-        acc = lax.fori_loop(skip, skip + 8, step, acc)
+        acc = lax.fori_loop(start, start + 4, step, acc)
 
     ys = [None] * RANK
     for k in range(RANK - 1, -1, -1):

time: 85.8 us -> 85.6 us (level)
  no operation moved by 1% of the time
where the time goes in v7:
time: 85.6 us
  Pallas kernels  84.9 us (99%)
    pallas_call x1, Pallas kernels, slab(): pl.pallas_call(slab_kernel, out_shape=(jax.ShapeDtypeStruct((MEMB * 64, 1...  58.4 us
    pallas_call x1, Pallas kernels, small_algebra(): pl.pallas_call(lambda *refs: small_kernel(float(rows_total), *refs), out_...  21.1 us
    pallas_call x1, Pallas kernels, rotate(): pl.pallas_call(rotate_kernel, grid=(rows // 1024,), out_shape=jax.ShapeDt...  5.45 us

profile of v7, /device:TPU:1, one launch (start us, length us, event | category | flops | bytes accessed | tf_op | source)
XLA Modules:
  0.0 85.6 jit_solution(13766916421851060883)
XLA Ops:
  0.6 0.0 copy-start.1
  0.6 0.0 copy-start
  0.7 58.4 %slab.1 = (f32[1024,128]{1,0:T(8,128)S(1)}, bf16[4,64,16,128]{3,2,1,0:T(8,128)(2,1)S(1)}, f32[32,16,128]{2,1,0:T(8,128)S(1)}) custom-call(f32[3,16]{1,0:T(4,128)} %table_hbm.1, f32[1024,128]{1,0:T(8,128)} %bitcast.13, s32[8,512]{1,0:T(8,128)} %rock_hbm.1, s32[1,256]{1,0:T(1,128)} %bitcast.14, f32[16,256]{1,0:T(8,128)} %rate_hbm.1, bf16[8192,256]{1,0:T(8,128)(2,1)} %bitcast.8), custom_call_target="tpu_custom_call" | custom-call | tf_op jit(solution)/shard_map/slab/pallas_call | solution.py:387
  59.0 0.0 copy-done.1
  59.0 21.1 %small_algebra.1 = (bf16[320,256]{1,0:T(8,128)(2,1)S(1)}, f32[1,256]{1,0:T(1,128)}, f32[1024,128]{1,0:T(8,128)}) custom-call(f32[512,128]{1,0:T(8,128)S(1)} %bitcast.10, f32[1,256]{1,0:T(1,128)S(1)} %bitcast.11, f32[1024,128]{1,0:T(8,128)S(1)} %get-tuple-element.10.refs_2_), custom_call_target="tpu_custom_call" | custom-call | tf_op jit(solution)/shard_map/small_algebra/pallas_call | solution.py:712
  80.1 0.0 copy-done
  80.1 5.5 %rotate.1 = bf16[8192,256]{1,0:T(8,128)(2,1)} custom-call(bf16[8192,256]{1,0:T(8,128)(2,1)S(1)} %bitcast.9, bf16[4,64,16,128]{3,2,1,0:T(8,128)(2,1)S(1)} %get-tuple-element.12.snaps_ref, bf16[320,256]{1,0:T(8,128)(2,1)S(1)} %get-tuple-element.13.mix_ref), custom_call_target="tpu_custom_call" | custom-call | tf_op jit(solution)/shard_map/rotate/pallas_call | solution.py:440
Async XLA Ops:
  0.6 58.4 %copy-start.1 = (f32[256]{0:T(256)S(1)}, f32[256]{0:T(256)}, u32[]{:S(2)}) copy-start(f32[256]{0:T(256)} %param.13) | copy-start | bytes 3076
  0.6 79.5 %copy-start = (bf16[1,64,128,256]{3,2,1,0:T(8,128)(2,1)S(1)}, bf16[1,64,128,256]{3,2,1,0:T(8,128)(2,1)}, u32[]{:S(2)}) copy-start(bf16[1,64,128,256]{3,2,1,0:T(8,128)(2,1)} %param.12) | copy-start | bytes 12582916
